TPU v7x, 256 devices: a whole 4x4x8 slice. The times are simulated.
256 devices in a mesh: ctx: 8 (over x, y_hi), chan: 32 (over z, y_lo, core).
Axes of the slice: x: 4, y: 4 (y_hi: 2, y_lo: 2; y = y_hi * 2 + y_lo), z: 8, core: 2. Of those that a mesh axis runs over, the one named last changes fastest.
Arguments:
- inputs: bfloat16 [4096, 4096], P('ctx', 'chan'), may hold values from -6 to 6
- w_in: bfloat16 [4096, 3, 4096], P(None, None, 'chan'), may hold values from -0.09375 to 0.09375
- conv_taps: bfloat16 [3, 3, 4096], P(None, None, 'chan'), may hold values from -3.59375 to 3.59375
- skip_gain: float32 [4096], P('chan'), may hold values from 0.5 to 1.5
- filter_taps: bfloat16 [4096, 4096], P('ctx', 'chan'), may hold values from -0.09375 to 0.09375
- w_out: bfloat16 [4096, 4096], P('chan'), may hold values from -0.1875 to 0.1875
Outputs:
- result: bfloat16 [4096, 4096], P('ctx', 'chan')
All inputs are finite; a program needn't handle non-finite values.
Results may differ from a plain program's by a relative error of at most 0.024.
Values may be sent and summed in bfloat16 or wider, within the bound.
A program may use at most 64 MiB of HBM per device.

v0:
```python
import math

import jax
import jax.numpy as jnp
from jax import lax
from jax.sharding import PartitionSpec as P

KERNEL = 3


def from_behind(block, axis, distance):
    devices = range(lax.axis_size(axis))
    route = [(i - distance, i) for i in devices if i - distance in devices]
    return lax.ppermute(block, axis, route)


def angles(row_count, col_count, double_len):
    row_ids = jnp.arange(row_count, dtype=jnp.int32)[:, None]
    col_ids = jnp.arange(col_count, dtype=jnp.int32)[None, :]
    return 2.0 * math.pi / double_len * (row_ids * col_ids % double_len).astype(jnp.float32)


def tables(span_len):
    double_len = 2 * span_len
    first = angles(double_len, span_len, double_len)
    forward_in = jnp.concatenate([jnp.cos(first), -jnp.sin(first)], 0).astype(jnp.bfloat16)
    second = angles(double_len, double_len, double_len)
    forward_taps = jnp.concatenate([jnp.cos(second), -jnp.sin(second)], 0).astype(jnp.bfloat16)
    third = angles(span_len, double_len, double_len)
    inverse = (jnp.concatenate([jnp.cos(third), -jnp.sin(third)], 1) / double_len).astype(
        jnp.bfloat16
    )
    return (forward_in, forward_taps, inverse)


def body(inputs, w_in, conv_taps, skip_gain, filter_taps, w_out):
    span_len, width_dev = inputs.shape
    double_len = 2 * span_len
    groups = lax.axis_size("ctx")
    position = lax.axis_index("ctx")
    w_flat = w_in.reshape(w_in.shape[0], 3 * width_dev)
    projected = jnp.dot(
        lax.all_gather(inputs, "chan", axis=1, tiled=True),
        w_flat,
        preferred_element_type=jnp.float32,
    )
    by_stream = projected.astype(jnp.bfloat16).reshape(span_len, 3, width_dev)
    rim_rows = from_behind(by_stream[span_len - (KERNEL - 1) :], "ctx", 1)
    padded = jnp.concatenate([rim_rows, by_stream], 0)
    filtered = jnp.zeros((span_len, 3, width_dev), jnp.float32)
    for lag in range(KERNEL):
        start_row = KERNEL - 1 - lag
        filtered = filtered + conv_taps[lag].astype(jnp.float32) * padded[
            start_row : start_row + span_len
        ].astype(jnp.float32)
    streams = filtered.astype(jnp.bfloat16)
    gate_out = streams[:, 0]
    gated_in = (streams[:, 1].astype(jnp.float32) * streams[:, 2].astype(jnp.float32)).astype(
        jnp.bfloat16
    )
    forward_in, forward_taps, inverse = tables(span_len)
    all_taps = lax.all_gather(filter_taps[None], "ctx", axis=0, tiled=True)
    previous = jnp.concatenate(
        [jnp.zeros((1, span_len, width_dev), jnp.bfloat16), all_taps[:-1]], 0
    )
    padded_taps = jnp.concatenate(
        [all_taps, jnp.zeros((groups, 1, width_dev), jnp.bfloat16), previous[:, 1:]], 1
    )
    spectra_taps = jnp.einsum(
        "fm,kmd->kfd", forward_taps, padded_taps, preferred_element_type=jnp.float32
    ).astype(jnp.bfloat16)

    def accumulate(spectra):
        pieces = spectra.shape[0]
        lag_index = position - jnp.arange(pieces, dtype=jnp.int32)
        causal = lag_index >= 0
        chosen = jnp.take(spectra_taps, jnp.clip(lag_index, 0, groups - 1), axis=0)
        real_g = chosen[:, :double_len].astype(jnp.float32)
        imag_g = chosen[:, double_len:].astype(jnp.float32)
        real_u = spectra[:, :double_len].astype(jnp.float32)
        imag_u = spectra[:, double_len:].astype(jnp.float32)
        product = jnp.concatenate(
            [real_g * real_u - imag_g * imag_u, real_g * imag_u + imag_g * real_u], 1
        )
        product = jnp.where(causal[:, None, None], product, 0.0)
        return jnp.sum(product, axis=0)

    empty = jnp.zeros((2 * double_len, width_dev), jnp.float32)
    incoming = lax.all_gather(gated_in[None], "ctx", axis=0, tiled=True)

    def transform(current):
        spectra = jnp.einsum(
            "fb,mbc->mfc", forward_in, incoming, preferred_element_type=jnp.float32
        ).astype(jnp.bfloat16)
        return accumulate(spectra)

    def unchanged(current):
        return current

    mixture = lax.cond(jnp.int32(0) <= position, transform, unchanged, empty)
    long_out = jnp.dot(inverse, mixture.astype(jnp.bfloat16), preferred_element_type=jnp.float32)
    long_out = long_out + skip_gain * gated_in.astype(jnp.float32)
    gated_out = (gate_out.astype(jnp.float32) * long_out).astype(jnp.bfloat16)
    shares = lax.psum_scatter(
        lax.dot_general(
            w_out, gated_out, (((0,), (1,)), ((), ())), preferred_element_type=jnp.float32
        ).astype(jnp.bfloat16),
        "chan",
        scatter_dimension=0,
        tiled=True,
    ).astype(jnp.float32)
    result = shares.T.astype(jnp.bfloat16)
    return result


def solution(mesh):
    return jax.shard_map(
        body,
        mesh=mesh,
        in_specs=(
            P("ctx", "chan"),
            P(None, None, "chan"),
            P(None, None, "chan"),
            P("chan"),
            P("ctx", "chan"),
            P("chan", None),
        ),
        out_specs=P("ctx", "chan"),
        check_vma=False,
    )
```

profile of v0, /device:TPU:1, one launch (start us, length us, event | category | flops | bytes accessed | tf_op | source)
XLA Modules:
  0.0 359.7 jit_solution(12032733363743126009)
XLA Ops:
  6.5 0.0 copy-start
  6.5 0.0 all-gather.6.cloned.1.call-start
  6.5 0.7 all-gather.6.cloned.1.call-update
  7.3 0.0 all-gather.8.cloned.1.call-start
  7.3 0.7 all-gather.8.cloned.1.call-update
  8.0 0.0 all-gather.10.cloned.1.call-start
  8.1 4.8 %copy.23 = bf16[4096,3,128]{0,2,1:T(8,128)(2,1)} copy(bf16[4096,3,128]{2,0,1:T(8,128)(2,1)} %param.9) | data formatting | bytes 6291456 | tf_op args[1]
  12.8 9.3 %negate_convert_fusion.1 = (bf16[1024,512]{1,0:T(8,128)(2,1)}, bf16[1024,512]{1,0:T(8,128)(2,1)}) fusion(), kind=kLoop, calls=%fused_computation.56 | loop fusion | flops 8912896 | bytes 2097152 | tf_op jit(solution)/shard_map/convert.8
  22.1 63.5 %all-gather.6.cloned.1.call-done = bf16[512,4096]{1,0:T(8,128)(2,1)} async-done(((bf16[512,128]{1,0:T(8,128)(2,1)}), bf16[512,4096]{1,0:T(8,128)(2,1)}) %all-gather.6.cloned.1.call-update) | async-done | bytes 4194320 | tf_op jit(solution)/shard_map/all_gather | solution.py:43
  85.7 0.0 copy-start.2
  85.7 5.5 %convolution_convert_fusion.1 = bf16[512,384]{1,0:T(8,128)(2,1)S(1)} fusion(bf16[512,4096]{1,0:T(8,128)(2,1)} %all-gather.6.cloned.1.call-done, bf16[4096,384]{0,1:T(8,128)(2,1)} %bitcast.54), kind=kOutput, calls=%fused_computation.66 | convolution fusion | flops 1610809344 | bytes 7733248 | tf_op jit(solution)/shard_map/dot_general | solution.py:42
  91.2 4.6 %collective-permute-start = (bf16[2,3,128]{2,0,1:T(2,128)(2,1)S(1)}, bf16[2,3,128]{2,0,1:T(2,128)(2,1)S(1)}, u32[]{:S(2)}, u32[]{:S(2)}) collective-permute-start(bf16[2,3,128]{2,0,1:T(2,128)(2,1)S(1)} %slice_bitcast_fusion.2), channel_id=1, source_target_pairs={{0,32},{32,64},{64,96},{96,128},{128,160},{160,192},{192,224},{1,3... | collective-permute-start | bytes 4616 | tf_op jit(solution)/shard_map/ppermute | solution.py:14
  95.8 0.0 copy-done.2
  95.8 0.2 copy.24
  96.0 0.2 copy.25
  96.2 0.3 collective-permute-done
  96.5 0.3 add_convert_fusion
  96.8 0.7 multiply_convert_fusion
  97.5 0.0 all-gather.10.cloned.1.call-update
  97.5 0.2 reduce-scatter.4.cloned.1.call-start
  97.7 9.1 %sine_negate_fusion = (f32[512,1024]{1,0:T(8,128)S(1)}, f32[512,1024]{1,0:T(8,128)}) fusion(), kind=kLoop, calls=%fused_computation.60 | loop fusion | flops 7864320 | bytes 4194304 | tf_op jit(solution)/shard_map/neg | solution.py:30
  106.8 3.0 pad_maximum_fusion
  109.8 17.8 %negate_convert_fusion = (bf16[1024,1024]{1,0:T(8,128)(2,1)}, bf16[1024,1024]{1,0:T(8,128)(2,1)}) fusion(), kind=kLoop, calls=%fused_computation.34 | loop fusion | flops 17825792 | bytes 4194304 | tf_op jit(solution)/shard_map/convert.6
  127.6 9.9 %all-gather.8.cloned.1.call-done = bf16[4096,128]{1,0:T(8,128)(2,1)} async-done(((bf16[512,128]{1,0:T(8,128)(2,1)}), bf16[4096,128]{1,0:T(8,128)(2,1)}) %all-gather.8.cloned.1.call-update) | async-done | bytes 1048592 | tf_op jit(solution)/shard_map/all_gather | solution.py:62
  137.6 2.2 slice.71
  139.7 2.3 copy.28
  142.0 2.3 copy.29
  144.3 1.6 pad_slice_fusion
  145.9 9.1 %convert_bitcast_fusion.1 = bf16[8,2048,128]{1,2,0:T(8,128)(2,1)} fusion(bf16[1024,1024]{1,0:T(8,128)(2,1)} %get-tuple-element.40, bf16[1024,1024]{1,0:T(8,128)(2,1)} %get-tuple-element.41, bf16[8,511,128]{1,2,0:T(8,128)(2,1)S(1)} %pad_slice_fusion, bf16[8,512,128]{1,2,0:T(8,128)(2,1)} %copy.29, bf16[1024]{0:T(1024)(128)(2,1)S(1)} %pad.8.clone), kind=kOutput, calls=%fused_computation.33 | convolution fusion | flops 4311744512 | bytes 10485760 | tf_op jit(solution)/shard_map/fm,kmd->kfd/dot_general | solution.py:69
  154.9 37.1 %all-gather.10.cloned.1.call-done = bf16[4096,1,128]{2,0,1:T(8,128)(2,1)} async-done(((bf16[512,1,128]{2,0,1:T(8,128)(2,1)}), bf16[4096,1,128]{2,0,1:T(8,128)(2,1)}) %all-gather.10.cloned.1.call-update) | async-done | bytes 1048592 | tf_op jit(solution)/shard_map/all_gather | solution.py:89
  192.0 0.0 copy-start.3
  192.0 28.0 %conditional.1 = (bf16[2048,128]{0,1:T(8,128)(2,1)}) conditional(s32[]{:T(128)} %convert_element_type.147, () %tuple.13, (s32[]{:T(128)}, bf16[8,2048,128]{1,2,0:T(8,128)(2,1)}, bf16[8,512,128]{2,1,0:T(8,128)(2,1)}, bf16[2048,512]{1,0:T(8,128)(2,1)}) %tuple.35), branch_computations={%region_0.1_spmd, %region_1.3_spmd} | conditional | flops 2168194048 | bytes 79171784 | solution.py:100
  192.0 6.5 %copy.30 = bf16[8,2048,128]{2,1,0:T(8,128)(2,1)} copy(bf16[8,2048,128]{1,2,0:T(8,128)(2,1)} %get-tuple-element.30) | data formatting | bytes 8388608 | tf_op jit(solution)/shard_map
  198.5 5.2 %gather_fusion = bf16[8,2048,128]{2,1,0:T(8,128)(2,1)} fusion(bf16[8,2048,128]{2,1,0:T(8,128)(2,1)} %copy.30, s32[1024]{0:T(1024)S(1)} %pad_clamp_fusion), kind=kCustom, calls=%fused_computation | custom fusion | bytes 8388640 | tf_op jit(solution)/shard_map/cond/branch_1_fun/jit(_take)/gather | solution.py:77
  203.7 6.5 %copy.22 = bf16[8,2048,128]{1,2,0:T(8,128)(2,1)} copy(bf16[8,2048,128]{2,1,0:T(8,128)(2,1)} %gather_fusion) | data formatting | bytes 8388608 | tf_op jit(solution)/shard_map/cond/branch_1_fun/jit(_take)/gather | solution.py:77
  210.3 0.0 copy-start.1
  210.3 0.0 copy-start.4
  210.3 2.8 broadcast_select_fusion
  213.1 0.0 copy-done.1
  213.1 0.3 copy-done.4
  213.4 2.4 convert_bitcast_fusion
  215.8 2.1 fusion.1
  217.9 2.1 fusion
  220.0 0.0 copy-done
  220.0 0.0 copy-done.3
  220.0 5.5 %fusion.6 = bf16[4096,512]{0,1:T(8,128)(2,1)} fusion(bf16[128,4096]{1,0:T(8,128)(2,1)S(1)} %copy-done, bf16[2048,128]{0,1:T(8,128)(2,1)} %get-tuple-element.46, f32[512,1024]{1,0:T(8,128)S(1)} %get-tuple-element.44, f32[512,1024]{1,0:T(8,128)} %get-tuple-element.45, bf16[512,3,128]{2,0,1:T(8,128)(2,1)S(1)} %add_convert_fusion, ...), kind=kOutput, calls=%fused_computation.23 | convolution fusion | flops 810942464 | bytes 10224128 | tf_op jit(solution)/shard_map/dot_general | solution.py:105
  225.5 6.5 %copy.33 = bf16[4096,512]{1,0:T(8,128)(2,1)} copy(bf16[4096,512]{0,1:T(8,128)(2,1)} %fusion.6) | data formatting | bytes 8388608
  232.1 0.0 reduce-scatter.4.cloned.1.call-update
  232.1 119.4 %reduce-scatter.4.cloned.1.call-done = bf16[128,512]{1,0:T(8,128)(2,1)} async-done(((bf16[4096,512]{1,0:T(8,128)(2,1)}), bf16[128,512]{1,0:T(8,128)(2,1)}) %reduce-scatter.4.cloned.1.call-update) | async-done | bytes 131088
  351.5 1.7 copy.34
  (6 shorter events, 0.0 us)
Async XLA Ops:
  6.5 213.5 %copy-start = (bf16[128,4096]{1,0:T(8,128)(2,1)S(1)}, bf16[128,4096]{1,0:T(8,128)(2,1)}, u32[]{:S(2)}) copy-start(bf16[128,4096]{1,0:T(8,128)(2,1)} %param.13) | copy-start | bytes 3145732
  6.5 79.1 %all-gather.6.cloned.1.call-start = ((), (), s32[]{:S(2)}) async-start(), calls=%async_computation.1 | async-start | bytes 4325376 | tf_op jit(solution)/shard_map/all_gather | solution.py:43
  7.3 130.3 %all-gather.8.cloned.1.call-start = ((), (), s32[]{:S(2)}) async-start(), calls=%async_computation.2 | async-start | bytes 1179648 | tf_op jit(solution)/shard_map/all_gather | solution.py:62
  8.0 184.0 %all-gather.10.cloned.1.call-start = ((), (), s32[]{:S(2)}) async-start(), calls=%async_computation.3 | async-start | bytes 1179648 | tf_op jit(solution)/shard_map/all_gather | solution.py:89
  85.7 10.1 %copy-start.2 = (bf16[3,3,128]{2,1,0:T(4,128)(2,1)S(1)}, bf16[3,3,128]{2,1,0:T(4,128)(2,1)}, u32[]{:S(2)}) copy-start(bf16[3,3,128]{2,1,0:T(4,128)(2,1)} %param.10) | copy-start | bytes 6916
  91.2 5.3 %collective-permute-start = (bf16[2,3,128]{2,0,1:T(2,128)(2,1)S(1)}, bf16[2,3,128]{2,0,1:T(2,128)(2,1)S(1)}, u32[]{:S(2)}, u32[]{:S(2)}) collective-permute-start(bf16[2,3,128]{2,0,1:T(2,128)(2,1)S(1)} %slice_bitcast_fusion.2), channel_id=1, source_target_pairs={{0,32},{32,64},{64,96},{96,128},{128,160},{160,192},{192,224},{1,3... | collective-permute-start | bytes 4616 | tf_op jit(solution)/shard_map/ppermute | solution.py:14
  97.5 254.0 %reduce-scatter.4.cloned.1.call-start = ((), (), s32[]{:S(2)}) async-start(), calls=%async_computation.4 | async-start | bytes 4325376
  192.0 28.0 %copy-start.3 = (f32[128]{0:T(128)S(1)}, f32[128]{0:T(128)}, u32[]{:S(2)}) copy-start(f32[128]{0:T(128)} %param.11) | copy-start | bytes 1540
  210.3 2.9 copy-start.1
  210.3 3.1 copy-start.4
Sparse Core Ops, SparseCore 0:
  9.1 76.4 all-gather.5
  88.3 49.2 all-gather.7
  140.2 51.7 all-gather.9
  232.2 119.2 reduce-scatter.3
where the time goes:
time: 364 us; the launch traced here: 360 us
  waiting for transfers between devices  232 us (64%)
  other arithmetic  47.2 us (13%)
  local copies, waits for them, and re-layouts  40.2 us (11%)
  matrix products  22.5 us (6%)
  between operations  13.2 us (4%)
  starting transfers between devices  4.88 us (1%)
    unnamed x5, waiting for transfers between devices  121 us
    all_gather x1, waiting for transfers between devices, body(): lax.all_gather(inputs, 'chan', axis=1, tiled=True)  63.5 us
    all_gather x1, waiting for transfers between devices, body(): incoming = lax.all_gather(gated_in[None], 'ctx', axis=0, tiled=True)  37.1 us
    another operation x2, other arithmetic  27.1 us
    unnamed x9, local copies, waits for them, and re-layouts  13 us
    gather x2, local copies, waits for them, and re-layouts, accumulate(): chosen = jnp.take(spectra_taps, jnp.clip(lag_index, 0, groups - 1), axis=0)  11.8 us
    all_gather x1, waiting for transfers between devices, body(): all_taps = lax.all_gather(filter_taps[None], 'ctx', axis=0, tiled=True)  9.93 us
    neg x1, other arithmetic, tables(): -jnp.sin(third)  9.1 us
  transfers between devices with their start and end apart: 5, of which 5 were waited for; matrix products, arithmetic and copies ran while one was open for 19% of the time, Pallas kernels for 0%

commit v1 on v0

v1 whole, which is shorter than its diff:
```python
import math

import jax
import jax.numpy as jnp
from jax import lax
from jax.sharding import PartitionSpec as P

KERNEL = 3


def dft_table(double_len):
    step = 32
    hi_ids = jnp.arange(double_len // step, dtype=jnp.int32)[:, None]
    lo_ids = jnp.arange(step, dtype=jnp.int32)[:, None]
    cols = jnp.arange(double_len, dtype=jnp.int32)[None, :]
    scale = 2.0 * math.pi / double_len
    hi_angle = scale * (hi_ids * step * cols % double_len).astype(jnp.float32)
    lo_angle = scale * (lo_ids * cols % double_len).astype(jnp.float32)
    hc, hs = jnp.cos(hi_angle)[:, None], jnp.sin(hi_angle)[:, None]
    lc, ls = jnp.cos(lo_angle)[None], jnp.sin(lo_angle)[None]
    cos = (hc * lc - hs * ls).reshape(double_len, double_len)
    sin = (hs * lc + hc * ls).reshape(double_len, double_len)
    return jnp.concatenate([cos, -sin], 0).astype(jnp.bfloat16)


def body(inputs, w_in, conv_taps, skip_gain, filter_taps, w_out):
    span_len, width_dev = inputs.shape
    double_len = 2 * span_len
    groups = lax.axis_size("ctx")
    position = lax.axis_index("ctx")
    own = width_dev // groups

    with jax.named_scope("out_weight_columns"):
        w_cols = lax.all_to_all(w_out, "chan", 1, 0, tiled=True)

    with jax.named_scope("filter_to_owner"):
        taps_t = filter_taps.T.reshape(groups, own, span_len)
        taps_t = lax.all_to_all(taps_t, "ctx", 0, 0, tiled=True)

    with jax.named_scope("input_projection"):
        inputs_t = lax.all_gather(inputs.T, "chan", axis=0, tiled=True)
        w_flat = w_in.reshape(w_in.shape[0], 3 * width_dev)
        proj_t = lax.dot_general(
            w_flat, inputs_t, (((0,), (0,)), ((), ())), preferred_element_type=jnp.float32
        ).astype(jnp.bfloat16)

    with jax.named_scope("projection_to_owner"):
        proj_t = proj_t.reshape(3, groups, own, span_len)
        proj_t = lax.all_to_all(proj_t, "ctx", 1, 1, tiled=True)

    with jax.named_scope("short_conv"):
        start = position * own
        taps = lax.dynamic_slice_in_dim(conv_taps, start, own, axis=2)
        rim = jnp.pad(proj_t[:, :-1, :, span_len - (KERNEL - 1) :], ((0, 0), (1, 0), (0, 0), (0, 0)))
        padded = jnp.concatenate([rim, proj_t], 3)
        filtered = jnp.zeros(proj_t.shape, jnp.float32)
        for lag in range(KERNEL):
            start_row = KERNEL - 1 - lag
            filtered = filtered + taps[lag].astype(jnp.float32)[:, None, :, None] * padded[
                ..., start_row : start_row + span_len
            ].astype(jnp.float32)
        streams = filtered.astype(jnp.bfloat16)
        gate_out = streams[0]
        gated_in = (streams[1].astype(jnp.float32) * streams[2].astype(jnp.float32)).astype(
            jnp.bfloat16
        )

    with jax.named_scope("spectra"):
        table = dft_table(double_len)
        forward_in = table[:, :span_len]
        spectra_in = jnp.einsum(
            "jdb,fb->jdf", gated_in, forward_in, preferred_element_type=jnp.float32
        ).astype(jnp.bfloat16)
        previous = jnp.pad(taps_t[:-1, :, 1:], ((1, 0), (0, 0), (0, 0)))
        padded_taps = jnp.concatenate(
            [taps_t, jnp.zeros((groups, own, 1), jnp.bfloat16), previous], 2
        )
        spectra_taps = jnp.einsum(
            "kdm,fm->kdf", padded_taps, table, preferred_element_type=jnp.float32
        ).astype(jnp.bfloat16)

    with jax.named_scope("mixture"):
        real_g = spectra_taps[:, :, :double_len].astype(jnp.float32)
        imag_g = spectra_taps[:, :, double_len:].astype(jnp.float32)
        real_u = spectra_in[:, :, :double_len].astype(jnp.float32)
        imag_u = spectra_in[:, :, double_len:].astype(jnp.float32)
        mixed = []
        for target in range(groups):
            acc_r = jnp.zeros((own, double_len), jnp.float32)
            acc_i = jnp.zeros((own, double_len), jnp.float32)
            for source in range(target + 1):
                lag = target - source
                acc_r = acc_r + (real_g[lag] * real_u[source] - imag_g[lag] * imag_u[source])
                acc_i = acc_i + (real_g[lag] * imag_u[source] + imag_g[lag] * real_u[source])
            mixed.append(jnp.concatenate([acc_r, acc_i], 1))
        mixture = jnp.stack(mixed, 0).astype(jnp.bfloat16)

    with jax.named_scope("inverse_and_gate"):
        long_out = jnp.einsum(
            "idf,fa->ida", mixture, forward_in, preferred_element_type=jnp.float32
        ) * (1.0 / double_len)
        gain = lax.dynamic_slice_in_dim(skip_gain, start, own)
        long_out = long_out + gain[None, :, None] * gated_in.astype(jnp.float32)
        gated_out = (gate_out.astype(jnp.float32) * long_out).astype(jnp.bfloat16)

    with jax.named_scope("gated_back_to_rows"):
        gated_out = lax.all_to_all(gated_out, "ctx", 0, 0, tiled=True)
        gated_out = gated_out.reshape(width_dev, span_len)

    with jax.named_scope("output_projection"):
        gathered = lax.all_gather(gated_out, "chan", axis=0, tiled=True)
        result = lax.dot_general(
            gathered, w_cols, (((0,), (0,)), ((), ())), preferred_element_type=jnp.float32
        ).astype(jnp.bfloat16)
    return result


def solution(mesh):
    return jax.shard_map(
        body,
        mesh=mesh,
        in_specs=(
            P("ctx", "chan"),
            P(None, None, "chan"),
            P(None, None, "chan"),
            P("chan"),
            P("ctx", "chan"),
            P("chan", None),
        ),
        out_specs=P("ctx", "chan"),
        check_vma=False,
    )
```

time: 364 us -> 209 us (0.57)
  waiting for transfers between devices: 232 us -> 96.6 us
  blocking collectives: 0 us -> 54.1 us
  other arithmetic: 47.2 us -> 6.84 us
  local copies, waits for them, and re-layouts: 40.2 us -> 8.15 us
  starting transfers between devices: 4.88 us -> 13.9 us
  matrix products: 22.5 us -> 14.9 us
    unnamed x5 -> x2, waiting for transfers between devices: 121 us -> 0.73 us
    all_to_all x0 -> x2, blocking collectives: none -> 54.1 us  [the longest x1 44.2 us: body(): w_cols = lax.all_to_all(w_out, 'chan', 1, 0, tiled=True)]
    another operation x2 -> x12, other arithmetic: 27.1 us -> 4.64 us
    all_gather x3 -> x2, waiting for transfers between devices: 111 us -> 89.8 us  [the longest x1 61.2 us: body(): inputs_t = lax.all_gather(inputs.T, 'chan', axis=0, tiled=True)]
    all_to_all x0 -> x2, starting transfers between devices: none -> 13.8 us  [the longest x1 7.48 us: body(): taps_t = lax.all_to_all(taps_t, 'ctx', 0, 0, tiled=True)]
    gather x2 -> x0, local copies, waits for them, and re-layouts: 11.8 us -> none  [accumulate(): chosen = jnp.take(spectra_taps, jnp.clip(lag_index, 0, groups - 1), axis=0)]
    neg x1 -> x0, other arithmetic: 9.1 us -> none  [tables(): -jnp.sin(third)]
    unnamed x9 -> x17, local copies, waits for them, and re-layouts: 13 us -> 4.57 us
  transfers between devices with their start and end apart: 5 -> 4, of which waited for: 5 -> 3; matrix products, arithmetic and copies ran while one was open for 19% -> 7% of each run, Pallas kernels for 0% -> 0%
where the time goes in v1:
time: 209 us; the launch traced here: 208 us
  waiting for transfers between devices  96.6 us (46%)
  blocking collectives  54.1 us (26%)
  matrix products  14.9 us (7%)
  starting transfers between devices  13.9 us (7%)
  between operations  13.7 us (7%)
  local copies, waits for them, and re-layouts  8.15 us (4%)
  other arithmetic  6.84 us (3%)
    all_gather x1, waiting for transfers between devices, body(): inputs_t = lax.all_gather(inputs.T, 'chan', axis=0, tiled=True)  61.2 us
    all_to_all x1, blocking collectives, body(): w_cols = lax.all_to_all(w_out, 'chan', 1, 0, tiled=True)  44.2 us
    all_gather x1, waiting for transfers between devices, body(): gathered = lax.all_gather(gated_out, 'chan', axis=0, tiled=True)  28.6 us
    all_to_all x1, blocking collectives, body(): gated_out = lax.all_to_all(gated_out, 'ctx', 0, 0, tiled=True)  9.83 us
    all_to_all x1, starting transfers between devices, body(): taps_t = lax.all_to_all(taps_t, 'ctx', 0, 0, tiled=True)  7.48 us
    all_to_all x1, starting transfers between devices, body(): proj_t = lax.all_to_all(proj_t, 'ctx', 1, 1, tiled=True)  6.35 us
    all_to_all x1, waiting for transfers between devices, body(): proj_t = lax.all_to_all(proj_t, 'ctx', 1, 1, tiled=True)  6.07 us
    dot_general x1, matrix products, body(): lax.dot_general(w_flat, inputs_t, (((0,), (0,)), ((), ())), preferred_ele...  5.1 us
  transfers between devices with their start and end apart: 4, of which 3 were waited for; matrix products, arithmetic and copies ran while one was open for 7% of the time, Pallas kernels for 0%

profile of v1, /device:TPU:1, one launch (start us, length us, event | category | flops | bytes accessed | tf_op | source)
XLA Modules:
  0.0 208.1 jit_solution(4928286048202900547)
XLA Ops:
  6.5 0.0 copy-start
  6.5 0.0 all-gather.3.cloned.1.call-start
  6.5 0.7 all-gather.3.cloned.1.call-update
  7.3 1.9 copy.19
  9.1 7.5 %all-to-all-start.1 = ((bf16[8,16,512]{2,1,0:T(8,128)(2,1)}), bf16[8,16,512]{2,1,0:T(8,128)(2,1)S(1)}, u32[]{:S(2)}, u32[]{:S(2)}) async-start(bf16[8,16,512]{2,1,0:T(8,128)(2,1)} %bitcast.8), calls=%async_computation.1 | async-start | bytes 262144 | tf_op jit(solution)/shard_map/filter_to_owner/all_to_all | solution.py:38
  16.6 0.5 fusion.45
  17.2 0.6 fusion.48
  17.8 3.5 %negate_convert_fusion = (bf16[32,32,1024]{2,1,0:T(8,128)(2,1)}, bf16[32,32,1024]{2,1,0:T(8,128)(2,1)}) fusion(f32[32,1024]{1,0:T(8,128)S(1)} %get-tuple-element.22, f32[32,1024]{1,0:T(8,128)S(1)} %get-tuple-element.21, f32[32,1024]{1,0:T(8,128)S(1)} %get-tuple-element.23, f32[32,1024]{1,0:T(8,128)S(1)} %get-tuple-element.20), kind=kLoop, calls=%fused_computation.5 | loop fusion | flops 9437184 | bytes 4718592 | tf_op jit(solution)/shard_map/convert.44
  21.3 0.0 copy-start.6
  21.3 0.0 copy-start.5
  21.3 0.0 copy-done
  21.3 2.9 %copy.14 = bf16[4096,3,128]{0,2,1:T(8,128)(2,1)} copy(bf16[4096,3,128]{2,0,1:T(8,128)(2,1)S(1)} %copy-done) | data formatting | bytes 6291456 | tf_op args[1]
  24.2 0.0 copy-done.6
  24.2 0.1 dynamic_slice.7
  24.3 0.0 copy-done.5
  24.3 0.1 fusion.68
  24.3 0.0 all-to-all-done.1
  24.4 0.0 copy-start.4
  24.4 0.1 slice.145
  24.5 61.2 %all-gather.3.cloned.1.call-done = bf16[4096,512]{0,1:T(8,128)(2,1)} async-done(((bf16[128,512]{0,1:T(8,128)(2,1)}), bf16[4096,512]{0,1:T(8,128)(2,1)}) %all-gather.3.cloned.1.call-update) | async-done | bytes 4194320 | tf_op jit(solution)/shard_map/input_projection/all_gather | solution.py:41
  85.6 0.0 copy-start.1
  85.6 5.1 %convolution_convert_fusion.1 = bf16[384,512]{1,0:T(8,128)(2,1)S(1)} fusion(bf16[4096,384]{0,1:T(8,128)(2,1)} %bitcast.117, bf16[4096,512]{0,1:T(8,128)(2,1)} %all-gather.3.cloned.1.call-done), kind=kOutput, calls=%fused_computation.11 | convolution fusion | flops 1610809344 | bytes 7733248 | tf_op jit(solution)/shard_map/input_projection/dot_general | solution.py:43
  90.7 0.0 copy-done.4
  90.7 0.8 copy.15
  91.5 6.4 %all-to-all-start = ((bf16[3,8,16,512]{3,2,0,1:T(8,128)(2,1)}), bf16[3,8,16,512]{3,2,0,1:T(8,128)(2,1)S(1)}, u32[]{:S(2)}, u32[]{:S(2)}) async-start(bf16[3,8,16,512]{3,2,0,1:T(8,128)(2,1)} %copy.15), calls=%async_computation | async-start | bytes 786432 | tf_op jit(solution)/shard_map/projection_to_owner/all_to_all | solution.py:49
  97.9 0.0 all-gather.5.cloned.1.call-start
  97.9 0.0 copy-done.1
  97.9 3.2 %fusion.3 = bf16[8,16,2048]{2,1,0:T(8,128)(2,1)S(1)} fusion(bf16[1024,1024]{1,0:T(8,128)(2,1)S(1)} %bitcast.118, bf16[1024,1024]{1,0:T(8,128)(2,1)} %bitcast.121, bf16[7,16,511]{2,1,0:T(8,128)(2,1)S(1)} %slice.145, bf16[8,16,512]{2,1,0:T(8,128)(2,1)} %copy-done.4, bf16[1024]{0:T(1024)(128)(2,1)S(1)} %pad.29.clone), kind=kOutput, calls=%fused_computation.7 | convolution fusion | flops 546570240 | bytes 4966176 | tf_op jit(solution)/shard_map/spectra/kdm,fm->kdf/dot_general | solution.py:78
  101.1 0.1 slice_convert_fusion.3
  101.2 6.1 %all-to-all-done = bf16[3,8,16,512]{3,2,0,1:T(8,128)(2,1)S(1)} async-done(((bf16[3,8,16,512]{3,2,0,1:T(8,128)(2,1)}), bf16[3,8,16,512]{3,2,0,1:T(8,128)(2,1)S(1)}, u32[]{:S(2)}, u32[]{:S(2)}) %all-to-all-start) | async-done | bytes 393248 | tf_op jit(solution)/shard_map/projection_to_owner/all_to_all | solution.py:49
  107.3 0.1 slice.141
  107.4 0.2 fusion.13
  107.7 0.4 add_convert_fusion
  108.0 2.0 convolution_convert_fusion
  110.1 0.1 slice_convert_fusion.2
  110.2 0.2 fusion.63
  110.4 0.2 fusion.64
  110.5 0.1 fusion.61
  110.7 0.1 fusion.62
  110.8 0.1 fusion.59
  110.9 0.1 fusion.60
  111.1 0.0 copy-start.2
  111.1 0.1 fusion.57
  111.1 0.1 fusion.58
  111.2 0.1 fusion.55
  111.3 0.1 fusion.56
  111.4 0.1 fusion.54
  111.5 0.1 fusion.53
  111.5 0.0 copy-start.3
  111.7 1.0 copy-done.2
  112.6 0.5 fusion.10
  113.1 9.8 %all_to_all.34 = bf16[8,16,512]{2,1,0:T(8,128)(2,1)} all-to-all(bf16[8,16,512]{2,1,0:T(8,128)(2,1)S(1)} %fusion.10), channel_id=1, replica_groups=mesh['ctx'=8,'chan'=32] {'ctx'}, dimensions={0} | all-to-all | bytes 262144 | tf_op jit(solution)/shard_map/gated_back_to_rows/all_to_all | solution.py:107
  122.9 0.0 all-gather.5.cloned.1.call-update
  123.0 0.0 copy-done.3
  123.0 0.7 copy.20
  123.7 44.2 %all_to_all.35 = bf16[128,32,128]{0,2,1:T(8,128)(2,1)S(1)} all-to-all(bf16[128,32,128]{0,2,1:T(8,128)(2,1)S(1)} %bitcast.116), channel_id=1, replica_groups=mesh['ctx'=8,'chan'=32] {'chan'}, dimensions={1} | all-to-all | bytes 2097152 | tf_op jit(solution)/shard_map/out_weight_columns/all_to_all | solution.py:34
  167.9 0.7 copy.21
  168.6 28.6 %all-gather.5.cloned.1.call-done = bf16[4096,512]{1,0:T(8,128)(2,1)} async-done(((bf16[128,512]{1,0:T(8,128)(2,1)}), bf16[4096,512]{1,0:T(8,128)(2,1)}) %all-gather.5.cloned.1.call-update) | async-done | bytes 4194320 | tf_op jit(solution)/shard_map/output_projection/all_gather | solution.py:111
  197.1 4.1 %convolution_convert_fusion.2 = bf16[512,128]{1,0:T(8,128)(2,1)} fusion(bf16[4096,512]{1,0:T(8,128)(2,1)} %all-gather.5.cloned.1.call-done, bf16[4096,128]{1,0:T(8,128)(2,1)S(1)} %bitcast.124), kind=kOutput, calls=%fused_computation.15 | convolution fusion | flops 536936448 | bytes 5373952 | tf_op jit(solution)/shard_map/output_projection/dot_general | solution.py:112
  (12 shorter events, 0.1 us)
Async XLA Ops:
  6.5 14.8 %copy-start = (bf16[4096,3,128]{2,0,1:T(8,128)(2,1)S(1)}, bf16[4096,3,128]{2,0,1:T(8,128)(2,1)}, u32[]{:S(2)}) copy-start(bf16[4096,3,128]{2,0,1:T(8,128)(2,1)} %param.7) | copy-start | bytes 9437188
  6.5 79.1 %all-gather.3.cloned.1.call-start = ((), (), s32[]{:S(2)}) async-start(), calls=%async_computation.4 | async-start | bytes 4325376 | tf_op jit(solution)/shard_map/input_projection/all_gather | solution.py:41
  9.1 15.2 %all-to-all-start.1 = ((bf16[8,16,512]{2,1,0:T(8,128)(2,1)}), bf16[8,16,512]{2,1,0:T(8,128)(2,1)S(1)}, u32[]{:S(2)}, u32[]{:S(2)}) async-start(bf16[8,16,512]{2,1,0:T(8,128)(2,1)} %bitcast.8), calls=%async_computation.1 | async-start | bytes 262144 | tf_op jit(solution)/shard_map/filter_to_owner/all_to_all | solution.py:38
  21.3 2.9 %copy-start.6 = (f32[128]{0:T(128)S(1)}, f32[128]{0:T(128)}, u32[]{:S(2)}) copy-start(f32[128]{0:T(128)} %param.9) | copy-start | bytes 1540
  21.3 3.0 %copy-start.5 = (bf16[3,3,128]{2,1,0:T(4,128)(2,1)S(1)}, bf16[3,3,128]{2,1,0:T(4,128)(2,1)}, u32[]{:S(2)}) copy-start(bf16[3,3,128]{2,1,0:T(4,128)(2,1)} %param.8) | copy-start | bytes 6916
  24.4 66.4 %copy-start.4 = (bf16[8,16,512]{2,1,0:T(8,128)(2,1)}, bf16[8,16,512]{2,1,0:T(8,128)(2,1)S(1)}, u32[]{:S(2)}) copy-start(bf16[8,16,512]{2,1,0:T(8,128)(2,1)S(1)} %all-to-all-done.1) | copy-start | bytes 393220
  85.6 12.3 %copy-start.1 = (bf16[32,32,1024]{2,1,0:T(8,128)(2,1)S(1)}, bf16[32,32,1024]{2,1,0:T(8,128)(2,1)}, u32[]{:S(2)}) copy-start(bf16[32,32,1024]{2,1,0:T(8,128)(2,1)} %get-tuple-element.15) | copy-start | bytes 6291460
  91.5 15.8 %all-to-all-start = ((bf16[3,8,16,512]{3,2,0,1:T(8,128)(2,1)}), bf16[3,8,16,512]{3,2,0,1:T(8,128)(2,1)S(1)}, u32[]{:S(2)}, u32[]{:S(2)}) async-start(bf16[3,8,16,512]{3,2,0,1:T(8,128)(2,1)} %copy.15), calls=%async_computation | async-start | bytes 786432 | tf_op jit(solution)/shard_map/projection_to_owner/all_to_all | solution.py:49
  97.9 99.3 %all-gather.5.cloned.1.call-start = ((), (), s32[]{:S(2)}) async-start(), calls=%async_computation.5 | async-start | bytes 4325376 | tf_op jit(solution)/shard_map/output_projection/all_gather | solution.py:111
  111.1 1.6 copy-start.2
  111.5 11.4 %copy-start.3 = (bf16[128,4096]{1,0:T(8,128)(2,1)S(1)}, bf16[128,4096]{1,0:T(8,128)(2,1)}, u32[]{:S(2)}) copy-start(bf16[128,4096]{1,0:T(8,128)(2,1)} %param.11) | copy-start | bytes 3145732
Sparse Core Ops, SparseCore 0:
  9.1 76.4 all-gather.2
  123.1 74.0 all-gather.4

commit v2 on v1

--- a/solution.py
+++ b/solution.py
@@ -1,11 +1,116 @@
 import math
+
+import functools
 
 import jax
 import jax.numpy as jnp
 from jax import lax
+from jax.experimental import pallas as pl
+from jax.experimental.pallas import tpu as pltpu
 from jax.sharding import PartitionSpec as P
 
 KERNEL = 3
+MESH = pl.DeviceIdType.MESH
+PER_Z = 4
+
+
+def gather_kernel(chips, x_ref, out_ref, local_sem, cross_send, cross_recv, ring_send, ring_recv,
+                  sib_send, sib_recv):
+    row = lax.axis_index("ctx")
+    me = lax.axis_index("chan")
+    z = me // PER_Z
+    y_lo = (me // 2) % 2
+    core = me % 2
+    way = 1 - 2 * core
+    after = ((z + way + chips) % chips) * PER_Z + y_lo * 2 + core
+    before = ((z - way + chips) % chips) * PER_Z + y_lo * 2 + core
+    sibling = me + 1 - 2 * core
+    across = me + 2 - 4 * y_lo
+    diagonal = across + 1 - 2 * core
+    partners = (sibling, across, diagonal)
+
+    barrier = pltpu.get_barrier_semaphore()
+    for peer in partners + (after, before):
+        pl.semaphore_signal(barrier, inc=1, device_id=(row, peer), device_id_type=MESH)
+    pl.semaphore_wait(barrier, 5)
+
+    local = pltpu.make_async_copy(x_ref, out_ref.at[me], local_sem)
+    local.start()
+
+    def cross(k, peer, slot):
+        return pltpu.make_async_remote_copy(
+            src_ref=x_ref, dst_ref=out_ref.at[slot], send_sem=cross_send.at[k],
+            recv_sem=cross_recv.at[k], device_id=(row, peer), device_id_type=MESH)
+
+    for k, peer in enumerate(partners):
+        cross(k, peer, me).start()
+    local.wait()
+    for k, peer in enumerate(partners):
+        cross(k, peer, me).wait_send()
+        cross(k, peer, peer).wait_recv()
+
+    def group(chip):
+        return out_ref.at[pl.ds(pl.multiple_of(chip * PER_Z, PER_Z), PER_Z)]
+
+    def ring(s, chip):
+        return pltpu.make_async_remote_copy(
+            src_ref=group(chip), dst_ref=group(chip), send_sem=ring_send.at[s],
+            recv_sem=ring_recv.at[s], device_id=(row, after), device_id_type=MESH)
+
+    def sib(s, chip):
+        return pltpu.make_async_remote_copy(
+            src_ref=group(chip), dst_ref=group(chip), send_sem=sib_send.at[s],
+            recv_sem=sib_recv.at[s], device_id=(row, sibling), device_id_type=MESH)
+
+    longest = chips // 2
+    for s in range(longest):
+        active = jnp.logical_or(core == 0, s < chips - 1 - longest)
+        sent = (z - way * s + chips) % chips
+        got = (z - way * (s + 1) + chips) % chips
+
+        @pl.when(active)
+        def _():
+            ring(s, sent).start()
+            ring(s, got).wait_recv()
+            sib(s, got).start()
+
+    for s in range(longest):
+        active = jnp.logical_or(core == 0, s < chips - 1 - longest)
+        sent = (z - way * s + chips) % chips
+        got = (z - way * (s + 1) + chips) % chips
+        other = jnp.logical_or(core == 1, s < chips - 1 - longest)
+        theirs = (z + way * (s + 1) + chips) % chips
+
+        @pl.when(active)
+        def _():
+            ring(s, sent).wait_send()
+            sib(s, got).wait_send()
+
+        @pl.when(other)
+        def _():
+            sib(s, theirs).wait_recv()
+
+
+def chan_gather(x, collective_id):
+    size = lax.axis_size("chan")
+    chips = size // PER_Z
+    longest = chips // 2
+    return pl.pallas_call(
+        functools.partial(gather_kernel, chips),
+        out_shape=jax.ShapeDtypeStruct((size,) + x.shape, x.dtype),
+        in_specs=[pl.BlockSpec(memory_space=pltpu.VMEM)],
+        out_specs=pl.BlockSpec(memory_space=pltpu.VMEM),
+        scratch_shapes=[
+            pltpu.SemaphoreType.DMA(()),
+            pltpu.SemaphoreType.DMA((3,)),
+            pltpu.SemaphoreType.DMA((3,)),
+            pltpu.SemaphoreType.DMA((longest,)),
+            pltpu.SemaphoreType.DMA((longest,)),
+            pltpu.SemaphoreType.DMA((longest,)),
+            pltpu.SemaphoreType.DMA((longest,)),
+        ],
+        compiler_params=pltpu.CompilerParams(collective_id=collective_id, has_side_effects=True),
+    )(x).reshape(size * x.shape[0], x.shape[1])
 
 
 def dft_table(double_len):
@@ -38,7 +143,7 @@
         taps_t = lax.all_to_all(taps_t, "ctx", 0, 0, tiled=True)
 
     with jax.named_scope("input_projection"):
-        inputs_t = lax.all_gather(inputs.T, "chan", axis=0, tiled=True)
+        inputs_t = chan_gather(inputs.T, 0)
         w_flat = w_in.reshape(w_in.shape[0], 3 * width_dev)
         proj_t = lax.dot_general(
             w_flat, inputs_t, (((0,), (0,)), ((), ())), preferred_element_type=jnp.float32
@@ -108,7 +213,7 @@
         gated_out = gated_out.reshape(width_dev, span_len)
 
     with jax.named_scope("output_projection"):
-        gathered = lax.all_gather(gated_out, "chan", axis=0, tiled=True)
+        gathered = chan_gather(gated_out, 1)
         result = lax.dot_general(
             gathered, w_cols, (((0,), (0,)), ((), ())), preferred_element_type=jnp.float32
         ).astype(jnp.bfloat16)

time: 209 us -> 181 us (0.87)
  Pallas kernels: 0 us -> 113 us
  waiting for transfers between devices: 96.6 us -> 8.98 us
  blocking collectives: 54.1 us -> 0 us
  between operations: 13.7 us -> 0.35 us
  starting transfers between devices: 13.9 us -> 23.5 us
  local copies, waits for them, and re-layouts: 8.15 us -> 12.2 us
    pallas_call x0 -> x2, Pallas kernels: none -> 113 us  [chan_gather(): pl.pallas_call(functools.partial(gather_kernel, chips), out_shape=jax.Sha...]
    all_gather x2 -> x0, waiting for transfers between devices: 89.8 us -> none  [the longest x1 61.2 us: body(): inputs_t = lax.all_gather(inputs.T, 'chan', axis=0, tiled=True)]
    all_to_all x2 -> x0, blocking collectives: 54.1 us -> none  [the longest x1 44.2 us: body(): w_cols = lax.all_to_all(w_out, 'chan', 1, 0, tiled=True)]
    all_to_all x0 -> x2, starting transfers between devices: none -> 9.41 us  [the longest x1 6.04 us: body(): w_cols = lax.all_to_all(w_out, 'chan', 1, 0, tiled=True)]
    all_to_all x0 -> x2, waiting for transfers between devices: none -> 3.77 us  [the longest x1 3.77 us: body(): gated_out = lax.all_to_all(gated_out, 'ctx', 0, 0, tiled=True)]
    unnamed x17 -> x18, local copies, waits for them, and re-layouts: 4.57 us -> 7.2 us
  transfers between devices with their start and end apart: 4 -> 4, of which waited for: 3 -> 2; matrix products, arithmetic and copies ran while one was open for 7% -> 12% of each run, Pallas kernels for 0% -> 63%
where the time goes in v2:
time: 181 us; the launch traced here: 180 us
  Pallas kernels  113 us (62%)
  starting transfers between devices  23.5 us (13%)
  matrix products  15.5 us (9%)
  local copies, waits for them, and re-layouts  12.2 us (7%)
  waiting for transfers between devices  8.98 us (5%)
  other arithmetic  6.81 us (4%)
    pallas_call x2, Pallas kernels, chan_gather(): pl.pallas_call(functools.partial(gather_kernel, chips), out_shape=jax.Sha...  113 us
    all_to_all x1, starting transfers between devices, body(): taps_t = lax.all_to_all(taps_t, 'ctx', 0, 0, tiled=True)  7.48 us
    unnamed x18, local copies, waits for them, and re-layouts  7.2 us
    all_to_all x1, starting transfers between devices, body(): proj_t = lax.all_to_all(proj_t, 'ctx', 1, 1, tiled=True)  6.61 us
    all_to_all x1, starting transfers between devices, body(): w_cols = lax.all_to_all(w_out, 'chan', 1, 0, tiled=True)  6.04 us
    all_to_all x1, waiting for transfers between devices, body(): proj_t = lax.all_to_all(proj_t, 'ctx', 1, 1, tiled=True)  5.21 us
    dot_general x1, matrix products, body(): lax.dot_general(w_flat, inputs_t, (((0,), (0,)), ((), ())), preferred_ele...  4.96 us
    dot_general x1, matrix products, body(): lax.dot_general(gathered, w_cols, (((0,), (0,)), ((), ())), preferred_ele...  4.15 us
  transfers between devices with their start and end apart: 4, of which 2 were waited for; matrix products, arithmetic and copies ran while one was open for 12% of the time, Pallas kernels for 63%

profile of v2, /device:TPU:1, one launch (start us, length us, event | category | flops | bytes accessed | tf_op | source)
XLA Modules:
  0.0 180.3 jit_solution(6729454889576091104)
XLA Ops:
  0.0 0.0 copy-start
  0.0 1.8 copy.22
  1.8 7.5 %all-to-all-start.1 = ((bf16[8,16,512]{2,1,0:T(8,128)(2,1)}), bf16[8,16,512]{2,1,0:T(8,128)(2,1)}, u32[]{:S(2)}, u32[]{:S(2)}) async-start(bf16[8,16,512]{2,1,0:T(8,128)(2,1)} %bitcast.9), calls=%async_computation.1 | async-start | bytes 262144 | tf_op jit(solution)/shard_map/filter_to_owner/all_to_all | solution.py:143
  9.3 1.2 fusion.47
  10.5 1.7 copy.17
  12.2 51.2 %input_projection.1 = bf16[32,128,512]{2,1,0:T(8,128)(2,1)} custom-call(bf16[128,512]{1,0:T(8,128)(2,1)} %bitcast.130), custom_call_target="tpu_custom_call" | custom-call | tf_op jit(solution)/shard_map/input_projection/pallas_call | solution.py:98
  63.4 0.0 copy-done
  63.4 2.9 %copy.16 = bf16[4096,3,128]{0,2,1:T(8,128)(2,1)} copy(bf16[4096,3,128]{2,0,1:T(8,128)(2,1)S(1)} %copy-done) | data formatting | bytes 6291456 | tf_op args[1]
  66.3 0.6 fusion.50
  66.9 0.0 copy-start.3
  66.9 0.0 copy-start.4
  66.9 5.0 %convolution_convert_fusion.1 = bf16[384,512]{1,0:T(8,128)(2,1)S(1)} fusion(bf16[4096,384]{0,1:T(8,128)(2,1)} %bitcast.122, bf16[4096,512]{1,0:T(8,128)(2,1)} %bitcast.120), kind=kOutput, calls=%fused_computation.11 | convolution fusion | flops 1610809344 | bytes 7733248 | tf_op jit(solution)/shard_map/input_projection/dot_general | solution.py:148
  71.8 0.0 copy-start.6
  71.9 0.0 copy-start.5
  71.9 0.0 copy-done.3
  71.9 0.0 copy-done.4
  71.9 2.8 %negate_convert_fusion = (bf16[32,32,1024]{2,1,0:T(8,128)(2,1)S(1)}, bf16[32,32,1024]{2,1,0:T(8,128)(2,1)}) fusion(f32[32,1024]{1,0:T(8,128)S(1)} %copy-done.3, f32[32,1024]{1,0:T(8,128)S(1)} %get-tuple-element.21, f32[32,1024]{1,0:T(8,128)S(1)} %copy-done.4, f32[32,1024]{1,0:T(8,128)S(1)} %get-tuple-element.20), kind=kLoop, calls=%fused_computation.5 | loop fusion | flops 9437184 | bytes 4718592 | tf_op jit(solution)/shard_map/convert.44
  74.7 0.8 copy.18
  75.5 0.0 copy-done.6
  75.5 0.1 dynamic_slice.7
  75.5 0.0 copy-done.5
  75.5 0.1 fusion.70
  75.6 0.0 all-to-all-done.1
  75.6 6.6 %all-to-all-start = ((bf16[3,8,16,512]{3,2,0,1:T(8,128)(2,1)}), bf16[3,8,16,512]{3,2,0,1:T(8,128)(2,1)S(1)}, u32[]{:S(2)}, u32[]{:S(2)}) async-start(bf16[3,8,16,512]{3,2,0,1:T(8,128)(2,1)} %copy.18), calls=%async_computation | async-start | bytes 786432 | tf_op jit(solution)/shard_map/projection_to_owner/all_to_all | solution.py:154
  82.2 1.0 slice.145
  83.2 3.2 %fusion.3 = bf16[8,16,2048]{2,1,0:T(8,128)(2,1)S(1)} fusion(bf16[1024,1024]{1,0:T(8,128)(2,1)S(1)} %bitcast.123, bf16[1024,1024]{1,0:T(8,128)(2,1)} %bitcast.126, bf16[7,16,511]{2,1,0:T(8,128)(2,1)S(1)} %slice.145, bf16[8,16,512]{2,1,0:T(8,128)(2,1)} %all-to-all-done.1, bf16[1024]{0:T(1024)(128)(2,1)S(1)} %pad.29.clone), kind=kOutput, calls=%fused_computation.7 | convolution fusion | flops 546570240 | bytes 4966176 | tf_op jit(solution)/shard_map/spectra/kdm,fm->kdf/dot_general | solution.py:183
  86.4 0.1 slice_convert_fusion.3
  86.5 5.2 %all-to-all-done = bf16[3,8,16,512]{3,2,0,1:T(8,128)(2,1)S(1)} async-done(((bf16[3,8,16,512]{3,2,0,1:T(8,128)(2,1)}), bf16[3,8,16,512]{3,2,0,1:T(8,128)(2,1)S(1)}, u32[]{:S(2)}, u32[]{:S(2)}) %all-to-all-start) | async-done | bytes 393248 | tf_op jit(solution)/shard_map/projection_to_owner/all_to_all | solution.py:154
  91.7 0.1 slice.141
  91.9 0.2 fusion.15
  92.1 0.4 add_convert_fusion
  92.5 2.0 %convolution_convert_fusion = bf16[8,16,2048]{2,1,0:T(8,128)(2,1)S(1)} fusion(bf16[1024,1024]{1,0:T(8,128)(2,1)} %bitcast.127, bf16[1024,1024]{1,0:T(8,128)(2,1)S(1)} %bitcast.124, bf16[3,8,16,512]{3,2,1,0:T(8,128)(2,1)S(1)} %add_convert_fusion), kind=kOutput, calls=%fused_computation.8 | convolution fusion | flops 273154048 | bytes 4980736 | tf_op jit(solution)/shard_map/spectra/jdb,fb->jdf/dot_general | solution.py:176
  94.5 0.1 slice_convert_fusion.2
  94.6 0.2 fusion.65
  94.8 0.2 fusion.66
  95.0 0.1 fusion.63
  95.1 0.1 fusion.64
  95.3 0.1 fusion.61
  95.4 0.1 fusion.62
  95.5 0.0 copy-start.1
  95.5 0.1 fusion.59
  95.6 0.1 fusion.60
  95.7 0.1 fusion.57
  95.8 0.1 fusion.58
  95.9 0.1 fusion.56
  95.9 0.1 fusion.55
  96.1 1.0 copy-done.1
  97.1 1.1 fusion.11
  98.2 3.4 %all-to-all-start.2 = ((bf16[8,16,512]{2,1,0:T(8,128)(2,1)}), bf16[8,16,512]{2,1,0:T(8,128)(2,1)S(1)}, u32[]{:S(2)}, u32[]{:S(2)}) async-start(bf16[8,16,512]{2,1,0:T(8,128)(2,1)} %fusion.11), calls=%async_computation.2 | async-start | bytes 262144 | tf_op jit(solution)/shard_map/gated_back_to_rows/all_to_all | solution.py:212
  101.6 1.6 copy.23
  103.2 1.3 copy.24
  104.5 3.8 %all-to-all-done.2 = bf16[8,16,512]{2,1,0:T(8,128)(2,1)S(1)} async-done(((bf16[8,16,512]{2,1,0:T(8,128)(2,1)}), bf16[8,16,512]{2,1,0:T(8,128)(2,1)S(1)}, u32[]{:S(2)}, u32[]{:S(2)}) %all-to-all-start.2) | async-done | bytes 131104 | tf_op jit(solution)/shard_map/gated_back_to_rows/all_to_all | solution.py:212
  108.3 0.0 copy-start.2
  108.3 6.0 %all-to-all-start.3 = ((bf16[128,32,128]{2,0,1:T(8,128)(2,1)}), bf16[128,32,128]{2,0,1:T(8,128)(2,1)S(1)}, u32[]{:S(2)}, u32[]{:S(2)}) async-start(bf16[128,32,128]{2,0,1:T(8,128)(2,1)} %copy.24), calls=%async_computation.3 | async-start | bytes 2097152 | tf_op jit(solution)/shard_map/out_weight_columns/all_to_all | solution.py:139
  114.4 0.0 copy-done.2
  114.4 61.8 %output_projection.1 = bf16[32,128,512]{2,1,0:T(8,128)(2,1)} custom-call(bf16[128,512]{1,0:T(8,128)(2,1)} %bitcast.129), custom_call_target="tpu_custom_call" | custom-call | tf_op jit(solution)/shard_map/output_projection/pallas_call | solution.py:98
  176.2 0.0 all-to-all-done.3
  176.2 4.1 %fusion.10 = bf16[512,128]{1,0:T(8,128)(2,1)} fusion(bf16[32,128,512]{2,1,0:T(8,128)(2,1)} %output_projection.1, bf16[128,32,128]{2,0,1:T(8,128)(2,1)S(1)} %all-to-all-done.3), kind=kOutput, calls=%fused_computation.16 | convolution fusion | flops 536936448 | bytes 5373952 | tf_op jit(solution)/shard_map/output_projection/dot_general | solution.py:217
  (12 shorter events, 0.1 us)
Async XLA Ops:
  0.0 63.4 %copy-start = (bf16[4096,3,128]{2,0,1:T(8,128)(2,1)S(1)}, bf16[4096,3,128]{2,0,1:T(8,128)(2,1)}, u32[]{:S(2)}) copy-start(bf16[4096,3,128]{2,0,1:T(8,128)(2,1)} %param.7) | copy-start | bytes 9437188
  1.8 73.8 %all-to-all-start.1 = ((bf16[8,16,512]{2,1,0:T(8,128)(2,1)}), bf16[8,16,512]{2,1,0:T(8,128)(2,1)}, u32[]{:S(2)}, u32[]{:S(2)}) async-start(bf16[8,16,512]{2,1,0:T(8,128)(2,1)} %bitcast.9), calls=%async_computation.1 | async-start | bytes 262144 | tf_op jit(solution)/shard_map/filter_to_owner/all_to_all | solution.py:143
  66.9 5.0 %copy-start.3 = (f32[32,1024]{1,0:T(8,128)S(1)}, f32[32,1024]{1,0:T(8,128)}, u32[]{:S(2)}) copy-start(f32[32,1024]{1,0:T(8,128)} %get-tuple-element.22) | copy-start | bytes 393220
  66.9 5.0 %copy-start.4 = (f32[32,1024]{1,0:T(8,128)S(1)}, f32[32,1024]{1,0:T(8,128)}, u32[]{:S(2)}) copy-start(f32[32,1024]{1,0:T(8,128)} %get-tuple-element.23) | copy-start | bytes 393220
  71.8 3.6 %copy-start.6 = (f32[128]{0:T(128)S(1)}, f32[128]{0:T(128)}, u32[]{:S(2)}) copy-start(f32[128]{0:T(128)} %param.9) | copy-start | bytes 1540
  71.9 3.7 %copy-start.5 = (bf16[3,3,128]{2,1,0:T(4,128)(2,1)S(1)}, bf16[3,3,128]{2,1,0:T(4,128)(2,1)}, u32[]{:S(2)}) copy-start(bf16[3,3,128]{2,1,0:T(4,128)(2,1)} %param.8) | copy-start | bytes 6916
  75.6 16.1 %all-to-all-start = ((bf16[3,8,16,512]{3,2,0,1:T(8,128)(2,1)}), bf16[3,8,16,512]{3,2,0,1:T(8,128)(2,1)S(1)}, u32[]{:S(2)}, u32[]{:S(2)}) async-start(bf16[3,8,16,512]{3,2,0,1:T(8,128)(2,1)} %copy.18), calls=%async_computation | async-start | bytes 786432 | tf_op jit(solution)/shard_map/projection_to_owner/all_to_all | solution.py:154
  95.5 1.6 copy-start.1
  98.2 10.1 %all-to-all-start.2 = ((bf16[8,16,512]{2,1,0:T(8,128)(2,1)}), bf16[8,16,512]{2,1,0:T(8,128)(2,1)S(1)}, u32[]{:S(2)}, u32[]{:S(2)}) async-start(bf16[8,16,512]{2,1,0:T(8,128)(2,1)} %fusion.11), calls=%async_computation.2 | async-start | bytes 262144 | tf_op jit(solution)/shard_map/gated_back_to_rows/all_to_all | solution.py:212
  108.3 6.1 %copy-start.2 = (bf16[8,16,512]{2,1,0:T(8,128)(2,1)}, bf16[8,16,512]{2,1,0:T(8,128)(2,1)S(1)}, u32[]{:S(2)}) copy-start(bf16[8,16,512]{2,1,0:T(8,128)(2,1)S(1)} %all-to-all-done.2) | copy-start | bytes 393220
  108.3 67.9 %all-to-all-start.3 = ((bf16[128,32,128]{2,0,1:T(8,128)(2,1)}), bf16[128,32,128]{2,0,1:T(8,128)(2,1)S(1)}, u32[]{:S(2)}, u32[]{:S(2)}) async-start(bf16[128,32,128]{2,0,1:T(8,128)(2,1)} %copy.24), calls=%async_computation.3 | async-start | bytes 2097152 | tf_op jit(solution)/shard_map/out_weight_columns/all_to_all | solution.py:139

commit v3 on v2

--- a/solution.py
+++ b/solution.py
@@ -91,6 +91,48 @@
             sib(s, theirs).wait_recv()
 
 
+def exchange_kernel(groups, x_ref, out_ref, local_sem, send_sem, recv_sem):
+    me = lax.axis_index("ctx")
+    col = lax.axis_index("chan")
+    barrier = pltpu.get_barrier_semaphore()
+    for k in range(1, groups):
+        pl.semaphore_signal(barrier, inc=1, device_id=((me + k) % groups, col),
+                            device_id_type=MESH)
+    pl.semaphore_wait(barrier, groups - 1)
+
+    local = pltpu.make_async_copy(x_ref.at[me], out_ref.at[me], local_sem)
+    local.start()
+
+    def send(k, peer, slot):
+        return pltpu.make_async_remote_copy(
+            src_ref=x_ref.at[peer], dst_ref=out_ref.at[slot], send_sem=send_sem.at[k - 1],
+            recv_sem=recv_sem.at[k - 1], device_id=(peer, col), device_id_type=MESH)
+
+    for k in range(1, groups):
+        send(k, (me + k) % groups, me).start()
+    local.wait()
+    for k in range(1, groups):
+        send(k, (me + k) % groups, me).wait_send()
+        source = (me - k + groups) % groups
+        send(k, source, source).wait_recv()
+
+
+def ctx_exchange(x, collective_id):
+    groups = lax.axis_size("ctx")
+    return pl.pallas_call(
+        functools.partial(exchange_kernel, groups),
+        out_shape=jax.ShapeDtypeStruct(x.shape, x.dtype),
+        in_specs=[pl.BlockSpec(memory_space=pltpu.VMEM)],
+        out_specs=pl.BlockSpec(memory_space=pltpu.VMEM),
+        scratch_shapes=[
+            pltpu.SemaphoreType.DMA(()),
+            pltpu.SemaphoreType.DMA((groups - 1,)),
+            pltpu.SemaphoreType.DMA((groups - 1,)),
+        ],
+        compiler_params=pltpu.CompilerParams(collective_id=collective_id, has_side_effects=True),
+    )(x)
+
+
 def chan_gather(x, collective_id):
     size = lax.axis_size("chan")
     chips = size // PER_Z
@@ -140,7 +182,7 @@
 
     with jax.named_scope("filter_to_owner"):
         taps_t = filter_taps.T.reshape(groups, own, span_len)
-        taps_t = lax.all_to_all(taps_t, "ctx", 0, 0, tiled=True)
+        taps_t = ctx_exchange(taps_t, 2)
 
     with jax.named_scope("input_projection"):
         inputs_t = chan_gather(inputs.T, 0)
@@ -150,23 +192,23 @@
         ).astype(jnp.bfloat16)
 
     with jax.named_scope("projection_to_owner"):
-        proj_t = proj_t.reshape(3, groups, own, span_len)
-        proj_t = lax.all_to_all(proj_t, "ctx", 1, 1, tiled=True)
+        proj_t = proj_t.reshape(3, groups, own, span_len).transpose(1, 0, 2, 3)
+        proj_t = ctx_exchange(proj_t, 3)
 
     with jax.named_scope("short_conv"):
         start = position * own
         taps = lax.dynamic_slice_in_dim(conv_taps, start, own, axis=2)
-        rim = jnp.pad(proj_t[:, :-1, :, span_len - (KERNEL - 1) :], ((0, 0), (1, 0), (0, 0), (0, 0)))
+        rim = jnp.pad(proj_t[:-1, :, :, span_len - (KERNEL - 1) :], ((1, 0), (0, 0), (0, 0), (0, 0)))
         padded = jnp.concatenate([rim, proj_t], 3)
         filtered = jnp.zeros(proj_t.shape, jnp.float32)
         for lag in range(KERNEL):
             start_row = KERNEL - 1 - lag
-            filtered = filtered + taps[lag].astype(jnp.float32)[:, None, :, None] * padded[
+            filtered = filtered + taps[lag].astype(jnp.float32)[None, :, :, None] * padded[
                 ..., start_row : start_row + span_len
             ].astype(jnp.float32)
         streams = filtered.astype(jnp.bfloat16)
-        gate_out = streams[0]
-        gated_in = (streams[1].astype(jnp.float32) * streams[2].astype(jnp.float32)).astype(
+        gate_out = streams[:, 0]
+        gated_in = (streams[:, 1].astype(jnp.float32) * streams[:, 2].astype(jnp.float32)).astype(
             jnp.bfloat16
         )
 
@@ -209,7 +251,7 @@
         gated_out = (gate_out.astype(jnp.float32) * long_out).astype(jnp.bfloat16)
 
     with jax.named_scope("gated_back_to_rows"):
-        gated_out = lax.all_to_all(gated_out, "ctx", 0, 0, tiled=True)
+        gated_out = ctx_exchange(gated_out, 4)
         gated_out = gated_out.reshape(width_dev, span_len)
 
     with jax.named_scope("output_projection"):

time: 181 us -> 184 us (1.017)
  Pallas kernels: 113 us -> 137 us
  starting transfers between devices: 23.5 us -> 11.5 us
  waiting for transfers between devices: 8.98 us -> 0.01 us
    pallas_call x0 -> x3, Pallas kernels: none -> 30.7 us  [ctx_exchange(): pl.pallas_call(functools.partial(exchange_kernel, groups), out_shape=jax....]
    all_to_all x3 -> x0, starting transfers between devices: 17.5 us -> none  [the longest x1 7.48 us: body(): taps_t = lax.all_to_all(taps_t, 'ctx', 0, 0, tiled=True)]
    all_to_all x3 -> x0, waiting for transfers between devices: 8.98 us -> none  [the longest x1 5.21 us: body(): proj_t = lax.all_to_all(proj_t, 'ctx', 1, 1, tiled=True)]
    pallas_call x2, Pallas kernels: 113 us -> 106 us  [chan_gather(): pl.pallas_call(functools.partial(gather_kernel, chips), out_shape=jax.Sha...]
    all_to_all x1, starting transfers between devices: 6.04 us -> 11.5 us  [body(): w_cols = lax.all_to_all(w_out, 'chan', 1, 0, tiled=True)]
    unnamed x18 -> x20, local copies, waits for them, and re-layouts: 7.2 us -> 7.64 us
  transfers between devices with their start and end apart: 4 -> 1, of which waited for: 2 -> 0; matrix products, arithmetic and copies ran while one was open for 12% -> 14% of each run, Pallas kernels for 63% -> 75%
where the time goes in v3:
time: 184 us; the launch traced here: 183 us
  Pallas kernels  137 us (74%)
  matrix products  15.5 us (8%)
  local copies, waits for them, and re-layouts  12.6 us (7%)
  starting transfers between devices  11.5 us (6%)
  other arithmetic  6.79 us (4%)
    pallas_call x2, Pallas kernels, chan_gather(): pl.pallas_call(functools.partial(gather_kernel, chips), out_shape=jax.Sha...  106 us
    pallas_call x3, Pallas kernels, ctx_exchange(): pl.pallas_call(functools.partial(exchange_kernel, groups), out_shape=jax....  30.7 us
    all_to_all x1, starting transfers between devices, body(): w_cols = lax.all_to_all(w_out, 'chan', 1, 0, tiled=True)  11.5 us
    unnamed x20, local copies, waits for them, and re-layouts  7.64 us
    dot_general x1, matrix products, body(): lax.dot_general(w_flat, inputs_t, (((0,), (0,)), ((), ())), preferred_ele...  4.93 us
    dot_general x1, matrix products, body(): lax.dot_general(gathered, w_cols, (((0,), (0,)), ((), ())), preferred_ele...  4.44 us
  transfers between devices with their start and end apart: 1, of which 0 were waited for; matrix products, arithmetic and copies ran while one was open for 14% of the time, Pallas kernels for 75%

profile of v3, /device:TPU:1, one launch (start us, length us, event | category | flops | bytes accessed | tf_op | source)
XLA Modules:
  0.0 183.4 jit_solution(5990501184633228946)
XLA Ops:
  0.0 0.0 copy-start.4
  0.0 1.6 copy.20
  1.7 1.3 copy.21
  3.0 0.0 copy-start
  3.0 11.5 %all-to-all-start = ((bf16[128,32,128]{2,0,1:T(8,128)(2,1)}), bf16[128,32,128]{2,0,1:T(8,128)(2,1)}, u32[]{:S(2)}, u32[]{:S(2)}) async-start(bf16[128,32,128]{2,0,1:T(8,128)(2,1)} %copy.21), calls=%async_computation | async-start | bytes 2097152 | tf_op jit(solution)/shard_map/out_weight_columns/all_to_all | solution.py:181
  14.5 0.5 fusion.47
  15.0 0.0 copy-done.4
  15.0 0.8 copy.14
  15.8 60.5 %input_projection.1 = bf16[32,128,512]{2,1,0:T(8,128)(2,1)} custom-call(bf16[128,512]{1,0:T(8,128)(2,1)} %bitcast.134), custom_call_target="tpu_custom_call" | custom-call | tf_op jit(solution)/shard_map/input_projection/pallas_call | solution.py:140
  76.3 0.0 copy-done
  76.3 2.9 %copy.13 = bf16[4096,3,128]{0,2,1:T(8,128)(2,1)} copy(bf16[4096,3,128]{2,0,1:T(8,128)(2,1)S(1)} %copy-done) | data formatting | bytes 6291456 | tf_op args[1]
  79.2 0.0 copy-start.6
  79.2 4.9 %convolution_convert_fusion.1 = bf16[384,512]{1,0:T(8,128)(2,1)S(1)} fusion(bf16[4096,384]{0,1:T(8,128)(2,1)} %bitcast.125, bf16[4096,512]{1,0:T(8,128)(2,1)} %bitcast.123), kind=kOutput, calls=%fused_computation.11 | convolution fusion | flops 1610809344 | bytes 7733248 | tf_op jit(solution)/shard_map/input_projection/dot_general | solution.py:190
  84.1 0.8 copy.28
  84.9 11.8 %projection_to_owner.1 = bf16[8,3,16,512]{3,2,1,0:T(8,128)(2,1)} custom-call(bf16[8,3,16,512]{3,2,1,0:T(8,128)(2,1)} %bitcast.132), custom_call_target="tpu_custom_call" | custom-call | tf_op jit(solution)/shard_map/projection_to_owner/pallas_call | solution.py:122
  96.7 1.0 slice.141
  97.7 1.2 fusion.15
  98.9 0.6 fusion.50
  99.5 0.0 copy-done.6
  99.5 0.1 fusion.70
  99.6 1.4 add_convert_fusion
  100.9 0.0 copy-start.3
  101.0 1.5 negate_convert_fusion
  102.4 0.0 copy-start.1
  102.4 0.0 copy-start.5
  102.5 1.3 copy-done.1
  103.8 0.8 convolution_convert_fusion
  104.6 0.0 copy-done.3
  104.6 0.1 slice_convert_fusion.2
  104.7 0.0 copy-done.5
  104.7 0.8 copy.19
  105.5 10.3 %filter_to_owner.1 = bf16[8,16,512]{2,1,0:T(8,128)(2,1)} custom-call(bf16[8,16,512]{2,1,0:T(8,128)(2,1)} %bitcast.135), custom_call_target="tpu_custom_call" | custom-call | tf_op jit(solution)/shard_map/filter_to_owner/pallas_call | solution.py:122
  115.9 1.0 slice.101
  116.9 3.2 %fusion.3 = bf16[8,16,2048]{2,1,0:T(8,128)(2,1)S(1)} fusion(bf16[1024,1024]{1,0:T(8,128)(2,1)S(1)} %bitcast.127, bf16[1024,1024]{1,0:T(8,128)(2,1)} %bitcast.130, bf16[7,16,511]{2,1,0:T(8,128)(2,1)S(1)} %slice.101, bf16[8,16,512]{2,1,0:T(8,128)(2,1)} %filter_to_owner.1, bf16[1024]{0:T(1024)(128)(2,1)S(1)} %pad.29.clone), kind=kOutput, calls=%fused_computation.7 | convolution fusion | flops 546570240 | bytes 4966176 | tf_op jit(solution)/shard_map/spectra/kdm,fm->kdf/dot_general | solution.py:225
  120.1 0.1 slice_convert_fusion.3
  120.2 0.1 fusion.61
  120.3 0.0 copy-start.7
  120.3 0.1 fusion.62
  120.4 0.1 fusion.59
  120.5 0.1 fusion.60
  120.6 0.1 fusion.57
  120.7 0.1 fusion.58
  120.8 0.1 fusion.56
  120.8 0.1 fusion.55
  120.9 0.1 copy-done.7
  121.0 0.1 dynamic_slice.7
  121.1 0.0 copy-start.2
  121.1 0.1 fusion.63
  121.3 0.1 fusion.64
  121.4 0.2 fusion.65
  121.6 0.2 fusion.66
  121.8 0.9 copy-done.2
  122.7 2.2 %fusion.11.x_ref = bf16[8,16,512]{2,1,0:T(8,128)(2,1)} fusion(bf16[8,16,2048]{2,1,0:T(8,128)(2,1)S(1)} %fusion.46, bf16[1024,1024]{1,0:T(8,128)(2,1)S(1)} %bitcast.131, bf16[1024,1024]{1,0:T(8,128)(2,1)S(1)} %bitcast.128, bf16[8,3,16,512]{3,2,0,1:T(8,128)(2,1)} %copy-done.3, f32[16]{0:T(128)S(1)} %dynamic_slice.7), kind=kOutput, calls=%fused_computation.17 | convolution fusion | flops 273350656 | bytes 5242944 | tf_op jit(solution)/shard_map/inverse_and_gate/idf,fa->ida/dot_general | solution.py:246
  124.8 8.6 %gated_back_to_rows.1 = bf16[8,16,512]{2,1,0:T(8,128)(2,1)} custom-call(bf16[8,16,512]{2,1,0:T(8,128)(2,1)} %fusion.11.x_ref), custom_call_target="tpu_custom_call" | custom-call | tf_op jit(solution)/shard_map/gated_back_to_rows/pallas_call | solution.py:122
  133.4 45.6 %output_projection.1 = bf16[32,128,512]{2,1,0:T(8,128)(2,1)} custom-call(bf16[128,512]{1,0:T(8,128)(2,1)} %bitcast.133), custom_call_target="tpu_custom_call" | custom-call | tf_op jit(solution)/shard_map/output_projection/pallas_call | solution.py:140
  179.0 0.0 all-to-all-done
  179.0 4.4 %fusion.10 = bf16[512,128]{1,0:T(8,128)(2,1)} fusion(bf16[32,128,512]{2,1,0:T(8,128)(2,1)} %output_projection.1, bf16[128,32,128]{2,0,1:T(8,128)(2,1)} %all-to-all-done), kind=kOutput, calls=%fused_computation.16 | convolution fusion | flops 536936448 | bytes 5373952 | tf_op jit(solution)/shard_map/output_projection/dot_general | solution.py:259
  (12 shorter events, 0.1 us)
Async XLA Ops:
  0.0 15.0 %copy-start.4 = (bf16[512,128]{1,0:T(8,128)(2,1)S(1)}, bf16[512,128]{1,0:T(8,128)(2,1)}, u32[]{:S(2)}) copy-start(bf16[512,128]{1,0:T(8,128)(2,1)} %param.6) | copy-start | bytes 393220
  3.0 73.3 %copy-start = (bf16[4096,3,128]{2,0,1:T(8,128)(2,1)S(1)}, bf16[4096,3,128]{2,0,1:T(8,128)(2,1)}, u32[]{:S(2)}) copy-start(bf16[4096,3,128]{2,0,1:T(8,128)(2,1)} %param.7) | copy-start | bytes 9437188
  3.0 176.0 %all-to-all-start = ((bf16[128,32,128]{2,0,1:T(8,128)(2,1)}), bf16[128,32,128]{2,0,1:T(8,128)(2,1)}, u32[]{:S(2)}, u32[]{:S(2)}) async-start(bf16[128,32,128]{2,0,1:T(8,128)(2,1)} %copy.21), calls=%async_computation | async-start | bytes 2097152 | tf_op jit(solution)/shard_map/out_weight_columns/all_to_all | solution.py:181
  79.2 20.3 %copy-start.6 = (bf16[3,3,128]{2,1,0:T(4,128)(2,1)S(1)}, bf16[3,3,128]{2,1,0:T(4,128)(2,1)}, u32[]{:S(2)}) copy-start(bf16[3,3,128]{2,1,0:T(4,128)(2,1)} %param.8) | copy-start | bytes 6916
  100.9 3.7 %copy-start.3 = (bf16[8,3,16,512]{3,2,0,1:T(8,128)(2,1)}, bf16[8,3,16,512]{3,2,0,1:T(8,128)(2,1)S(1)}, u32[]{:S(2)}) copy-start(bf16[8,3,16,512]{3,2,0,1:T(8,128)(2,1)S(1)} %add_convert_fusion) | copy-start | bytes 1179652
  102.4 1.3 copy-start.1
  102.4 2.3 %copy-start.5 = (bf16[512,128]{1,0:T(8,128)(2,1)S(1)}, bf16[512,128]{1,0:T(8,128)(2,1)}, u32[]{:S(2)}) copy-start(bf16[512,128]{1,0:T(8,128)(2,1)} %param.10) | copy-start | bytes 393220
  120.3 0.7 copy-start.7
  121.1 1.6 copy-start.2

commit v4 on v3

--- a/solution.py
+++ b/solution.py
@@ -14,8 +14,13 @@
 PER_Z = 4
 
 
-def gather_kernel(chips, x_ref, out_ref, local_sem, cross_send, cross_recv, ring_send, ring_recv,
-                  sib_send, sib_recv):
+def gather_kernel(chips, groups, *refs):
+    if groups:
+        (x_ref, t_ref, out_ref, t_out_ref, local_sem, cross_send, cross_recv, ring_send, ring_recv,
+         sib_send, sib_recv, t_local_sem, t_send, t_recv) = refs
+    else:
+        (x_ref, out_ref, local_sem, cross_send, cross_recv, ring_send, ring_recv,
+         sib_send, sib_recv) = refs
     row = lax.axis_index("ctx")
     me = lax.axis_index("chan")
     z = me // PER_Z
@@ -32,7 +37,16 @@
     barrier = pltpu.get_barrier_semaphore()
     for peer in partners + (after, before):
         pl.semaphore_signal(barrier, inc=1, device_id=(row, peer), device_id_type=MESH)
-    pl.semaphore_wait(barrier, 5)
+    for peer in ctx_peers(groups) if groups else ():
+        pl.semaphore_signal(barrier, inc=1, device_id=(peer, me), device_id_type=MESH)
+    pl.semaphore_wait(barrier, 5 + max(groups - 1, 0))
+
+    if groups:
+        t_local, t_sends, t_receipts = exchange_copies(
+            groups, t_ref, t_out_ref, t_local_sem, t_send, t_recv)
+        t_local.start()
+        for copy in t_sends:
+            copy.start()
 
     local = pltpu.make_async_copy(x_ref, out_ref.at[me], local_sem)
     local.start()
@@ -90,31 +104,48 @@
         def _():
             sib(s, theirs).wait_recv()
 
-
-def exchange_kernel(groups, x_ref, out_ref, local_sem, send_sem, recv_sem):
+    if groups:
+        t_local.wait()
+        for copy, receipt in zip(t_sends, t_receipts):
+            copy.wait_send()
+            receipt.wait_recv()
+
+
+def exchange_copies(groups, x_ref, out_ref, local_sem, send_sem, recv_sem):
     me = lax.axis_index("ctx")
     col = lax.axis_index("chan")
-    barrier = pltpu.get_barrier_semaphore()
-    for k in range(1, groups):
-        pl.semaphore_signal(barrier, inc=1, device_id=((me + k) % groups, col),
-                            device_id_type=MESH)
-    pl.semaphore_wait(barrier, groups - 1)
-
     local = pltpu.make_async_copy(x_ref.at[me], out_ref.at[me], local_sem)
-    local.start()
 
     def send(k, peer, slot):
         return pltpu.make_async_remote_copy(
             src_ref=x_ref.at[peer], dst_ref=out_ref.at[slot], send_sem=send_sem.at[k - 1],
             recv_sem=recv_sem.at[k - 1], device_id=(peer, col), device_id_type=MESH)
 
-    for k in range(1, groups):
-        send(k, (me + k) % groups, me).start()
+    sends = [send(k, (me + k) % groups, me) for k in range(1, groups)]
+    sources = [(me - k + groups) % groups for k in range(1, groups)]
+    receipts = [send(k, source, source) for k, source in zip(range(1, groups), sources)]
+    return local, sends, receipts
+
+
+def ctx_peers(groups):
+    me = lax.axis_index("ctx")
+    return [(me + k) % groups for k in range(1, groups)]
+
+
+def exchange_kernel(groups, x_ref, out_ref, local_sem, send_sem, recv_sem):
+    col = lax.axis_index("chan")
+    barrier = pltpu.get_barrier_semaphore()
+    for peer in ctx_peers(groups):
+        pl.semaphore_signal(barrier, inc=1, device_id=(peer, col), device_id_type=MESH)
+    pl.semaphore_wait(barrier, groups - 1)
+    local, sends, receipts = exchange_copies(groups, x_ref, out_ref, local_sem, send_sem, recv_sem)
+    local.start()
+    for copy in sends:
+        copy.start()
     local.wait()
-    for k in range(1, groups):
-        send(k, (me + k) % groups, me).wait_send()
-        source = (me - k + groups) % groups
-        send(k, source, source).wait_recv()
+    for copy, receipt in zip(sends, receipts):
+        copy.wait_send()
+        receipt.wait_recv()
 
 
 def ctx_exchange(x, collective_id):
@@ -133,26 +164,39 @@
     )(x)
 
 
-def chan_gather(x, collective_id):
+def chan_gather(x, t, collective_id):
     size = lax.axis_size("chan")
+    groups = lax.axis_size("ctx") if t is not None else 0
     chips = size // PER_Z
     longest = chips // 2
-    return pl.pallas_call(
-        functools.partial(gather_kernel, chips),
-        out_shape=jax.ShapeDtypeStruct((size,) + x.shape, x.dtype),
-        in_specs=[pl.BlockSpec(memory_space=pltpu.VMEM)],
-        out_specs=pl.BlockSpec(memory_space=pltpu.VMEM),
-        scratch_shapes=[
+    operands = (x,) if t is None else (x, t)
+    out_shape = [jax.ShapeDtypeStruct((size,) + x.shape, x.dtype)]
+    scratch = [
+        pltpu.SemaphoreType.DMA(()),
+        pltpu.SemaphoreType.DMA((3,)),
+        pltpu.SemaphoreType.DMA((3,)),
+        pltpu.SemaphoreType.DMA((longest,)),
+        pltpu.SemaphoreType.DMA((longest,)),
+        pltpu.SemaphoreType.DMA((longest,)),
+        pltpu.SemaphoreType.DMA((longest,)),
+    ]
+    if t is not None:
+        out_shape.append(jax.ShapeDtypeStruct(t.shape, t.dtype))
+        scratch += [
             pltpu.SemaphoreType.DMA(()),
-            pltpu.SemaphoreType.DMA((3,)),
-            pltpu.SemaphoreType.DMA((3,)),
-            pltpu.SemaphoreType.DMA((longest,)),
-            pltpu.SemaphoreType.DMA((longest,)),
-            pltpu.SemaphoreType.DMA((longest,)),
-            pltpu.SemaphoreType.DMA((longest,)),
-        ],
+            pltpu.SemaphoreType.DMA((groups - 1,)),
+            pltpu.SemaphoreType.DMA((groups - 1,)),
+        ]
+    outs = pl.pallas_call(
+        functools.partial(gather_kernel, chips, groups),
+        out_shape=tuple(out_shape),
+        in_specs=[pl.BlockSpec(memory_space=pltpu.VMEM)] * len(operands),
+        out_specs=[pl.BlockSpec(memory_space=pltpu.VMEM)] * len(out_shape),
+        scratch_shapes=scratch,
         compiler_params=pltpu.CompilerParams(collective_id=collective_id, has_side_effects=True),
-    )(x).reshape(size * x.shape[0], x.shape[1])
+    )(*operands)
+    gathered = outs[0].reshape(size * x.shape[0], x.shape[1])
+    return gathered if t is None else (gathered, outs[1])
 
 
 def dft_table(double_len):
@@ -177,15 +221,15 @@
     position = lax.axis_index("ctx")
     own = width_dev // groups
 
+    with jax.named_scope("input_gather_and_filter_to_owner"):
+        taps_t = filter_taps.T.reshape(groups, own, span_len)
+        inputs_t, taps_t = chan_gather(inputs.T, taps_t, 0)
+
     with jax.named_scope("out_weight_columns"):
-        w_cols = lax.all_to_all(w_out, "chan", 1, 0, tiled=True)
-
-    with jax.named_scope("filter_to_owner"):
-        taps_t = filter_taps.T.reshape(groups, own, span_len)
-        taps_t = ctx_exchange(taps_t, 2)
+        w_late, inputs_t = lax.optimization_barrier((w_out, inputs_t))
+        w_cols = lax.all_to_all(w_late, "chan", 1, 0, tiled=True)
 
     with jax.named_scope("input_projection"):
-        inputs_t = chan_gather(inputs.T, 0)
         w_flat = w_in.reshape(w_in.shape[0], 3 * width_dev)
         proj_t = lax.dot_general(
             w_flat, inputs_t, (((0,), (0,)), ((), ())), preferred_element_type=jnp.float32
@@ -213,6 +257,7 @@
         )
 
     with jax.named_scope("spectra"):
+        w_cols, gated_in = lax.optimization_barrier((w_cols, gated_in))
         table = dft_table(double_len)
         forward_in = table[:, :span_len]
         spectra_in = jnp.einsum(
@@ -255,7 +300,7 @@
         gated_out = gated_out.reshape(width_dev, span_len)
 
     with jax.named_scope("output_projection"):
-        gathered = chan_gather(gated_out, 1)
+        gathered = chan_gather(gated_out, None, 1)
         result = lax.dot_general(
             gathered, w_cols, (((0,), (0,)), ((), ())), preferred_element_type=jnp.float32
         ).astype(jnp.bfloat16)

time: 184 us -> 171 us (0.929)
  Pallas kernels: 137 us -> 129 us
  starting transfers between devices: 11.5 us -> 4.29 us
  local copies, waits for them, and re-layouts: 12.6 us -> 15 us
    pallas_call x3 -> x2, Pallas kernels: 30.7 us -> 23.2 us  [ctx_exchange(): pl.pallas_call(functools.partial(exchange_kernel, groups), out_shape=jax....]
    all_to_all x1, starting transfers between devices: 11.5 us -> 4.29 us  [body(): w_cols = lax.all_to_all(w_late, 'chan', 1, 0, tiled=True)]
    optimization_barrier x0 -> x1, local copies, waits for them, and re-layouts: none -> 2.31 us  [body(): w_late, inputs_t = lax.optimization_barrier((w_out, inputs_t))]
    unnamed x20 -> x19, local copies, waits for them, and re-layouts: 7.64 us -> 8.46 us
  transfers between devices with their start and end apart: 1 -> 1, of which waited for: 0 -> 0; matrix products, arithmetic and copies ran while one was open for 14% -> 11% of each run, Pallas kernels for 75% -> 7%
where the time goes in v4:
time: 171 us
  Pallas kernels  129 us (75%)
  local copies, waits for them, and re-layouts  15 us (9%)
  matrix products  14.1 us (8%)
  other arithmetic  7.48 us (4%)
  starting transfers between devices  4.29 us (3%)
    pallas_call x2, Pallas kernels, chan_gather(): pl.pallas_call(functools.partial(gather_kernel, chips, groups), out_shape...  106 us
    pallas_call x2, Pallas kernels, ctx_exchange(): pl.pallas_call(functools.partial(exchange_kernel, groups), out_shape=jax....  23.2 us
    unnamed x19, local copies, waits for them, and re-layouts  8.46 us
    dot_general x1, matrix products, body(): lax.dot_general(w_flat, inputs_t, (((0,), (0,)), ((), ())), preferred_ele...  4.95 us
    all_to_all x1, starting transfers between devices, body(): w_cols = lax.all_to_all(w_late, 'chan', 1, 0, tiled=True)  4.29 us
    dot_general x1, matrix products, body(): lax.dot_general(gathered, w_cols, (((0,), (0,)), ((), ())), preferred_ele...  4.14 us
  transfers between devices with their start and end apart: 1, of which 0 were waited for; matrix products, arithmetic and copies ran while one was open for 11% of the time, Pallas kernels for 7%

profile of v4, /device:TPU:1, one launch (start us, length us, event | category | flops | bytes accessed | tf_op | source)
XLA Modules:
  0.0 170.7 jit_solution(16924062989054512417)
XLA Ops:
  0.0 1.7 copy.19
  1.7 1.7 copy.20
  3.3 56.7 %input_gather_and_filter_to_owner.1 = (bf16[32,128,512]{2,1,0:T(8,128)(2,1)}, bf16[8,16,512]{2,1,0:T(8,128)(2,1)}) custom-call(bf16[128,512]{1,0:T(8,128)(2,1)} %bitcast.132, bf16[8,16,512]{2,1,0:T(8,128)(2,1)} %bitcast.133), custom_call_target="tpu_custom_call" | custom-call | tf_op jit(solution)/shard_map/input_gather_and_filter_to_owner/pallas_call | solution.py:190
  60.1 2.3 %copy.26 = bf16[128,4096]{0,1:T(8,128)(2,1)} copy(bf16[128,4096]{1,0:T(8,128)(2,1)} %param.11) | data formatting | bytes 2097152 | tf_op jit(solution)/shard_map/out_weight_columns/optimization_barrier | solution.py:229
  62.4 4.3 %all-to-all-start = ((bf16[128,32,128]{0,2,1:T(8,128)(2,1)}), bf16[128,32,128]{0,2,1:T(8,128)(2,1)S(1)}, u32[]{:S(2)}, u32[]{:S(2)}) async-start(bf16[128,32,128]{0,2,1:T(8,128)(2,1)} %bitcast.15), calls=%async_computation | async-start | bytes 2097152 | tf_op jit(solution)/shard_map/out_weight_columns/all_to_all | solution.py:230
  66.7 4.7 %copy.21 = bf16[4096,3,128]{0,2,1:T(8,128)(2,1)} copy(bf16[4096,3,128]{2,0,1:T(8,128)(2,1)} %param.7) | data formatting | bytes 6291456 | tf_op args[1]
  71.4 0.0 copy-start.6
  71.4 0.0 copy-start.5
  71.4 0.0 copy-start.7
  71.4 5.0 %convolution_convert_fusion.1 = bf16[512,384]{0,1:T(8,128)(2,1)S(1)} fusion(bf16[4096,384]{0,1:T(8,128)(2,1)} %bitcast.122, bf16[4096,512]{1,0:T(8,128)(2,1)} %bitcast.136), kind=kOutput, calls=%fused_computation.11 | convolution fusion | flops 1610809344 | bytes 7733248 | tf_op jit(solution)/shard_map/input_projection/dot_general | solution.py:234
  76.4 0.0 copy-done.6
  76.4 0.1 fusion.67
  76.5 0.8 copy.32
  77.2 12.0 %projection_to_owner.1 = bf16[8,3,16,512]{3,2,1,0:T(8,128)(2,1)} custom-call(bf16[8,3,16,512]{3,2,1,0:T(8,128)(2,1)} %bitcast.129), custom_call_target="tpu_custom_call" | custom-call | tf_op jit(solution)/shard_map/projection_to_owner/pallas_call | solution.py:153
  89.2 1.0 slice.141
  90.2 0.0 copy-done.5
  90.2 0.1 slice.101
  90.3 0.0 copy-done.7
  90.3 0.1 dynamic_slice.7
  90.4 0.5 fusion.45
  90.9 1.2 fusion.13
  92.2 1.4 add_convert_fusion
  93.5 0.7 fusion.28
  94.2 0.6 fusion.48
  94.8 1.5 negate_convert_fusion
  96.3 0.0 copy-start
  96.3 0.0 copy-start.2
  96.3 1.5 fusion.3
  97.9 0.0 copy-done
  97.9 0.4 copy-done.2
  98.3 0.1 slice_convert_fusion.3
  98.4 0.0 all-to-all-done
  98.4 0.7 copy.27
  99.1 2.4 %convolution_convert_fusion = bf16[8,16,2048]{2,1,0:T(8,128)(2,1)S(1)} fusion(bf16[8,16,512]{2,1,0:T(8,128)(2,1)} %fusion.28, bf16[1024,1024]{1,0:T(8,128)(2,1)} %bitcast.127, bf16[1024,1024]{1,0:T(8,128)(2,1)} %bitcast.124), kind=kOutput, calls=%fused_computation.8 | convolution fusion | flops 272891904 | bytes 4849664 | tf_op jit(solution)/shard_map/spectra/jdb,fb->jdf/dot_general | solution.py:263
  101.5 0.1 slice_convert_fusion.2
  101.6 0.2 fusion.63
  101.8 0.2 fusion.64
  102.0 0.1 fusion.61
  102.1 0.1 fusion.62
  102.3 0.1 fusion.59
  102.4 0.1 fusion.60
  102.5 0.0 copy-start.1
  102.5 0.0 copy-start.3
  102.5 0.0 copy-start.4
  102.5 0.1 fusion.57
  102.6 0.1 fusion.58
  102.7 0.1 fusion.55
  102.8 0.1 fusion.56
  102.9 0.1 fusion.54
  102.9 0.1 fusion.53
  103.1 1.0 copy-done.1
  104.1 0.6 copy-done.3
  104.7 0.0 copy-done.4
  104.7 1.1 fusion.10.x_ref
  105.8 11.3 %gated_back_to_rows.1 = bf16[8,16,512]{2,1,0:T(8,128)(2,1)} custom-call(bf16[8,16,512]{2,1,0:T(8,128)(2,1)} %fusion.10.x_ref), custom_call_target="tpu_custom_call" | custom-call | tf_op jit(solution)/shard_map/gated_back_to_rows/pallas_call | solution.py:153
  117.1 49.5 %output_projection.1 = bf16[32,128,512]{2,1,0:T(8,128)(2,1)} custom-call(bf16[128,512]{1,0:T(8,128)(2,1)} %bitcast.131), custom_call_target="tpu_custom_call" | custom-call | tf_op jit(solution)/shard_map/output_projection/pallas_call | solution.py:190
  166.6 4.1 %convolution_convert_fusion.2 = bf16[512,128]{1,0:T(8,128)(2,1)} fusion(bf16[4096,512]{1,0:T(8,128)(2,1)} %bitcast.120, bf16[4096,128]{1,0:T(8,128)(2,1)S(1)} %bitcast.130), kind=kOutput, calls=%fused_computation.15 | convolution fusion | flops 536936448 | bytes 5373952 | tf_op jit(solution)/shard_map/output_projection/dot_general | solution.py:304
  (12 shorter events, 0.1 us)
Async XLA Ops:
  62.4 36.0 %all-to-all-start = ((bf16[128,32,128]{0,2,1:T(8,128)(2,1)}), bf16[128,32,128]{0,2,1:T(8,128)(2,1)S(1)}, u32[]{:S(2)}, u32[]{:S(2)}) async-start(bf16[128,32,128]{0,2,1:T(8,128)(2,1)} %bitcast.15), calls=%async_computation | async-start | bytes 2097152 | tf_op jit(solution)/shard_map/out_weight_columns/all_to_all | solution.py:230
  71.4 5.0 %copy-start.6 = (bf16[3,3,128]{2,1,0:T(4,128)(2,1)S(1)}, bf16[3,3,128]{2,1,0:T(4,128)(2,1)}, u32[]{:S(2)}) copy-start(bf16[3,3,128]{2,1,0:T(4,128)(2,1)} %param.8) | copy-start | bytes 6916
  71.4 18.8 %copy-start.5 = (bf16[8,16,512]{2,1,0:T(8,128)(2,1)S(1)}, bf16[8,16,512]{2,1,0:T(8,128)(2,1)}, u32[]{:S(2)}) copy-start(bf16[8,16,512]{2,1,0:T(8,128)(2,1)} %get-tuple-element.13) | copy-start | bytes 393220
  71.4 18.9 %copy-start.7 = (f32[128]{0:T(128)S(1)}, f32[128]{0:T(128)}, u32[]{:S(2)}) copy-start(f32[128]{0:T(128)} %param.9) | copy-start | bytes 1540
  96.3 1.5 copy-start
  96.3 2.0 %copy-start.2 = (bf16[32,32,1024]{2,1,0:T(8,128)(2,1)}, bf16[32,32,1024]{2,1,0:T(8,128)(2,1)S(1)}, u32[]{:S(2)}) copy-start(bf16[32,32,1024]{2,1,0:T(8,128)(2,1)S(1)} %get-tuple-element.28) | copy-start | bytes 6291460
  102.5 1.6 copy-start.1
  102.5 2.2 %copy-start.3 = (bf16[32,32,1024]{2,1,0:T(8,128)(2,1)S(1)}, bf16[32,32,1024]{2,1,0:T(8,128)(2,1)}, u32[]{:S(2)}) copy-start(bf16[32,32,1024]{2,1,0:T(8,128)(2,1)} %copy-done.2) | copy-start | bytes 6291460
  102.5 2.2 %copy-start.4 = (bf16[8,16,512]{2,1,0:T(8,128)(2,1)S(1)}, bf16[8,16,512]{2,1,0:T(8,128)(2,1)}, u32[]{:S(2)}) copy-start(bf16[8,16,512]{2,1,0:T(8,128)(2,1)} %fusion.28) | copy-start | bytes 393220

commit v5 on v4

--- a/solution.py
+++ b/solution.py
@@ -223,17 +223,25 @@
 
     with jax.named_scope("input_gather_and_filter_to_owner"):
         taps_t = filter_taps.T.reshape(groups, own, span_len)
-        inputs_t, taps_t = chan_gather(inputs.T, taps_t, 0)
+        inputs_t = inputs.T
+        half = width_dev // 2
+        by_offload = lax.all_gather(inputs_t[:half], "chan", axis=0, tiled=True)
+        by_kernel, taps_t = chan_gather(inputs_t[half:], taps_t, 0)
 
     with jax.named_scope("out_weight_columns"):
-        w_late, inputs_t = lax.optimization_barrier((w_out, inputs_t))
+        w_late, by_kernel = lax.optimization_barrier((w_out, by_kernel))
         w_cols = lax.all_to_all(w_late, "chan", 1, 0, tiled=True)
 
     with jax.named_scope("input_projection"):
-        w_flat = w_in.reshape(w_in.shape[0], 3 * width_dev)
+        w_split = w_in.reshape(-1, width_dev, 3 * width_dev)
         proj_t = lax.dot_general(
-            w_flat, inputs_t, (((0,), (0,)), ((), ())), preferred_element_type=jnp.float32
-        ).astype(jnp.bfloat16)
+            w_split[:, :half].reshape(-1, 3 * width_dev), by_offload, (((0,), (0,)), ((), ())),
+            preferred_element_type=jnp.float32,
+        ) + lax.dot_general(
+            w_split[:, half:].reshape(-1, 3 * width_dev), by_kernel, (((0,), (0,)), ((), ())),
+            preferred_element_type=jnp.float32,
+        )
+        proj_t = proj_t.astype(jnp.bfloat16)
 
     with jax.named_scope("projection_to_owner"):
         proj_t = proj_t.reshape(3, groups, own, span_len).transpose(1, 0, 2, 3)

time: 171 us -> 184 us (1.076)
  Pallas kernels: 129 us -> 111 us
  between operations: 0.37 us -> 13.8 us
  local copies, waits for them, and re-layouts: 15 us -> 26.7 us
  waiting for transfers between devices: 0.01 us -> 8.53 us
  matrix products: 14.1 us -> 11.9 us
    pallas_call x2, Pallas kernels: 106 us -> 89.9 us  [chan_gather(): pl.pallas_call(functools.partial(gather_kernel, chips, groups), out_shape...]
    slice x0 -> x4, local copies, waits for them, and re-layouts: none -> 13.3 us  [the longest x2 7.13 us: body(): w_split[:, half:].reshape(-1, 3 * width_dev)]
    all_to_all x1, waiting for transfers between devices: 0.01 us -> 8.51 us  [body(): w_cols = lax.all_to_all(w_late, 'chan', 1, 0, tiled=True)]
    unnamed x19 -> x20, local copies, waits for them, and re-layouts: 8.46 us -> 5.1 us
    pallas_call x2, Pallas kernels: 23.2 us -> 21 us  [ctx_exchange(): pl.pallas_call(functools.partial(exchange_kernel, groups), out_shape=jax....]
    dot_general x1 -> x2, matrix products: 4.95 us -> 4.23 us  [the longest x1 3.21 us: body(): lax.dot_general(w_split[:, :half].reshape(-1, 3 * width_dev), by_offload,...]
  transfers between devices with their start and end apart: 1 -> 2, of which waited for: 0 -> 1; matrix products, arithmetic and copies ran while one was open for 11% -> 15% of each run, Pallas kernels for 7% -> 24%
where the time goes in v5:
time: 184 us; the launch traced here: 183 us
  Pallas kernels  111 us (60%)
  local copies, waits for them, and re-layouts  26.7 us (15%)
  between operations  13.8 us (8%)
  matrix products  11.9 us (6%)
  waiting for transfers between devices  8.53 us (5%)
  other arithmetic  6.82 us (4%)
  starting transfers between devices  4.47 us (2%)
    pallas_call x2, Pallas kernels, chan_gather(): pl.pallas_call(functools.partial(gather_kernel, chips, groups), out_shape...  89.9 us
    pallas_call x2, Pallas kernels, ctx_exchange(): pl.pallas_call(functools.partial(exchange_kernel, groups), out_shape=jax....  21 us
    all_to_all x1, waiting for transfers between devices, body(): w_cols = lax.all_to_all(w_late, 'chan', 1, 0, tiled=True)  8.51 us
    slice x2, local copies, waits for them, and re-layouts, body(): w_split[:, half:].reshape(-1, 3 * width_dev)  7.13 us
    slice x1, local copies, waits for them, and re-layouts, body(): w_split[:, :half].reshape(-1, 3 * width_dev)  5.54 us
    unnamed x20, local copies, waits for them, and re-layouts  5.1 us
    all_to_all x1, starting transfers between devices, body(): w_cols = lax.all_to_all(w_late, 'chan', 1, 0, tiled=True)  4.46 us
    dot_general x1, matrix products, body(): lax.dot_general(gathered, w_cols, (((0,), (0,)), ((), ())), preferred_ele...  4.14 us
  transfers between devices with their start and end apart: 2, of which 1 were waited for; matrix products, arithmetic and copies ran while one was open for 15% of the time, Pallas kernels for 24%

profile of v5, /device:TPU:1, one launch (start us, length us, event | category | flops | bytes accessed | tf_op | source)
XLA Modules:
  0.0 183.1 jit_solution(11873941863960968064)
XLA Ops:
  6.5 0.0 all-gather.2.cloned.1.call-start
  6.5 1.0 copy.21
  7.5 0.7 fusion.76
  8.2 0.0 all-gather.2.cloned.1.call-update
  8.2 1.7 copy.22
  9.9 44.4 %input_gather_and_filter_to_owner.1 = (bf16[32,64,512]{2,1,0:T(8,128)(2,1)}, bf16[8,16,512]{2,1,0:T(8,128)(2,1)}) custom-call(bf16[64,512]{1,0:T(8,128)(2,1)} %get-tuple-element.32.refs_0_, bf16[8,16,512]{2,1,0:T(8,128)(2,1)} %bitcast.146), custom_call_target="tpu_custom_call" | custom-call | tf_op jit(solution)/shard_map/input_gather_and_filter_to_owner/pallas_call | solution.py:190
  54.3 2.3 %copy.28 = bf16[128,4096]{0,1:T(8,128)(2,1)} copy(bf16[128,4096]{1,0:T(8,128)(2,1)} %param.11) | data formatting | bytes 2097152 | tf_op jit(solution)/shard_map/out_weight_columns/optimization_barrier | solution.py:232
  56.6 4.5 %all-to-all-start = ((bf16[128,32,128]{0,2,1:T(8,128)(2,1)}), bf16[128,32,128]{0,2,1:T(8,128)(2,1)}, u32[]{:S(2)}, u32[]{:S(2)}) async-start(bf16[128,32,128]{0,2,1:T(8,128)(2,1)} %bitcast.16), calls=%async_computation | async-start | bytes 2097152 | tf_op jit(solution)/shard_map/out_weight_columns/all_to_all | solution.py:233
  61.1 3.2 %copy.19 = bf16[4096,3,128]{0,2,1:T(8,128)(2,1)S(1)} copy(bf16[4096,3,128]{2,0,1:T(8,128)(2,1)} %param.7) | data formatting | bytes 6291456 | tf_op args[1]
  64.3 0.8 copy.30
  65.1 3.0 %fusion.75 = (bf16[32,64,384]{1,0,2:T(8,128)(2,1)S(1)}, bf16[32,64,384]{1,0,2:T(8,128)(2,1)}) fusion(bf16[32,128,384]{1,0,2:T(8,128)(2,1)S(1)} %bitcast.132), kind=kLoop, calls=%fused_computation.122 | loop fusion | bytes 6291456 | tf_op jit(solution)/shard_map/input_projection/slice | solution.py:241
  68.2 5.5 %copy.20 = bf16[32,64,384]{2,1,0:T(8,128)(2,1)} copy(bf16[32,64,384]{1,0,2:T(8,128)(2,1)} %get-tuple-element.18) | data formatting | bytes 3145728 | tf_op jit(solution)/shard_map/input_projection/slice | solution.py:238
  73.7 0.0 copy-start.4
  73.7 0.0 copy-start.7
  73.7 0.0 copy-start.5
  73.7 4.1 %copy.23 = bf16[32,64,384]{2,1,0:T(8,128)(2,1)} copy(bf16[32,64,384]{1,0,2:T(8,128)(2,1)S(1)} %get-tuple-element.17) | data formatting | bytes 3145728 | tf_op jit(solution)/shard_map/input_projection/slice | solution.py:241
  77.8 0.0 copy-done.4
  77.8 0.1 slice.113
  77.9 0.0 copy-done.7
  78.0 0.1 dynamic_slice.7
  78.0 0.0 copy-done.5
  78.0 0.1 fusion.69
  78.1 0.5 fusion.47
  78.7 0.6 fusion.50
  79.2 1.5 negate_convert_fusion
  80.7 0.0 copy-start
  80.7 1.5 fusion.3
  82.3 0.0 copy-done
  82.3 0.1 slice_convert_fusion.3
  82.4 8.5 %all-to-all-done = bf16[128,32,128]{0,2,1:T(8,128)(2,1)} async-done(((bf16[128,32,128]{0,2,1:T(8,128)(2,1)}), bf16[128,32,128]{0,2,1:T(8,128)(2,1)}, u32[]{:S(2)}, u32[]{:S(2)}) %all-to-all-start) | async-done | bytes 1048608 | tf_op jit(solution)/shard_map/out_weight_columns/all_to_all | solution.py:233
  90.9 2.3 %copy.29 = bf16[32,128,128]{2,1,0:T(8,128)(2,1)} copy(bf16[32,128,128]{1,2,0:T(8,128)(2,1)} %bitcast.17) | data formatting | bytes 2097152 | tf_op jit(solution)/shard_map/out_weight_columns/all_to_all | solution.py:233
  93.2 0.0 all-gather.2.cloned.1.call-done
  93.2 0.0 copy-start.2
  93.2 0.0 copy-start.6
  93.2 3.2 %fusion.77 = f32[384,512]{1,0:T(8,128)S(1)} fusion(bf16[2048,384]{1,0:T(8,128)(2,1)} %bitcast.142, bf16[2048,512]{1,0:T(8,128)(2,1)} %all-gather.2.cloned.1.call-done), kind=kOutput, calls=%fused_computation.124 | convolution fusion | flops 805306368 | bytes 4456448 | tf_op jit(solution)/shard_map/input_projection/dot_general | solution.py:237
  96.4 0.0 copy-done.2
  96.4 0.0 copy-done.6
  96.4 1.0 fusion.9
  97.4 0.8 copy.35
  98.2 11.5 %projection_to_owner.1 = bf16[8,3,16,512]{3,2,1,0:T(8,128)(2,1)} custom-call(bf16[8,3,16,512]{3,2,1,0:T(8,128)(2,1)} %bitcast.141), custom_call_target="tpu_custom_call" | custom-call | tf_op jit(solution)/shard_map/projection_to_owner/pallas_call | solution.py:153
  109.7 0.0 copy-start.1
  109.7 1.1 slice.157
  110.9 1.2 fusion.15
  112.1 1.4 add_convert_fusion
  113.5 0.0 copy-done.1
  113.5 0.8 convolution_convert_fusion
  114.4 0.1 slice_convert_fusion.2
  114.5 0.2 fusion.65
  114.6 0.2 fusion.66
  114.8 0.1 fusion.63
  115.0 0.1 fusion.64
  115.1 0.1 fusion.61
  115.2 0.1 fusion.62
  115.3 0.1 fusion.59
  115.4 0.1 fusion.60
  115.5 0.1 fusion.57
  115.6 0.1 fusion.58
  115.7 0.1 fusion.56
  115.7 0.1 fusion.55
  115.9 1.1 fusion.12.x_ref
  117.0 9.5 %gated_back_to_rows.1 = bf16[8,16,512]{2,1,0:T(8,128)(2,1)} custom-call(bf16[8,16,512]{2,1,0:T(8,128)(2,1)} %fusion.12.x_ref), custom_call_target="tpu_custom_call" | custom-call | tf_op jit(solution)/shard_map/gated_back_to_rows/pallas_call | solution.py:153
  126.5 45.5 %output_projection.1 = bf16[32,128,512]{2,1,0:T(8,128)(2,1)} custom-call(bf16[128,512]{1,0:T(8,128)(2,1)} %bitcast.145), custom_call_target="tpu_custom_call" | custom-call | tf_op jit(solution)/shard_map/output_projection/pallas_call | solution.py:190
  172.1 0.0 copy-done.3
  172.1 4.1 %convolution_convert_fusion.1 = bf16[512,128]{1,0:T(8,128)(2,1)} fusion(bf16[4096,512]{1,0:T(8,128)(2,1)} %bitcast.134, bf16[4096,128]{1,0:T(8,128)(2,1)S(1)} %bitcast.144), kind=kOutput, calls=%fused_computation.17 | convolution fusion | flops 536936448 | bytes 5373952 | tf_op jit(solution)/shard_map/output_projection/dot_general | solution.py:312
  (14 shorter events, 0.1 us)
Async XLA Ops:
  6.5 86.6 %all-gather.2.cloned.1.call-start = ((), (), s32[]{:S(2)}) async-start(), calls=%async_computation.1 | async-start | bytes 2162688 | tf_op jit(solution)/shard_map/input_gather_and_filter_to_owner/all_gather | solution.py:228
  56.6 34.3 %all-to-all-start = ((bf16[128,32,128]{0,2,1:T(8,128)(2,1)}), bf16[128,32,128]{0,2,1:T(8,128)(2,1)}, u32[]{:S(2)}, u32[]{:S(2)}) async-start(bf16[128,32,128]{0,2,1:T(8,128)(2,1)} %bitcast.16), calls=%async_computation | async-start | bytes 2097152 | tf_op jit(solution)/shard_map/out_weight_columns/all_to_all | solution.py:233
  73.7 4.1 %copy-start.4 = (bf16[8,16,512]{2,1,0:T(8,128)(2,1)S(1)}, bf16[8,16,512]{2,1,0:T(8,128)(2,1)}, u32[]{:S(2)}) copy-start(bf16[8,16,512]{2,1,0:T(8,128)(2,1)} %get-tuple-element.13) | copy-start | bytes 393220
  73.7 4.2 %copy-start.7 = (f32[128]{0:T(128)S(1)}, f32[128]{0:T(128)}, u32[]{:S(2)}) copy-start(f32[128]{0:T(128)} %param.9) | copy-start | bytes 1540
  73.7 4.3 %copy-start.5 = (bf16[3,3,128]{2,1,0:T(4,128)(2,1)S(1)}, bf16[3,3,128]{2,1,0:T(4,128)(2,1)}, u32[]{:S(2)}) copy-start(bf16[3,3,128]{2,1,0:T(4,128)(2,1)} %param.8) | copy-start | bytes 6916
  80.7 1.5 copy-start
  93.2 3.2 %copy-start.2 = (bf16[32,64,384]{2,1,0:T(8,128)(2,1)S(1)}, bf16[32,64,384]{2,1,0:T(8,128)(2,1)}, u32[]{:S(2)}) copy-start(bf16[32,64,384]{2,1,0:T(8,128)(2,1)} %copy.23) | copy-start | bytes 4718596
  93.2 3.2 %copy-start.6 = (bf16[32,64,512]{2,1,0:T(8,128)(2,1)S(1)}, bf16[32,64,512]{2,1,0:T(8,128)(2,1)}, u32[]{:S(2)}) copy-start(bf16[32,64,512]{2,1,0:T(8,128)(2,1)} %get-tuple-element.11) | copy-start | bytes 6291460
  109.7 3.8 %copy-start.1 = (bf16[32,32,1024]{2,1,0:T(8,128)(2,1)S(1)}, bf16[32,32,1024]{2,1,0:T(8,128)(2,1)}, u32[]{:S(2)}) copy-start(bf16[32,32,1024]{2,1,0:T(8,128)(2,1)} %copy-done) | copy-start | bytes 6291460
  117.0 55.0 %copy-start.3 = (bf16[32,128,128]{2,1,0:T(8,128)(2,1)S(1)}, bf16[32,128,128]{2,1,0:T(8,128)(2,1)}, u32[]{:S(2)}) copy-start(bf16[32,128,128]{2,1,0:T(8,128)(2,1)} %copy.29) | copy-start | bytes 3145732
Sparse Core Ops, SparseCore 0:
  9.2 74.2 all-gather.1

commit v6 on v4

--- a/solution.py
+++ b/solution.py
@@ -199,6 +199,92 @@
     return gathered if t is None else (gathered, outs[1])
 
 
+def half_gather_kernel(chips, x_ref, out_ref, local_sem, cross_send, cross_recv, up_send, up_recv,
+                       down_send, down_recv):
+    row = lax.axis_index("ctx")
+    me = lax.axis_index("chan")
+    z = me // PER_Z
+    y_lo = (me // 2) % 2
+    core = me % 2
+    across = me + 2 - 4 * y_lo
+    ahead = ((z + 1) % chips) * PER_Z + y_lo * 2 + core
+    behind = ((z + chips - 1) % chips) * PER_Z + y_lo * 2 + core
+    mine = me // 2
+    theirs = across // 2
+
+    barrier = pltpu.get_barrier_semaphore()
+    for peer in (across, ahead, behind):
+        pl.semaphore_signal(barrier, inc=1, device_id=(row, peer), device_id_type=MESH)
+    pl.semaphore_wait(barrier, 3)
+
+    local = pltpu.make_async_copy(x_ref, out_ref.at[mine], local_sem)
+    local.start()
+
+    def cross(slot):
+        return pltpu.make_async_remote_copy(
+            src_ref=x_ref, dst_ref=out_ref.at[slot], send_sem=cross_send,
+            recv_sem=cross_recv, device_id=(row, across), device_id_type=MESH)
+
+    cross(mine).start()
+    local.wait()
+    cross(mine).wait_send()
+    cross(theirs).wait_recv()
+
+    def pair(chip):
+        return out_ref.at[pl.ds(pl.multiple_of(chip * 2, 2), 2)]
+
+    def up(s, chip):
+        return pltpu.make_async_remote_copy(
+            src_ref=pair(chip), dst_ref=pair(chip), send_sem=up_send.at[s],
+            recv_sem=up_recv.at[s], device_id=(row, ahead), device_id_type=MESH)
+
+    def down(s, chip):
+        return pltpu.make_async_remote_copy(
+            src_ref=pair(chip), dst_ref=pair(chip), send_sem=down_send.at[s],
+            recv_sem=down_recv.at[s], device_id=(row, behind), device_id_type=MESH)
+
+    ups = chips // 2
+    downs = chips - 1 - ups
+    for s in range(ups):
+        if s > 0:
+            up(s - 1, (z - s + chips) % chips).wait_recv()
+        up(s, (z - s + chips) % chips).start()
+        if s < downs:
+            if s > 0:
+                down(s - 1, (z + s) % chips).wait_recv()
+            down(s, (z + s) % chips).start()
+    up(ups - 1, (z - ups + chips) % chips).wait_recv()
+    down(downs - 1, (z + downs) % chips).wait_recv()
+    for s in range(ups):
+        up(s, (z - s + chips) % chips).wait_send()
+    for s in range(downs):
+        down(s, (z + s) % chips).wait_send()
+
+
+def half_gather(x, collective_id):
+    size = lax.axis_size("chan")
+    chips = size // PER_Z
+    ups = chips // 2
+    downs = chips - 1 - ups
+    out = pl.pallas_call(
+        functools.partial(half_gather_kernel, chips),
+        out_shape=jax.ShapeDtypeStruct((size // 2,) + x.shape, x.dtype),
+        in_specs=[pl.BlockSpec(memory_space=pltpu.VMEM)],
+        out_specs=pl.BlockSpec(memory_space=pltpu.VMEM),
+        scratch_shapes=[
+            pltpu.SemaphoreType.DMA(()),
+            pltpu.SemaphoreType.DMA(()),
+            pltpu.SemaphoreType.DMA(()),
+            pltpu.SemaphoreType.DMA((ups,)),
+            pltpu.SemaphoreType.DMA((ups,)),
+            pltpu.SemaphoreType.DMA((downs,)),
+            pltpu.SemaphoreType.DMA((downs,)),
+        ],
+        compiler_params=pltpu.CompilerParams(collective_id=collective_id, has_side_effects=True),
+    )(x)
+    return out.reshape(size // 2 * x.shape[0], x.shape[1])
+
+
 def dft_table(double_len):
     step = 32
     hi_ids = jnp.arange(double_len // step, dtype=jnp.int32)[:, None]
@@ -227,7 +313,9 @@
 
     with jax.named_scope("out_weight_columns"):
         w_late, inputs_t = lax.optimization_barrier((w_out, inputs_t))
-        w_cols = lax.all_to_all(w_late, "chan", 1, 0, tiled=True)
+        size = lax.axis_size("chan")
+        same_core = [list(range(c, size, 2)) for c in range(2)]
+        w_cols = lax.all_to_all(w_late, "chan", 1, 0, tiled=True, axis_index_groups=same_core)
 
     with jax.named_scope("input_projection"):
         w_flat = w_in.reshape(w_in.shape[0], 3 * width_dev)
@@ -300,10 +388,15 @@
         gated_out = gated_out.reshape(width_dev, span_len)
 
     with jax.named_scope("output_projection"):
-        gathered = chan_gather(gated_out, None, 1)
-        result = lax.dot_general(
+        gathered = half_gather(gated_out, 1)
+        partial = lax.dot_general(
             gathered, w_cols, (((0,), (0,)), ((), ())), preferred_element_type=jnp.float32
-        ).astype(jnp.bfloat16)
+        )
+        core = lax.axis_index("chan") % 2
+        mine = lax.dynamic_slice_in_dim(partial, core * width_dev, width_dev, axis=1)
+        other = lax.dynamic_slice_in_dim(partial, (1 - core) * width_dev, width_dev, axis=1)
+        pairs = [(h, h + 1 - 2 * (h % 2)) for h in range(lax.axis_size("chan"))]
+        result = (mine + lax.ppermute(other, "chan", pairs)).astype(jnp.bfloat16)
     return result
 
 

time: 171 us -> 164 us (0.959)
  Pallas kernels: 129 us -> 117 us
  starting transfers between devices: 4.29 us -> 8.04 us
    pallas_call x2 -> x1, Pallas kernels: 106 us -> 56.7 us  [chan_gather(): pl.pallas_call(functools.partial(gather_kernel, chips, groups), out_shape...]
    pallas_call x0 -> x1, Pallas kernels: none -> 33 us  [half_gather(): pl.pallas_call(functools.partial(half_gather_kernel, chips), out_shape=ja...]
    ppermute x0 -> x1, starting transfers between devices: none -> 4.23 us  [body(): result = (mine + lax.ppermute(other, 'chan', pairs)).astype(jnp.bfloat16)]
    pallas_call x2, Pallas kernels: 23.2 us -> 27.3 us  [ctx_exchange(): pl.pallas_call(functools.partial(exchange_kernel, groups), out_shape=jax....]
    dot_general x1, matrix products: 4.14 us -> 2.33 us  [body(): lax.dot_general(gathered, w_cols, (((0,), (0,)), ((), ())), preferred_ele...]
  transfers between devices with their start and end apart: 1 -> 2, of which waited for: 0 -> 1; matrix products, arithmetic and copies ran while one was open for 11% -> 12% of each run, Pallas kernels for 7% -> 10%
where the time goes in v6:
time: 164 us; the launch traced here: 162 us
  Pallas kernels  117 us (71%)
  local copies, waits for them, and re-layouts  15.1 us (9%)
  matrix products  12.4 us (8%)
  other arithmetic  8.16 us (5%)
  starting transfers between devices  8.04 us (5%)
    pallas_call x1, Pallas kernels, chan_gather(): pl.pallas_call(functools.partial(gather_kernel, chips, groups), out_shape...  56.7 us
    pallas_call x1, Pallas kernels, half_gather(): pl.pallas_call(functools.partial(half_gather_kernel, chips), out_shape=ja...  33 us
    pallas_call x2, Pallas kernels, ctx_exchange(): pl.pallas_call(functools.partial(exchange_kernel, groups), out_shape=jax....  27.3 us
    unnamed x19, local copies, waits for them, and re-layouts  8.6 us
    dot_general x1, matrix products, body(): lax.dot_general(w_flat, inputs_t, (((0,), (0,)), ((), ())), preferred_ele...  4.95 us
    ppermute x1, starting transfers between devices, body(): result = (mine + lax.ppermute(other, 'chan', pairs)).astype(jnp.bfloat16)  4.23 us
    all_to_all x1, starting transfers between devices, body(): lax.all_to_all(w_late, 'chan', 1, 0, tiled=True, axis_index_groups=same_c...  3.81 us
  transfers between devices with their start and end apart: 2, of which 1 were waited for; matrix products, arithmetic and copies ran while one was open for 12% of the time, Pallas kernels for 10%

profile of v6, /device:TPU:1, one launch (start us, length us, event | category | flops | bytes accessed | tf_op | source)
XLA Modules:
  0.0 162.3 jit_solution(11486312539333483931)
XLA Ops:
  0.0 1.7 %copy.19 = bf16[512,128]{0,1:T(8,128)(2,1)} copy(bf16[512,128]{1,0:T(8,128)(2,1)} %param.6) | data formatting | bytes 262144 | tf_op args[0]
  1.7 1.7 %copy.20 = bf16[128,512]{1,0:T(8,128)(2,1)} copy(bf16[128,512]{0,1:T(8,128)(2,1)} %bitcast.135) | data formatting | bytes 262144 | tf_op jit(solution)/shard_map/input_gather_and_filter_to_owner/transpose | solution.py:311
  3.3 56.7 %input_gather_and_filter_to_owner.1 = (bf16[32,128,512]{2,1,0:T(8,128)(2,1)}, bf16[8,16,512]{2,1,0:T(8,128)(2,1)}) custom-call(bf16[128,512]{1,0:T(8,128)(2,1)} %bitcast.132, bf16[8,16,512]{2,1,0:T(8,128)(2,1)} %bitcast.133), custom_call_target="tpu_custom_call" | custom-call | tf_op jit(solution)/shard_map/input_gather_and_filter_to_owner/pallas_call | solution.py:190
  60.0 2.3 %copy.26 = bf16[128,4096]{0,1:T(8,128)(2,1)} copy(bf16[128,4096]{1,0:T(8,128)(2,1)} %param.11) | data formatting | bytes 2097152 | tf_op jit(solution)/shard_map/out_weight_columns/optimization_barrier | solution.py:315
  62.4 3.8 %all-to-all-start = ((bf16[128,16,256]{0,2,1:T(8,128)(2,1)}), bf16[128,16,256]{0,2,1:T(8,128)(2,1)S(1)}, u32[]{:S(2)}, u32[]{:S(2)}) async-start(bf16[128,16,256]{0,2,1:T(8,128)(2,1)} %bitcast.15), calls=%async_computation | async-start | bytes 2097152 | tf_op jit(solution)/shard_map/out_weight_columns/all_to_all | solution.py:318
  66.2 0.5 fusion.45
  66.7 4.8 %copy.21 = bf16[4096,3,128]{0,2,1:T(8,128)(2,1)} copy(bf16[4096,3,128]{2,0,1:T(8,128)(2,1)} %param.7) | data formatting | bytes 6291456 | tf_op args[1]
  71.5 0.0 copy-start.5
  71.5 0.0 copy-start.7
  71.5 0.0 copy-start.6
  71.5 5.0 %convolution_convert_fusion.1 = bf16[512,384]{0,1:T(8,128)(2,1)S(1)} fusion(bf16[4096,384]{0,1:T(8,128)(2,1)} %bitcast.123, bf16[4096,512]{1,0:T(8,128)(2,1)} %bitcast.136), kind=kOutput, calls=%fused_computation.11 | convolution fusion | flops 1610809344 | bytes 7733248 | tf_op jit(solution)/shard_map/input_projection/dot_general | solution.py:322
  76.5 0.8 copy.32
  77.2 16.0 %projection_to_owner.1 = bf16[8,3,16,512]{3,2,1,0:T(8,128)(2,1)} custom-call(bf16[8,3,16,512]{3,2,1,0:T(8,128)(2,1)} %bitcast.130), custom_call_target="tpu_custom_call" | custom-call | tf_op jit(solution)/shard_map/projection_to_owner/pallas_call | solution.py:153
  93.3 1.0 slice.141
  94.3 0.0 copy-done.5
  94.3 0.1 slice.101
  94.4 0.0 copy-done.7
  94.4 0.1 dynamic_slice.13
  94.5 0.0 copy-done.6
  94.5 0.1 fusion.68
  94.6 1.2 fusion.13
  95.8 1.4 add_convert_fusion
  97.2 0.7 fusion.28
  97.9 0.6 fusion.48
  98.5 1.5 negate_convert_fusion
  100.0 0.0 copy-start
  100.0 0.0 copy-start.2
  100.0 1.5 fusion.3
  101.5 0.0 copy-done
  101.5 0.4 copy-done.2
  101.9 0.1 slice_convert_fusion.3
  102.0 0.0 all-to-all-done
  102.0 0.5 copy.27
  102.6 2.4 %convolution_convert_fusion = bf16[8,16,2048]{2,1,0:T(8,128)(2,1)S(1)} fusion(bf16[8,16,512]{2,1,0:T(8,128)(2,1)} %fusion.28, bf16[1024,1024]{1,0:T(8,128)(2,1)} %bitcast.128, bf16[1024,1024]{1,0:T(8,128)(2,1)} %bitcast.125), kind=kOutput, calls=%fused_computation.8 | convolution fusion | flops 272891904 | bytes 4849664 | tf_op jit(solution)/shard_map/spectra/jdb,fb->jdf/dot_general | solution.py:351
  105.0 0.1 slice_convert_fusion.2
  105.1 0.2 fusion.63
  105.3 0.2 fusion.64
  105.5 0.1 fusion.61
  105.6 0.1 fusion.62
  105.8 0.1 fusion.59
  105.9 0.1 fusion.60
  106.0 0.1 fusion.57
  106.1 0.0 copy-start.1
  106.1 0.0 copy-start.3
  106.1 0.0 copy-start.4
  106.1 0.1 fusion.58
  106.2 0.1 fusion.55
  106.3 0.1 fusion.56
  106.4 0.1 fusion.54
  106.4 0.1 fusion.53
  106.6 1.1 copy-done.1
  107.7 0.6 copy-done.3
  108.3 0.0 copy-done.4
  108.3 1.1 fusion.10.x_ref
  109.5 11.3 %gated_back_to_rows.1 = bf16[8,16,512]{2,1,0:T(8,128)(2,1)} custom-call(bf16[8,16,512]{2,1,0:T(8,128)(2,1)} %fusion.10.x_ref), custom_call_target="tpu_custom_call" | custom-call | tf_op jit(solution)/shard_map/gated_back_to_rows/pallas_call | solution.py:153
  120.8 33.0 %output_projection.1 = bf16[16,128,512]{2,1,0:T(8,128)(2,1)} custom-call(bf16[128,512]{1,0:T(8,128)(2,1)} %bitcast.131), custom_call_target="tpu_custom_call" | custom-call | tf_op jit(solution)/shard_map/output_projection/pallas_call | solution.py:269
  153.8 2.3 %fusion.76 = f32[512,256]{1,0:T(8,128)S(1)} fusion(bf16[2048,512]{1,0:T(8,128)(2,1)} %bitcast.120, bf16[2048,256]{1,0:T(8,128)(2,1)S(1)} %bitcast.121), kind=kOutput, calls=%fused_computation.124 | convolution fusion | flops 536870912 | bytes 3670016 | tf_op jit(solution)/shard_map/output_projection/dot_general | solution.py:392
  156.2 4.2 %collective-permute-start = (f32[512,128]{1,0:T(8,128)S(1)}, f32[512,128]{1,0:T(8,128)S(1)}, u32[]{:S(2)}, u32[]{:S(2)}) collective-permute-start(f32[512,128]{1,0:T(8,128)S(1)} %constant_dynamic-slice_fusion.2), channel_id=1, source_target_pairs={{0,1},{1,0},{2,3},{3,2},{4,5},{5,4},{6,7},{7,6},{8,9},{9,8},{10,11... | collective-permute-start | bytes 786440 | tf_op jit(solution)/shard_map/output_projection/ppermute | solution.py:399
  160.4 1.2 collective-permute-done
  161.6 0.7 add_convert_fusion.1
  (13 shorter events, 0.1 us)
Async XLA Ops:
  62.4 39.7 %all-to-all-start = ((bf16[128,16,256]{0,2,1:T(8,128)(2,1)}), bf16[128,16,256]{0,2,1:T(8,128)(2,1)S(1)}, u32[]{:S(2)}, u32[]{:S(2)}) async-start(bf16[128,16,256]{0,2,1:T(8,128)(2,1)} %bitcast.15), calls=%async_computation | async-start | bytes 2097152 | tf_op jit(solution)/shard_map/out_weight_columns/all_to_all | solution.py:318
  71.5 22.8 %copy-start.5 = (bf16[8,16,512]{2,1,0:T(8,128)(2,1)S(1)}, bf16[8,16,512]{2,1,0:T(8,128)(2,1)}, u32[]{:S(2)}) copy-start(bf16[8,16,512]{2,1,0:T(8,128)(2,1)} %get-tuple-element.13) | copy-start | bytes 393220
  71.5 22.9 %copy-start.7 = (f32[128]{0:T(128)S(1)}, f32[128]{0:T(128)}, u32[]{:S(2)}) copy-start(f32[128]{0:T(128)} %param.9) | copy-start | bytes 1540
  71.5 23.0 %copy-start.6 = (bf16[3,3,128]{2,1,0:T(4,128)(2,1)S(1)}, bf16[3,3,128]{2,1,0:T(4,128)(2,1)}, u32[]{:S(2)}) copy-start(bf16[3,3,128]{2,1,0:T(4,128)(2,1)} %param.8) | copy-start | bytes 6916
  100.0 1.5 copy-start
  100.0 2.0 %copy-start.2 = (bf16[32,32,1024]{2,1,0:T(8,128)(2,1)}, bf16[32,32,1024]{2,1,0:T(8,128)(2,1)S(1)}, u32[]{:S(2)}) copy-start(bf16[32,32,1024]{2,1,0:T(8,128)(2,1)S(1)} %get-tuple-element.28) | copy-start | bytes 6291460
  106.1 1.6 copy-start.1
  106.1 2.2 %copy-start.3 = (bf16[32,32,1024]{2,1,0:T(8,128)(2,1)S(1)}, bf16[32,32,1024]{2,1,0:T(8,128)(2,1)}, u32[]{:S(2)}) copy-start(bf16[32,32,1024]{2,1,0:T(8,128)(2,1)} %copy-done.2) | copy-start | bytes 6291460
  106.1 2.2 %copy-start.4 = (bf16[8,16,512]{2,1,0:T(8,128)(2,1)S(1)}, bf16[8,16,512]{2,1,0:T(8,128)(2,1)}, u32[]{:S(2)}) copy-start(bf16[8,16,512]{2,1,0:T(8,128)(2,1)} %fusion.28) | copy-start | bytes 393220
  156.2 5.4 %collective-permute-start = (f32[512,128]{1,0:T(8,128)S(1)}, f32[512,128]{1,0:T(8,128)S(1)}, u32[]{:S(2)}, u32[]{:S(2)}) collective-permute-start(f32[512,128]{1,0:T(8,128)S(1)} %constant_dynamic-slice_fusion.2), channel_id=1, source_target_pairs={{0,1},{1,0},{2,3},{3,2},{4,5},{5,4},{6,7},{7,6},{8,9},{9,8},{10,11... | collective-permute-start | bytes 786440 | tf_op jit(solution)/shard_map/output_projection/ppermute | solution.py:399

commit v7 on v6

--- a/solution.py
+++ b/solution.py
@@ -311,12 +311,6 @@
         taps_t = filter_taps.T.reshape(groups, own, span_len)
         inputs_t, taps_t = chan_gather(inputs.T, taps_t, 0)
 
-    with jax.named_scope("out_weight_columns"):
-        w_late, inputs_t = lax.optimization_barrier((w_out, inputs_t))
-        size = lax.axis_size("chan")
-        same_core = [list(range(c, size, 2)) for c in range(2)]
-        w_cols = lax.all_to_all(w_late, "chan", 1, 0, tiled=True, axis_index_groups=same_core)
-
     with jax.named_scope("input_projection"):
         w_flat = w_in.reshape(w_in.shape[0], 3 * width_dev)
         proj_t = lax.dot_general(
@@ -326,6 +320,12 @@
     with jax.named_scope("projection_to_owner"):
         proj_t = proj_t.reshape(3, groups, own, span_len).transpose(1, 0, 2, 3)
         proj_t = ctx_exchange(proj_t, 3)
+
+    with jax.named_scope("out_weight_columns"):
+        w_late, proj_t = lax.optimization_barrier((w_out, proj_t))
+        size = lax.axis_size("chan")
+        same_core = [list(range(c, size, 2)) for c in range(2)]
+        w_cols = lax.all_to_all(w_late, "chan", 1, 0, tiled=True, axis_index_groups=same_core)
 
     with jax.named_scope("short_conv"):
         start = position * own
@@ -345,7 +345,6 @@
         )
 
     with jax.named_scope("spectra"):
-        w_cols, gated_in = lax.optimization_barrier((w_cols, gated_in))
         table = dft_table(double_len)
         forward_in = table[:, :span_len]
         spectra_in = jnp.einsum(
@@ -384,6 +383,7 @@
         gated_out = (gate_out.astype(jnp.float32) * long_out).astype(jnp.bfloat16)
 
     with jax.named_scope("gated_back_to_rows"):
+        w_cols, gated_out = lax.optimization_barrier((w_cols, gated_out))
         gated_out = ctx_exchange(gated_out, 4)
         gated_out = gated_out.reshape(width_dev, span_len)
 

time: 164 us -> 165 us (level)
  waiting for transfers between devices: 1.16 us -> 7.32 us
  Pallas kernels: 117 us -> 112 us
  other arithmetic: 8.16 us -> 12.5 us
  local copies, waits for them, and re-layouts: 15.1 us -> 11.8 us
    pallas_call x2, Pallas kernels: 27.3 us -> 20.3 us  [ctx_exchange(): pl.pallas_call(functools.partial(exchange_kernel, groups), out_shape=jax....]
    all_to_all x1, waiting for transfers between devices: 0.01 us -> 6.16 us  [body(): lax.all_to_all(w_late, 'chan', 1, 0, tiled=True, axis_index_groups=same_c...]
    unnamed x7, other arithmetic: 0.05 us -> 5.21 us
    unnamed x19 -> x18, local copies, waits for them, and re-layouts: 8.6 us -> 6.24 us
  transfers between devices with their start and end apart: 2 -> 2, of which waited for: 1 -> 2; matrix products, arithmetic and copies ran while one was open for 12% -> 10% of each run, Pallas kernels for 10% -> 0%
where the time goes in v7:
time: 165 us; the launch traced here: 163 us
  Pallas kernels  112 us (68%)
  other arithmetic  12.5 us (8%)
  local copies, waits for them, and re-layouts  11.8 us (7%)
  matrix products  10.8 us (7%)
  starting transfers between devices  8.61 us (5%)
  waiting for transfers between devices  7.32 us (4%)
    pallas_call x1, Pallas kernels, chan_gather(): pl.pallas_call(functools.partial(gather_kernel, chips, groups), out_shape...  56.9 us
    pallas_call x1, Pallas kernels, half_gather(): pl.pallas_call(functools.partial(half_gather_kernel, chips), out_shape=ja...  34.4 us
    pallas_call x2, Pallas kernels, ctx_exchange(): pl.pallas_call(functools.partial(exchange_kernel, groups), out_shape=jax....  20.3 us
    unnamed x18, local copies, waits for them, and re-layouts  6.24 us
    all_to_all x1, waiting for transfers between devices, body(): lax.all_to_all(w_late, 'chan', 1, 0, tiled=True, axis_index_groups=same_c...  6.16 us
    unnamed x7, other arithmetic  5.21 us
    ppermute x1, starting transfers between devices, body(): result = (mine + lax.ppermute(other, 'chan', pairs)).astype(jnp.bfloat16)  4.79 us
    dot_general x1, matrix products, body(): lax.dot_general(w_flat, inputs_t, (((0,), (0,)), ((), ())), preferred_ele...  3.97 us
  transfers between devices with their start and end apart: 2, of which 2 were waited for; matrix products, arithmetic and copies ran while one was open for 10% of the time, Pallas kernels for 0%

profile of v7, /device:TPU:1, one launch (start us, length us, event | category | flops | bytes accessed | tf_op | source)
XLA Modules:
  0.0 163.0 jit_solution(13121867865706454046)
XLA Ops:
  0.0 1.7 %copy.19 = bf16[512,128]{0,1:T(8,128)(2,1)} copy(bf16[512,128]{1,0:T(8,128)(2,1)} %param.6) | data formatting | bytes 262144 | tf_op args[0]
  1.7 1.7 %copy.20 = bf16[128,512]{1,0:T(8,128)(2,1)} copy(bf16[128,512]{0,1:T(8,128)(2,1)} %bitcast.137) | data formatting | bytes 262144 | tf_op jit(solution)/shard_map/input_gather_and_filter_to_owner/transpose | solution.py:311
  3.3 3.2 %copy.21 = bf16[4096,3,128]{0,2,1:T(8,128)(2,1)S(1)} copy(bf16[4096,3,128]{2,0,1:T(8,128)(2,1)} %param.7) | data formatting | bytes 6291456 | tf_op args[1]
  6.5 56.9 %input_gather_and_filter_to_owner.1 = (bf16[32,128,512]{2,1,0:T(8,128)(2,1)}, bf16[8,16,512]{2,1,0:T(8,128)(2,1)}) custom-call(bf16[128,512]{1,0:T(8,128)(2,1)} %bitcast.134, bf16[8,16,512]{2,1,0:T(8,128)(2,1)} %bitcast.135), custom_call_target="tpu_custom_call" | custom-call | tf_op jit(solution)/shard_map/input_gather_and_filter_to_owner/pallas_call | solution.py:190
  63.4 4.0 %convolution_convert_fusion.1 = bf16[512,384]{0,1:T(8,128)(2,1)S(1)} fusion(bf16[4096,384]{0,1:T(8,128)(2,1)S(1)} %bitcast.125, bf16[4096,512]{1,0:T(8,128)(2,1)} %bitcast.138), kind=kOutput, calls=%fused_computation.11 | convolution fusion | flops 1610809344 | bytes 7733248 | tf_op jit(solution)/shard_map/input_projection/dot_general | solution.py:316
  67.4 0.8 copy.32
  68.2 10.8 %projection_to_owner.1 = bf16[8,3,16,512]{3,2,1,0:T(8,128)(2,1)} custom-call(bf16[8,3,16,512]{3,2,1,0:T(8,128)(2,1)} %bitcast.132), custom_call_target="tpu_custom_call" | custom-call | tf_op jit(solution)/shard_map/projection_to_owner/pallas_call | solution.py:153
  79.0 0.0 copy-start
  79.0 0.0 copy-start.6
  79.0 2.3 %copy.23 = bf16[128,4096]{0,1:T(8,128)(2,1)} copy(bf16[128,4096]{1,0:T(8,128)(2,1)} %param.11) | data formatting | bytes 2097152 | tf_op jit(solution)/shard_map/out_weight_columns/optimization_barrier | solution.py:325
  81.3 3.8 %all-to-all-start = ((bf16[128,16,256]{0,2,1:T(8,128)(2,1)}), bf16[128,16,256]{0,2,1:T(8,128)(2,1)S(1)}, u32[]{:S(2)}, u32[]{:S(2)}) async-start(bf16[128,16,256]{0,2,1:T(8,128)(2,1)} %bitcast.8), calls=%async_computation | async-start | bytes 2097152 | tf_op jit(solution)/shard_map/out_weight_columns/all_to_all | solution.py:328
  85.2 0.5 fusion.45
  85.7 0.0 copy-done
  85.8 0.1 slice.141
  85.9 0.2 fusion.13
  86.1 0.6 fusion.48
  86.7 0.0 copy-done.6
  86.7 0.1 fusion.69
  86.8 0.4 add_convert_fusion
  87.2 1.5 negate_convert_fusion
  88.7 0.0 copy-start.1
  88.7 0.0 copy-start.3
  88.7 0.0 copy-start.5
  88.7 0.8 convolution_convert_fusion
  89.5 0.1 slice_convert_fusion.2
  89.6 0.1 copy-done.5
  89.7 0.1 slice.101
  89.9 0.1 copy-done.1
  90.0 0.7 copy-done.3
  90.6 1.5 fusion.3
  92.1 0.1 slice_convert_fusion.3
  92.2 0.7 fusion.59
  93.0 0.7 fusion.60
  93.7 0.1 fusion.57
  93.7 0.0 copy-start.7
  93.8 0.1 fusion.58
  93.8 0.1 fusion.55
  93.9 0.1 fusion.56
  94.0 0.1 fusion.54
  94.1 0.1 fusion.53
  94.1 0.7 fusion.37
  94.8 0.6 fusion.38
  95.4 0.6 fusion.39
  96.0 0.6 fusion.40
  96.7 0.6 fusion.41
  97.3 0.0 copy-done.7
  97.3 0.1 dynamic_slice.13
  97.4 1.4 fusion.42
  98.8 0.1 fusion.61
  99.0 0.1 fusion.62
  99.1 0.6 fusion.43
  99.7 0.2 fusion.63
  99.9 0.2 fusion.64
  100.1 0.6 fusion.44
  100.7 0.5 copy-done.4
  101.2 2.2 %fusion.10.x_ref = bf16[8,16,512]{2,1,0:T(8,128)(2,1)} fusion(bf16[8,16,2048]{2,1,0:T(8,128)(2,1)} %fusion.44, bf16[1024,1024]{1,0:T(8,128)(2,1)S(1)} %bitcast.131, bf16[1024,1024]{1,0:T(8,128)(2,1)S(1)} %bitcast.128, bf16[8,3,16,512]{3,2,0,1:T(8,128)(2,1)S(1)} %add_convert_fusion, f32[16]{0:T(128)S(1)} %dynamic_slice.13), kind=kOutput, calls=%fused_computation.15 | convolution fusion | flops 273350656 | bytes 5242944 | tf_op jit(solution)/shard_map/inverse_and_gate/idf,fa->ida/dot_general | solution.py:378
  103.4 6.2 %all-to-all-done = bf16[128,16,256]{0,2,1:T(8,128)(2,1)S(1)} async-done(((bf16[128,16,256]{0,2,1:T(8,128)(2,1)}), bf16[128,16,256]{0,2,1:T(8,128)(2,1)S(1)}, u32[]{:S(2)}, u32[]{:S(2)}) %all-to-all-start) | async-done | bytes 1048608 | tf_op jit(solution)/shard_map/out_weight_columns/all_to_all | solution.py:328
  109.6 0.5 copy.24
  110.1 9.5 %gated_back_to_rows.1 = bf16[8,16,512]{2,1,0:T(8,128)(2,1)} custom-call(bf16[8,16,512]{2,1,0:T(8,128)(2,1)} %fusion.10.x_ref), custom_call_target="tpu_custom_call" | custom-call | tf_op jit(solution)/shard_map/gated_back_to_rows/pallas_call | solution.py:153
  119.6 34.4 %output_projection.1 = bf16[16,128,512]{2,1,0:T(8,128)(2,1)} custom-call(bf16[128,512]{1,0:T(8,128)(2,1)} %bitcast.133), custom_call_target="tpu_custom_call" | custom-call | tf_op jit(solution)/shard_map/output_projection/pallas_call | solution.py:269
  154.0 2.3 %fusion.77 = f32[512,256]{1,0:T(8,128)S(1)} fusion(bf16[2048,512]{1,0:T(8,128)(2,1)} %bitcast.122, bf16[2048,256]{1,0:T(8,128)(2,1)S(1)} %bitcast.123), kind=kOutput, calls=%fused_computation.124 | convolution fusion | flops 536870912 | bytes 3670016 | tf_op jit(solution)/shard_map/output_projection/dot_general | solution.py:392
  156.4 4.8 %collective-permute-start = (f32[512,128]{1,0:T(8,128)S(1)}, f32[512,128]{1,0:T(8,128)S(1)}, u32[]{:S(2)}, u32[]{:S(2)}) collective-permute-start(f32[512,128]{1,0:T(8,128)S(1)} %constant_dynamic-slice_fusion.2), channel_id=1, source_target_pairs={{0,1},{1,0},{2,3},{3,2},{4,5},{5,4},{6,7},{7,6},{8,9},{9,8},{10,11... | collective-permute-start | bytes 786440 | tf_op jit(solution)/shard_map/output_projection/ppermute | solution.py:399
  161.2 1.2 collective-permute-done
  162.3 0.7 add_convert_fusion.1
  (8 shorter events, 0.1 us)
Async XLA Ops:
  79.0 6.7 %copy-start = (bf16[8,3,16,512]{3,2,1,0:T(8,128)(2,1)S(1)}, bf16[8,3,16,512]{3,2,1,0:T(8,128)(2,1)}, u32[]{:S(2)}) copy-start(bf16[8,3,16,512]{3,2,1,0:T(8,128)(2,1)} %projection_to_owner.1) | copy-start | bytes 1179652
  79.0 7.7 %copy-start.6 = (bf16[3,3,128]{2,1,0:T(4,128)(2,1)S(1)}, bf16[3,3,128]{2,1,0:T(4,128)(2,1)}, u32[]{:S(2)}) copy-start(bf16[3,3,128]{2,1,0:T(4,128)(2,1)} %param.8) | copy-start | bytes 6916
  81.3 28.2 %all-to-all-start = ((bf16[128,16,256]{0,2,1:T(8,128)(2,1)}), bf16[128,16,256]{0,2,1:T(8,128)(2,1)S(1)}, u32[]{:S(2)}, u32[]{:S(2)}) async-start(bf16[128,16,256]{0,2,1:T(8,128)(2,1)} %bitcast.8), calls=%async_computation | async-start | bytes 2097152 | tf_op jit(solution)/shard_map/out_weight_columns/all_to_all | solution.py:328
  88.7 1.3 copy-start.1
  88.7 2.0 %copy-start.3 = (bf16[32,32,1024]{2,1,0:T(8,128)(2,1)}, bf16[32,32,1024]{2,1,0:T(8,128)(2,1)S(1)}, u32[]{:S(2)}) copy-start(bf16[32,32,1024]{2,1,0:T(8,128)(2,1)S(1)} %get-tuple-element.28) | copy-start | bytes 6291460
  88.7 1.1 copy-start.5
  93.7 3.6 %copy-start.7 = (f32[128]{0:T(128)S(1)}, f32[128]{0:T(128)}, u32[]{:S(2)}) copy-start(f32[128]{0:T(128)} %param.9) | copy-start | bytes 1540
  98.9 1.8 %copy-start.2 = (bf16[32,32,1024]{2,1,0:T(8,128)(2,1)S(1)}, bf16[32,32,1024]{2,1,0:T(8,128)(2,1)}, u32[]{:S(2)}) copy-start(bf16[32,32,1024]{2,1,0:T(8,128)(2,1)} %copy-done.1) | copy-start | bytes 6291460
  98.9 2.3 %copy-start.4 = (bf16[32,32,1024]{2,1,0:T(8,128)(2,1)S(1)}, bf16[32,32,1024]{2,1,0:T(8,128)(2,1)}, u32[]{:S(2)}) copy-start(bf16[32,32,1024]{2,1,0:T(8,128)(2,1)} %copy-done.3) | copy-start | bytes 6291460
  156.4 6.0 %collective-permute-start = (f32[512,128]{1,0:T(8,128)S(1)}, f32[512,128]{1,0:T(8,128)S(1)}, u32[]{:S(2)}, u32[]{:S(2)}) collective-permute-start(f32[512,128]{1,0:T(8,128)S(1)} %constant_dynamic-slice_fusion.2), channel_id=1, source_target_pairs={{0,1},{1,0},{2,3},{3,2},{4,5},{5,4},{6,7},{7,6},{8,9},{9,8},{10,11... | collective-permute-start | bytes 786440 | tf_op jit(solution)/shard_map/output_projection/ppermute | solution.py:399

commit v8 on v6

--- a/solution.py
+++ b/solution.py
@@ -63,46 +63,38 @@
         cross(k, peer, me).wait_send()
         cross(k, peer, peer).wait_recv()
 
-    def group(chip):
-        return out_ref.at[pl.ds(pl.multiple_of(chip * PER_Z, PER_Z), PER_Z)]
+    last = chips // 2 - 1
+
+    def part(chip, s, half):
+        if s < last:
+            return out_ref.at[pl.ds(pl.multiple_of(chip * PER_Z, PER_Z), PER_Z)]
+        start = pl.multiple_of(chip * PER_Z + half * (PER_Z // 2), PER_Z // 2)
+        return out_ref.at[pl.ds(start, PER_Z // 2)]
 
     def ring(s, chip):
         return pltpu.make_async_remote_copy(
-            src_ref=group(chip), dst_ref=group(chip), send_sem=ring_send.at[s],
+            src_ref=part(chip, s, core), dst_ref=part(chip, s, core), send_sem=ring_send.at[s],
             recv_sem=ring_recv.at[s], device_id=(row, after), device_id_type=MESH)
 
-    def sib(s, chip):
-        return pltpu.make_async_remote_copy(
-            src_ref=group(chip), dst_ref=group(chip), send_sem=sib_send.at[s],
+    def sib(s, chip, half):
+        return pltpu.make_async_remote_copy(
+            src_ref=part(chip, s, half), dst_ref=part(chip, s, half), send_sem=sib_send.at[s],
             recv_sem=sib_recv.at[s], device_id=(row, sibling), device_id_type=MESH)
 
-    longest = chips // 2
-    for s in range(longest):
-        active = jnp.logical_or(core == 0, s < chips - 1 - longest)
+    for s in range(last + 1):
         sent = (z - way * s + chips) % chips
         got = (z - way * (s + 1) + chips) % chips
-
-        @pl.when(active)
-        def _():
-            ring(s, sent).start()
-            ring(s, got).wait_recv()
-            sib(s, got).start()
-
-    for s in range(longest):
-        active = jnp.logical_or(core == 0, s < chips - 1 - longest)
+        ring(s, sent).start()
+        ring(s, got).wait_recv()
+        sib(s, got, core).start()
+
+    for s in range(last + 1):
         sent = (z - way * s + chips) % chips
         got = (z - way * (s + 1) + chips) % chips
-        other = jnp.logical_or(core == 1, s < chips - 1 - longest)
         theirs = (z + way * (s + 1) + chips) % chips
-
-        @pl.when(active)
-        def _():
-            ring(s, sent).wait_send()
-            sib(s, got).wait_send()
-
-        @pl.when(other)
-        def _():
-            sib(s, theirs).wait_recv()
+        ring(s, sent).wait_send()
+        sib(s, got, core).wait_send()
+        sib(s, theirs, 1 - core).wait_recv()
 
     if groups:
         t_local.wait()
@@ -169,6 +161,7 @@
     groups = lax.axis_size("ctx") if t is not None else 0
     chips = size // PER_Z
     longest = chips // 2
+    assert chips % 2 == 0
     operands = (x,) if t is None else (x, t)
     out_shape = [jax.ShapeDtypeStruct((size,) + x.shape, x.dtype)]
     scratch = [
@@ -233,39 +226,42 @@
     def pair(chip):
         return out_ref.at[pl.ds(pl.multiple_of(chip * 2, 2), 2)]
 
+    steps = chips // 2
+
+    def piece(chip, s, half):
+        if s < steps - 1:
+            return pair(chip)
+        return out_ref.at[pl.ds(chip * 2 + half, 1)]
+
     def up(s, chip):
         return pltpu.make_async_remote_copy(
-            src_ref=pair(chip), dst_ref=pair(chip), send_sem=up_send.at[s],
+            src_ref=piece(chip, s, 0), dst_ref=piece(chip, s, 0), send_sem=up_send.at[s],
             recv_sem=up_recv.at[s], device_id=(row, ahead), device_id_type=MESH)
 
     def down(s, chip):
         return pltpu.make_async_remote_copy(
-            src_ref=pair(chip), dst_ref=pair(chip), send_sem=down_send.at[s],
+            src_ref=piece(chip, s, 1), dst_ref=piece(chip, s, 1), send_sem=down_send.at[s],
             recv_sem=down_recv.at[s], device_id=(row, behind), device_id_type=MESH)
 
-    ups = chips // 2
-    downs = chips - 1 - ups
-    for s in range(ups):
+    for s in range(steps):
         if s > 0:
             up(s - 1, (z - s + chips) % chips).wait_recv()
         up(s, (z - s + chips) % chips).start()
-        if s < downs:
-            if s > 0:
-                down(s - 1, (z + s) % chips).wait_recv()
-            down(s, (z + s) % chips).start()
-    up(ups - 1, (z - ups + chips) % chips).wait_recv()
-    down(downs - 1, (z + downs) % chips).wait_recv()
-    for s in range(ups):
+        if s > 0:
+            down(s - 1, (z + s) % chips).wait_recv()
+        down(s, (z + s) % chips).start()
+    up(steps - 1, (z - steps + chips) % chips).wait_recv()
+    down(steps - 1, (z + steps) % chips).wait_recv()
+    for s in range(steps):
         up(s, (z - s + chips) % chips).wait_send()
-    for s in range(downs):
         down(s, (z + s) % chips).wait_send()
 
 
 def half_gather(x, collective_id):
     size = lax.axis_size("chan")
     chips = size // PER_Z
-    ups = chips // 2
-    downs = chips - 1 - ups
+    assert chips % 2 == 0
+    ups = downs = chips // 2
     out = pl.pallas_call(
         functools.partial(half_gather_kernel, chips),
         out_shape=jax.ShapeDtypeStruct((size // 2,) + x.shape, x.dtype),
@@ -345,7 +341,6 @@
         )
 
     with jax.named_scope("spectra"):
-        w_cols, gated_in = lax.optimization_barrier((w_cols, gated_in))
         table = dft_table(double_len)
         forward_in = table[:, :span_len]
         spectra_in = jnp.einsum(
@@ -385,6 +380,7 @@
 
     with jax.named_scope("gated_back_to_rows"):
         gated_out = ctx_exchange(gated_out, 4)
+        w_cols, gated_out = lax.optimization_barrier((w_cols, gated_out))
         gated_out = gated_out.reshape(width_dev, span_len)
 
     with jax.named_scope("output_projection"):

time: 164 us -> 164 us (level)
  other arithmetic: 8.16 us -> 14.4 us
  Pallas kernels: 117 us -> 113 us
    unnamed x7, other arithmetic: 0.05 us -> 5.13 us
    pallas_call x1, Pallas kernels: 56.7 us -> 53.5 us  [chan_gather(): pl.pallas_call(functools.partial(gather_kernel, chips, groups), out_shape...]
    unnamed x19 -> x17, local copies, waits for them, and re-layouts: 8.6 us -> 7.81 us
  transfers between devices with their start and end apart: 2 -> 2, of which waited for: 1 -> 1; matrix products, arithmetic and copies ran while one was open for 12% -> 18% of each run, Pallas kernels for 10% -> 17%
where the time goes in v8:
time: 164 us; the launch traced here: 163 us
  Pallas kernels  113 us (69%)
  other arithmetic  14.4 us (9%)
  local copies, waits for them, and re-layouts  14.3 us (9%)
  matrix products  11.8 us (7%)
  starting transfers between devices  8.1 us (5%)
    pallas_call x1, Pallas kernels, chan_gather(): pl.pallas_call(functools.partial(gather_kernel, chips, groups), out_shape...  53.5 us
    pallas_call x1, Pallas kernels, half_gather(): pl.pallas_call(functools.partial(half_gather_kernel, chips), out_shape=ja...  32 us
    pallas_call x2, Pallas kernels, ctx_exchange(): pl.pallas_call(functools.partial(exchange_kernel, groups), out_shape=jax....  27.4 us
    unnamed x17, local copies, waits for them, and re-layouts  7.81 us
    unnamed x7, other arithmetic  5.13 us
    dot_general x1, matrix products, body(): lax.dot_general(w_flat, inputs_t, (((0,), (0,)), ((), ())), preferred_ele...  4.92 us
    ppermute x1, starting transfers between devices, body(): result = (mine + lax.ppermute(other, 'chan', pairs)).astype(jnp.bfloat16)  4.29 us
    all_to_all x1, starting transfers between devices, body(): lax.all_to_all(w_late, 'chan', 1, 0, tiled=True, axis_index_groups=same_c...  3.81 us
  transfers between devices with their start and end apart: 2, of which 1 were waited for; matrix products, arithmetic and copies ran while one was open for 18% of the time, Pallas kernels for 17%

profile of v8, /device:TPU:1, one launch (start us, length us, event | category | flops | bytes accessed | tf_op | source)
XLA Modules:
  0.0 162.9 jit_solution(10691060377049353687)
XLA Ops:
  0.0 1.7 %copy.19 = bf16[512,128]{0,1:T(8,128)(2,1)} copy(bf16[512,128]{1,0:T(8,128)(2,1)} %param.6) | data formatting | bytes 262144 | tf_op args[0]
  1.7 1.7 %copy.20 = bf16[128,512]{1,0:T(8,128)(2,1)} copy(bf16[128,512]{0,1:T(8,128)(2,1)} %bitcast.137) | data formatting | bytes 262144 | tf_op jit(solution)/shard_map/input_gather_and_filter_to_owner/transpose | solution.py:307
  3.3 53.5 %input_gather_and_filter_to_owner.1 = (bf16[32,128,512]{2,1,0:T(8,128)(2,1)}, bf16[8,16,512]{2,1,0:T(8,128)(2,1)}) custom-call(bf16[128,512]{1,0:T(8,128)(2,1)} %bitcast.134, bf16[8,16,512]{2,1,0:T(8,128)(2,1)} %bitcast.135), custom_call_target="tpu_custom_call" | custom-call | tf_op jit(solution)/shard_map/input_gather_and_filter_to_owner/pallas_call | solution.py:183
  56.9 2.3 %copy.21 = bf16[128,4096]{0,1:T(8,128)(2,1)} copy(bf16[128,4096]{1,0:T(8,128)(2,1)} %param.11) | data formatting | bytes 2097152 | tf_op jit(solution)/shard_map/out_weight_columns/optimization_barrier | solution.py:311
  59.2 3.8 %all-to-all-start = ((bf16[128,16,256]{0,2,1:T(8,128)(2,1)}), bf16[128,16,256]{0,2,1:T(8,128)(2,1)S(1)}, u32[]{:S(2)}, u32[]{:S(2)}) async-start(bf16[128,16,256]{0,2,1:T(8,128)(2,1)} %bitcast.4), calls=%async_computation | async-start | bytes 2097152 | tf_op jit(solution)/shard_map/out_weight_columns/all_to_all | solution.py:314
  63.0 0.5 fusion.45
  63.5 4.7 %copy.23 = bf16[4096,3,128]{0,2,1:T(8,128)(2,1)} copy(bf16[4096,3,128]{2,0,1:T(8,128)(2,1)} %param.7) | data formatting | bytes 6291456 | tf_op args[1]
  68.3 4.9 %convolution_convert_fusion.1 = bf16[512,384]{0,1:T(8,128)(2,1)S(1)} fusion(bf16[4096,384]{0,1:T(8,128)(2,1)} %bitcast.125, bf16[4096,512]{1,0:T(8,128)(2,1)} %bitcast.138), kind=kOutput, calls=%fused_computation.11 | convolution fusion | flops 1610809344 | bytes 7733248 | tf_op jit(solution)/shard_map/input_projection/dot_general | solution.py:318
  73.2 0.0 copy-start.5
  73.2 0.8 copy.32
  74.0 16.1 %projection_to_owner.1 = bf16[8,3,16,512]{3,2,1,0:T(8,128)(2,1)} custom-call(bf16[8,3,16,512]{3,2,1,0:T(8,128)(2,1)} %bitcast.132), custom_call_target="tpu_custom_call" | custom-call | tf_op jit(solution)/shard_map/projection_to_owner/pallas_call | solution.py:145
  90.1 1.0 slice.141
  91.1 1.2 fusion.13
  92.3 0.6 fusion.48
  92.9 0.0 copy-done.5
  92.9 0.1 fusion.69
  93.0 1.4 add_convert_fusion
  94.4 1.5 negate_convert_fusion
  95.8 0.0 copy-start
  95.9 0.0 copy-start.2
  95.9 0.0 copy-start.4
  95.9 0.8 convolution_convert_fusion
  96.7 0.1 slice_convert_fusion.2
  96.8 0.1 copy-done.4
  96.9 0.1 slice.101
  97.1 0.1 copy-done
  97.2 0.7 copy-done.2
  97.8 1.5 fusion.3
  99.3 0.1 slice_convert_fusion.3
  99.4 0.7 fusion.59
  100.1 0.7 fusion.60
  100.8 0.1 fusion.57
  100.9 0.0 copy-start.6
  100.9 0.1 fusion.58
  101.0 0.1 fusion.55
  101.1 0.1 fusion.56
  101.2 0.1 fusion.54
  101.3 0.1 fusion.53
  101.3 0.6 fusion.37
  101.9 0.6 fusion.38
  102.6 0.6 fusion.39
  103.2 0.6 fusion.40
  103.8 0.6 fusion.41
  104.4 0.0 copy-done.6
  104.4 0.1 dynamic_slice.13
  104.5 1.4 fusion.42
  105.9 0.1 fusion.61
  106.0 0.0 copy-start.1
  106.1 0.1 fusion.62
  106.2 0.6 fusion.43
  106.8 0.2 fusion.63
  107.0 0.2 fusion.64
  107.2 0.6 fusion.44
  107.8 0.0 copy-done.1
  107.8 0.5 copy-done.3
  108.3 2.2 %fusion.10.x_ref = bf16[8,16,512]{2,1,0:T(8,128)(2,1)} fusion(bf16[8,16,2048]{2,1,0:T(8,128)(2,1)} %fusion.44, bf16[1024,1024]{1,0:T(8,128)(2,1)S(1)} %bitcast.131, bf16[1024,1024]{1,0:T(8,128)(2,1)S(1)} %bitcast.128, bf16[8,3,16,512]{3,2,0,1:T(8,128)(2,1)S(1)} %add_convert_fusion, f32[16]{0:T(128)S(1)} %dynamic_slice.13), kind=kOutput, calls=%fused_computation.15 | convolution fusion | flops 273350656 | bytes 5242944 | tf_op jit(solution)/shard_map/inverse_and_gate/idf,fa->ida/dot_general | solution.py:374
  110.5 11.3 %gated_back_to_rows.1 = bf16[8,16,512]{2,1,0:T(8,128)(2,1)} custom-call(bf16[8,16,512]{2,1,0:T(8,128)(2,1)} %fusion.10.x_ref), custom_call_target="tpu_custom_call" | custom-call | tf_op jit(solution)/shard_map/gated_back_to_rows/pallas_call | solution.py:145
  121.8 0.0 all-to-all-done
  121.8 0.5 copy.22
  122.4 32.0 %output_projection.1 = bf16[16,128,512]{2,1,0:T(8,128)(2,1)} custom-call(bf16[128,512]{1,0:T(8,128)(2,1)} %bitcast.133), custom_call_target="tpu_custom_call" | custom-call | tf_op jit(solution)/shard_map/output_projection/pallas_call | solution.py:265
  154.4 2.3 %fusion.77 = f32[512,256]{1,0:T(8,128)S(1)} fusion(bf16[2048,512]{1,0:T(8,128)(2,1)} %bitcast.122, bf16[2048,256]{1,0:T(8,128)(2,1)S(1)} %bitcast.123), kind=kOutput, calls=%fused_computation.124 | convolution fusion | flops 536870912 | bytes 3670016 | tf_op jit(solution)/shard_map/output_projection/dot_general | solution.py:388
  156.8 4.3 %collective-permute-start = (f32[512,128]{1,0:T(8,128)S(1)}, f32[512,128]{1,0:T(8,128)S(1)}, u32[]{:S(2)}, u32[]{:S(2)}) collective-permute-start(f32[512,128]{1,0:T(8,128)S(1)} %constant_dynamic-slice_fusion.2), channel_id=1, source_target_pairs={{0,1},{1,0},{2,3},{3,2},{4,5},{5,4},{6,7},{7,6},{8,9},{9,8},{10,11... | collective-permute-start | bytes 786440 | tf_op jit(solution)/shard_map/output_projection/ppermute | solution.py:395
  161.1 1.2 collective-permute-done
  162.2 0.7 add_convert_fusion.1
  (6 shorter events, 0.1 us)
Async XLA Ops:
  59.2 62.6 %all-to-all-start = ((bf16[128,16,256]{0,2,1:T(8,128)(2,1)}), bf16[128,16,256]{0,2,1:T(8,128)(2,1)S(1)}, u32[]{:S(2)}, u32[]{:S(2)}) async-start(bf16[128,16,256]{0,2,1:T(8,128)(2,1)} %bitcast.4), calls=%async_computation | async-start | bytes 2097152 | tf_op jit(solution)/shard_map/out_weight_columns/all_to_all | solution.py:314
  73.2 19.7 %copy-start.5 = (bf16[3,3,128]{2,1,0:T(4,128)(2,1)S(1)}, bf16[3,3,128]{2,1,0:T(4,128)(2,1)}, u32[]{:S(2)}) copy-start(bf16[3,3,128]{2,1,0:T(4,128)(2,1)} %param.8) | copy-start | bytes 6916
  95.8 1.3 copy-start
  95.9 2.0 %copy-start.2 = (bf16[32,32,1024]{2,1,0:T(8,128)(2,1)}, bf16[32,32,1024]{2,1,0:T(8,128)(2,1)S(1)}, u32[]{:S(2)}) copy-start(bf16[32,32,1024]{2,1,0:T(8,128)(2,1)S(1)} %get-tuple-element.28) | copy-start | bytes 6291460
  95.9 1.1 copy-start.4
  100.9 3.5 %copy-start.6 = (f32[128]{0:T(128)S(1)}, f32[128]{0:T(128)}, u32[]{:S(2)}) copy-start(f32[128]{0:T(128)} %param.9) | copy-start | bytes 1540
  106.0 1.8 %copy-start.1 = (bf16[32,32,1024]{2,1,0:T(8,128)(2,1)S(1)}, bf16[32,32,1024]{2,1,0:T(8,128)(2,1)}, u32[]{:S(2)}) copy-start(bf16[32,32,1024]{2,1,0:T(8,128)(2,1)} %copy-done) | copy-start | bytes 6291460
  106.1 2.3 %copy-start.3 = (bf16[32,32,1024]{2,1,0:T(8,128)(2,1)S(1)}, bf16[32,32,1024]{2,1,0:T(8,128)(2,1)}, u32[]{:S(2)}) copy-start(bf16[32,32,1024]{2,1,0:T(8,128)(2,1)} %copy-done.2) | copy-start | bytes 6291460
  156.8 5.5 %collective-permute-start = (f32[512,128]{1,0:T(8,128)S(1)}, f32[512,128]{1,0:T(8,128)S(1)}, u32[]{:S(2)}, u32[]{:S(2)}) collective-permute-start(f32[512,128]{1,0:T(8,128)S(1)} %constant_dynamic-slice_fusion.2), channel_id=1, source_target_pairs={{0,1},{1,0},{2,3},{3,2},{4,5},{5,4},{6,7},{7,6},{8,9},{9,8},{10,11... | collective-permute-start | bytes 786440 | tf_op jit(solution)/shard_map/output_projection/ppermute | solution.py:395

commit v9 on v8

--- a/solution.py
+++ b/solution.py
@@ -307,12 +307,6 @@
         taps_t = filter_taps.T.reshape(groups, own, span_len)
         inputs_t, taps_t = chan_gather(inputs.T, taps_t, 0)
 
-    with jax.named_scope("out_weight_columns"):
-        w_late, inputs_t = lax.optimization_barrier((w_out, inputs_t))
-        size = lax.axis_size("chan")
-        same_core = [list(range(c, size, 2)) for c in range(2)]
-        w_cols = lax.all_to_all(w_late, "chan", 1, 0, tiled=True, axis_index_groups=same_core)
-
     with jax.named_scope("input_projection"):
         w_flat = w_in.reshape(w_in.shape[0], 3 * width_dev)
         proj_t = lax.dot_general(
@@ -322,6 +316,12 @@
     with jax.named_scope("projection_to_owner"):
         proj_t = proj_t.reshape(3, groups, own, span_len).transpose(1, 0, 2, 3)
         proj_t = ctx_exchange(proj_t, 3)
+
+    with jax.named_scope("out_weight_columns"):
+        w_late, proj_t = lax.optimization_barrier((w_out, proj_t))
+        size = lax.axis_size("chan")
+        same_core = [list(range(c, size, 2)) for c in range(2)]
+        w_cols = lax.all_to_all(w_late, "chan", 1, 0, tiled=True, axis_index_groups=same_core)
 
     with jax.named_scope("short_conv"):
         start = position * own

time: 164 us -> 153 us (0.933)
  Pallas kernels: 113 us -> 107 us
  local copies, waits for them, and re-layouts: 14.3 us -> 11.8 us
  other arithmetic: 14.4 us -> 12.5 us
    pallas_call x2, Pallas kernels: 27.4 us -> 23.1 us  [ctx_exchange(): pl.pallas_call(functools.partial(exchange_kernel, groups), out_shape=jax....]
    pallas_call x1, Pallas kernels: 32 us -> 30.1 us  [half_gather(): pl.pallas_call(functools.partial(half_gather_kernel, chips), out_shape=ja...]
    unnamed x17 -> x18, local copies, waits for them, and re-layouts: 7.81 us -> 6.24 us
  transfers between devices with their start and end apart: 2 -> 2, of which waited for: 1 -> 1; matrix products, arithmetic and copies ran while one was open for 18% -> 11% of each run, Pallas kernels for 17% -> 8%
where the time goes in v9:
time: 153 us
  Pallas kernels  107 us (70%)
  other arithmetic  12.5 us (8%)
  local copies, waits for them, and re-layouts  11.8 us (8%)
  matrix products  10.8 us (7%)
  starting transfers between devices  9.32 us (6%)
    pallas_call x1, Pallas kernels, chan_gather(): pl.pallas_call(functools.partial(gather_kernel, chips, groups), out_shape...  53.7 us
    pallas_call x1, Pallas kernels, half_gather(): pl.pallas_call(functools.partial(half_gather_kernel, chips), out_shape=ja...  30.1 us
    pallas_call x2, Pallas kernels, ctx_exchange(): pl.pallas_call(functools.partial(exchange_kernel, groups), out_shape=jax....  23.1 us
    unnamed x18, local copies, waits for them, and re-layouts  6.24 us
    ppermute x1, starting transfers between devices, body(): result = (mine + lax.ppermute(other, 'chan', pairs)).astype(jnp.bfloat16)  5.5 us
    unnamed x7, other arithmetic  5.21 us
    dot_general x1, matrix products, body(): lax.dot_general(w_flat, inputs_t, (((0,), (0,)), ((), ())), preferred_ele...  3.97 us
    all_to_all x1, starting transfers between devices, body(): lax.all_to_all(w_late, 'chan', 1, 0, tiled=True, axis_index_groups=same_c...  3.81 us
  transfers between devices with their start and end apart: 2, of which 1 were waited for; matrix products, arithmetic and copies ran while one was open for 11% of the time, Pallas kernels for 8%

profile of v9, /device:TPU:1, one launch (start us, length us, event | category | flops | bytes accessed | tf_op | source)
XLA Modules:
  0.0 152.8 jit_solution(283657892501789272)
XLA Ops:
  0.0 1.7 %copy.19 = bf16[512,128]{0,1:T(8,128)(2,1)} copy(bf16[512,128]{1,0:T(8,128)(2,1)} %param.6) | data formatting | bytes 262144 | tf_op args[0]
  1.7 1.7 %copy.20 = bf16[128,512]{1,0:T(8,128)(2,1)} copy(bf16[128,512]{0,1:T(8,128)(2,1)} %bitcast.137) | data formatting | bytes 262144 | tf_op jit(solution)/shard_map/input_gather_and_filter_to_owner/transpose | solution.py:307
  3.3 3.2 %copy.21 = bf16[4096,3,128]{0,2,1:T(8,128)(2,1)S(1)} copy(bf16[4096,3,128]{2,0,1:T(8,128)(2,1)} %param.7) | data formatting | bytes 6291456 | tf_op args[1]
  6.5 53.7 %input_gather_and_filter_to_owner.1 = (bf16[32,128,512]{2,1,0:T(8,128)(2,1)}, bf16[8,16,512]{2,1,0:T(8,128)(2,1)}) custom-call(bf16[128,512]{1,0:T(8,128)(2,1)} %bitcast.134, bf16[8,16,512]{2,1,0:T(8,128)(2,1)} %bitcast.135), custom_call_target="tpu_custom_call" | custom-call | tf_op jit(solution)/shard_map/input_gather_and_filter_to_owner/pallas_call | solution.py:183
  60.2 4.0 %convolution_convert_fusion.1 = bf16[512,384]{0,1:T(8,128)(2,1)S(1)} fusion(bf16[4096,384]{0,1:T(8,128)(2,1)S(1)} %bitcast.125, bf16[4096,512]{1,0:T(8,128)(2,1)} %bitcast.138), kind=kOutput, calls=%fused_computation.11 | convolution fusion | flops 1610809344 | bytes 7733248 | tf_op jit(solution)/shard_map/input_projection/dot_general | solution.py:312
  64.2 0.8 copy.32
  65.0 10.8 %projection_to_owner.1 = bf16[8,3,16,512]{3,2,1,0:T(8,128)(2,1)} custom-call(bf16[8,3,16,512]{3,2,1,0:T(8,128)(2,1)} %bitcast.132), custom_call_target="tpu_custom_call" | custom-call | tf_op jit(solution)/shard_map/projection_to_owner/pallas_call | solution.py:145
  75.8 0.0 copy-start
  75.8 0.0 copy-start.6
  75.8 2.3 %copy.23 = bf16[128,4096]{0,1:T(8,128)(2,1)} copy(bf16[128,4096]{1,0:T(8,128)(2,1)} %param.11) | data formatting | bytes 2097152 | tf_op jit(solution)/shard_map/out_weight_columns/optimization_barrier | solution.py:321
  78.2 3.8 %all-to-all-start = ((bf16[128,16,256]{0,2,1:T(8,128)(2,1)}), bf16[128,16,256]{0,2,1:T(8,128)(2,1)S(1)}, u32[]{:S(2)}, u32[]{:S(2)}) async-start(bf16[128,16,256]{0,2,1:T(8,128)(2,1)} %bitcast.8), calls=%async_computation | async-start | bytes 2097152 | tf_op jit(solution)/shard_map/out_weight_columns/all_to_all | solution.py:324
  82.0 0.5 fusion.45
  82.5 0.0 copy-done
  82.6 0.1 slice.141
  82.7 0.2 fusion.13
  82.9 0.6 fusion.48
  83.5 0.0 copy-done.6
  83.5 0.1 fusion.69
  83.6 0.4 add_convert_fusion
  84.0 1.5 negate_convert_fusion
  85.5 0.0 copy-start.1
  85.5 0.0 copy-start.3
  85.5 0.8 convolution_convert_fusion
  86.3 0.1 slice_convert_fusion.2
  86.5 0.1 copy-done.5
  86.6 0.1 slice.101
  86.7 0.1 copy-done.1
  86.8 0.7 copy-done.3
  87.4 1.5 fusion.3
  88.9 0.1 slice_convert_fusion.3
  89.1 0.7 fusion.59
  89.8 0.7 fusion.60
  90.5 0.1 fusion.57
  90.6 0.0 copy-start.7
  90.6 0.1 fusion.58
  90.7 0.1 fusion.55
  90.7 0.1 fusion.56
  90.8 0.1 fusion.54
  90.9 0.1 fusion.53
  91.0 0.7 fusion.37
  91.6 0.6 fusion.38
  92.2 0.6 fusion.39
  92.9 0.6 fusion.40
  93.5 0.6 fusion.41
  94.1 0.1 dynamic_slice.13
  94.2 1.4 fusion.42
  95.6 0.1 fusion.61
  95.8 0.0 copy-start.2
  95.8 0.0 copy-start.4
  95.8 0.1 fusion.62
  95.9 0.6 fusion.43
  96.5 0.2 fusion.63
  96.7 0.2 fusion.64
  96.9 0.6 fusion.44
  97.5 0.5 copy-done.4
  98.0 2.2 %fusion.10.x_ref = bf16[8,16,512]{2,1,0:T(8,128)(2,1)} fusion(bf16[8,16,2048]{2,1,0:T(8,128)(2,1)} %fusion.44, bf16[1024,1024]{1,0:T(8,128)(2,1)S(1)} %bitcast.131, bf16[1024,1024]{1,0:T(8,128)(2,1)S(1)} %bitcast.128, bf16[8,3,16,512]{3,2,0,1:T(8,128)(2,1)S(1)} %add_convert_fusion, f32[16]{0:T(128)S(1)} %dynamic_slice.13), kind=kOutput, calls=%fused_computation.15 | convolution fusion | flops 273350656 | bytes 5242944 | tf_op jit(solution)/shard_map/inverse_and_gate/idf,fa->ida/dot_general | solution.py:374
  100.2 12.2 %gated_back_to_rows.1 = bf16[8,16,512]{2,1,0:T(8,128)(2,1)} custom-call(bf16[8,16,512]{2,1,0:T(8,128)(2,1)} %fusion.10.x_ref), custom_call_target="tpu_custom_call" | custom-call | tf_op jit(solution)/shard_map/gated_back_to_rows/pallas_call | solution.py:145
  112.5 0.0 all-to-all-done
  112.5 0.5 copy.24
  113.0 30.1 %output_projection.1 = bf16[16,128,512]{2,1,0:T(8,128)(2,1)} custom-call(bf16[128,512]{1,0:T(8,128)(2,1)} %bitcast.133), custom_call_target="tpu_custom_call" | custom-call | tf_op jit(solution)/shard_map/output_projection/pallas_call | solution.py:265
  143.1 2.3 %fusion.77 = f32[512,256]{1,0:T(8,128)S(1)} fusion(bf16[2048,512]{1,0:T(8,128)(2,1)} %bitcast.122, bf16[2048,256]{1,0:T(8,128)(2,1)S(1)} %bitcast.123), kind=kOutput, calls=%fused_computation.124 | convolution fusion | flops 536870912 | bytes 3670016 | tf_op jit(solution)/shard_map/output_projection/dot_general | solution.py:388
  145.5 5.5 %collective-permute-start = (f32[512,128]{1,0:T(8,128)S(1)}, f32[512,128]{1,0:T(8,128)S(1)}, u32[]{:S(2)}, u32[]{:S(2)}) collective-permute-start(f32[512,128]{1,0:T(8,128)S(1)} %constant_dynamic-slice_fusion.2), channel_id=1, source_target_pairs={{0,1},{1,0},{2,3},{3,2},{4,5},{5,4},{6,7},{7,6},{8,9},{9,8},{10,11... | collective-permute-start | bytes 786440 | tf_op jit(solution)/shard_map/output_projection/ppermute | solution.py:395
  151.0 1.2 collective-permute-done
  152.1 0.7 add_convert_fusion.1
  (8 shorter events, 0.1 us)
Async XLA Ops:
  75.8 6.7 %copy-start = (bf16[8,3,16,512]{3,2,1,0:T(8,128)(2,1)S(1)}, bf16[8,3,16,512]{3,2,1,0:T(8,128)(2,1)}, u32[]{:S(2)}) copy-start(bf16[8,3,16,512]{3,2,1,0:T(8,128)(2,1)} %projection_to_owner.1) | copy-start | bytes 1179652
  75.8 7.7 %copy-start.6 = (bf16[3,3,128]{2,1,0:T(4,128)(2,1)S(1)}, bf16[3,3,128]{2,1,0:T(4,128)(2,1)}, u32[]{:S(2)}) copy-start(bf16[3,3,128]{2,1,0:T(4,128)(2,1)} %param.8) | copy-start | bytes 6916
  78.2 34.3 %all-to-all-start = ((bf16[128,16,256]{0,2,1:T(8,128)(2,1)}), bf16[128,16,256]{0,2,1:T(8,128)(2,1)S(1)}, u32[]{:S(2)}, u32[]{:S(2)}) async-start(bf16[128,16,256]{0,2,1:T(8,128)(2,1)} %bitcast.8), calls=%async_computation | async-start | bytes 2097152 | tf_op jit(solution)/shard_map/out_weight_columns/all_to_all | solution.py:324
  85.5 1.3 copy-start.1
  85.5 2.0 %copy-start.3 = (bf16[32,32,1024]{2,1,0:T(8,128)(2,1)}, bf16[32,32,1024]{2,1,0:T(8,128)(2,1)S(1)}, u32[]{:S(2)}) copy-start(bf16[32,32,1024]{2,1,0:T(8,128)(2,1)S(1)} %get-tuple-element.28) | copy-start | bytes 6291460
  85.5 1.1 copy-start.5
  90.6 3.6 %copy-start.7 = (f32[128]{0:T(128)S(1)}, f32[128]{0:T(128)}, u32[]{:S(2)}) copy-start(f32[128]{0:T(128)} %param.9) | copy-start | bytes 1540
  95.8 1.8 %copy-start.2 = (bf16[32,32,1024]{2,1,0:T(8,128)(2,1)S(1)}, bf16[32,32,1024]{2,1,0:T(8,128)(2,1)}, u32[]{:S(2)}) copy-start(bf16[32,32,1024]{2,1,0:T(8,128)(2,1)} %copy-done.1) | copy-start | bytes 6291460
  95.8 2.3 %copy-start.4 = (bf16[32,32,1024]{2,1,0:T(8,128)(2,1)S(1)}, bf16[32,32,1024]{2,1,0:T(8,128)(2,1)}, u32[]{:S(2)}) copy-start(bf16[32,32,1024]{2,1,0:T(8,128)(2,1)} %copy-done.3) | copy-start | bytes 6291460
  145.5 6.7 %collective-permute-start = (f32[512,128]{1,0:T(8,128)S(1)}, f32[512,128]{1,0:T(8,128)S(1)}, u32[]{:S(2)}, u32[]{:S(2)}) collective-permute-start(f32[512,128]{1,0:T(8,128)S(1)} %constant_dynamic-slice_fusion.2), channel_id=1, source_target_pairs={{0,1},{1,0},{2,3},{3,2},{4,5},{5,4},{6,7},{7,6},{8,9},{9,8},{10,11... | collective-permute-start | bytes 786440 | tf_op jit(solution)/shard_map/output_projection/ppermute | solution.py:395

commit v10 on v9

--- a/solution.py
+++ b/solution.py
@@ -192,8 +192,8 @@
     return gathered if t is None else (gathered, outs[1])
 
 
-def half_gather_kernel(chips, x_ref, out_ref, local_sem, cross_send, cross_recv, up_send, up_recv,
-                       down_send, down_recv):
+def half_gather_kernel(chips, groups, t_ref, out_ref, x_ref, local_sem, cross_send, cross_recv,
+                       up_send, up_recv, down_send, down_recv, t_local_sem, t_send, t_recv):
     row = lax.axis_index("ctx")
     me = lax.axis_index("chan")
     z = me // PER_Z
@@ -208,7 +208,29 @@
     barrier = pltpu.get_barrier_semaphore()
     for peer in (across, ahead, behind):
         pl.semaphore_signal(barrier, inc=1, device_id=(row, peer), device_id_type=MESH)
-    pl.semaphore_wait(barrier, 3)
+    for peer in ctx_peers(groups):
+        pl.semaphore_signal(barrier, inc=1, device_id=(peer, me), device_id_type=MESH)
+    pl.semaphore_wait(barrier, 3 + groups - 1)
+
+    slab = t_ref.shape[1]
+
+    def slot(g):
+        return x_ref.at[pl.ds(pl.multiple_of(g * slab, slab), slab)]
+
+    def give(k, peer, g):
+        return pltpu.make_async_remote_copy(
+            src_ref=t_ref.at[peer], dst_ref=slot(g), send_sem=t_send.at[k - 1],
+            recv_sem=t_recv.at[k - 1], device_id=(peer, me), device_id_type=MESH)
+
+    t_local = pltpu.make_async_copy(t_ref.at[row], slot(row), t_local_sem)
+    t_local.start()
+    for k in range(1, groups):
+        give(k, (row + k) % groups, row).start()
+    t_local.wait()
+    for k in range(1, groups):
+        give(k, (row + k) % groups, row).wait_send()
+        source = (row - k + groups) % groups
+        give(k, source, source).wait_recv()
 
     local = pltpu.make_async_copy(x_ref, out_ref.at[mine], local_sem)
     local.start()
@@ -257,17 +279,20 @@
         down(s, (z + s) % chips).wait_send()
 
 
-def half_gather(x, collective_id):
+def half_gather(t, collective_id):
     size = lax.axis_size("chan")
+    groups = lax.axis_size("ctx")
     chips = size // PER_Z
     assert chips % 2 == 0
     ups = downs = chips // 2
+    block = (t.shape[0] * t.shape[1], t.shape[2])
     out = pl.pallas_call(
-        functools.partial(half_gather_kernel, chips),
-        out_shape=jax.ShapeDtypeStruct((size // 2,) + x.shape, x.dtype),
+        functools.partial(half_gather_kernel, chips, groups),
+        out_shape=jax.ShapeDtypeStruct((size // 2,) + block, t.dtype),
         in_specs=[pl.BlockSpec(memory_space=pltpu.VMEM)],
         out_specs=pl.BlockSpec(memory_space=pltpu.VMEM),
         scratch_shapes=[
+            pltpu.VMEM(block, t.dtype),
             pltpu.SemaphoreType.DMA(()),
             pltpu.SemaphoreType.DMA(()),
             pltpu.SemaphoreType.DMA(()),
@@ -275,10 +300,13 @@
             pltpu.SemaphoreType.DMA((ups,)),
             pltpu.SemaphoreType.DMA((downs,)),
             pltpu.SemaphoreType.DMA((downs,)),
+            pltpu.SemaphoreType.DMA(()),
+            pltpu.SemaphoreType.DMA((groups - 1,)),
+            pltpu.SemaphoreType.DMA((groups - 1,)),
         ],
         compiler_params=pltpu.CompilerParams(collective_id=collective_id, has_side_effects=True),
-    )(x)
-    return out.reshape(size // 2 * x.shape[0], x.shape[1])
+    )(t)
+    return out.reshape(size // 2 * block[0], block[1])
 
 
 def dft_table(double_len):
@@ -378,12 +406,8 @@
         long_out = long_out + gain[None, :, None] * gated_in.astype(jnp.float32)
         gated_out = (gate_out.astype(jnp.float32) * long_out).astype(jnp.bfloat16)
 
-    with jax.named_scope("gated_back_to_rows"):
-        gated_out = ctx_exchange(gated_out, 4)
+    with jax.named_scope("output_projection"):
         w_cols, gated_out = lax.optimization_barrier((w_cols, gated_out))
-        gated_out = gated_out.reshape(width_dev, span_len)
-
-    with jax.named_scope("output_projection"):
         gathered = half_gather(gated_out, 1)
         partial = lax.dot_general(
             gathered, w_cols, (((0,), (0,)), ((), ())), preferred_element_type=jnp.float32

time: 153 us -> 157 us (1.026)
  waiting for transfers between devices: 1.16 us -> 7.32 us
  Pallas kernels: 107 us -> 103 us
    pallas_call x2 -> x1, Pallas kernels: 23.1 us -> 10.8 us  [ctx_exchange(): pl.pallas_call(functools.partial(exchange_kernel, groups), out_shape=jax....]
    pallas_call x1, Pallas kernels: 30.1 us -> 38.7 us  [half_gather(): pl.pallas_call(functools.partial(half_gather_kernel, chips, groups), out_...]
    all_to_all x1, waiting for transfers between devices: 0.01 us -> 6.15 us  [body(): lax.all_to_all(w_late, 'chan', 1, 0, tiled=True, axis_index_groups=same_c...]
  transfers between devices with their start and end apart: 2 -> 2, of which waited for: 1 -> 2; matrix products, arithmetic and copies ran while one was open for 11% -> 11% of each run, Pallas kernels for 8% -> 0%
where the time goes in v10:
time: 157 us; the launch traced here: 156 us
  Pallas kernels  103 us (66%)
  other arithmetic  12.5 us (8%)
  local copies, waits for them, and re-layouts  11.8 us (8%)
  matrix products  10.8 us (7%)
  starting transfers between devices  9.97 us (6%)
  waiting for transfers between devices  7.32 us (5%)
    pallas_call x1, Pallas kernels, chan_gather(): pl.pallas_call(functools.partial(gather_kernel, chips, groups), out_shape...  53.7 us
    pallas_call x1, Pallas kernels, half_gather(): pl.pallas_call(functools.partial(half_gather_kernel, chips, groups), out_...  38.7 us
    pallas_call x1, Pallas kernels, ctx_exchange(): pl.pallas_call(functools.partial(exchange_kernel, groups), out_shape=jax....  10.8 us
    unnamed x18, local copies, waits for them, and re-layouts  6.24 us
    ppermute x1, starting transfers between devices, body(): result = (mine + lax.ppermute(other, 'chan', pairs)).astype(jnp.bfloat16)  6.15 us
    all_to_all x1, waiting for transfers between devices, body(): lax.all_to_all(w_late, 'chan', 1, 0, tiled=True, axis_index_groups=same_c...  6.15 us
    unnamed x7, other arithmetic  5.21 us
    dot_general x1, matrix products, body(): lax.dot_general(w_flat, inputs_t, (((0,), (0,)), ((), ())), preferred_ele...  3.97 us
  transfers between devices with their start and end apart: 2, of which 2 were waited for; matrix products, arithmetic and copies ran while one was open for 11% of the time, Pallas kernels for 0%

profile of v10, /device:TPU:1, one launch (start us, length us, event | category | flops | bytes accessed | tf_op | source)
XLA Modules:
  0.0 156.0 jit_solution(3401705999671868049)
XLA Ops:
  0.0 1.7 %copy.19 = bf16[512,128]{0,1:T(8,128)(2,1)} copy(bf16[512,128]{1,0:T(8,128)(2,1)} %param.6) | data formatting | bytes 262144 | tf_op args[0]
  1.7 1.7 %copy.20 = bf16[128,512]{1,0:T(8,128)(2,1)} copy(bf16[128,512]{0,1:T(8,128)(2,1)} %bitcast.135) | data formatting | bytes 262144 | tf_op jit(solution)/shard_map/input_gather_and_filter_to_owner/transpose | solution.py:335
  3.3 3.2 %copy.21 = bf16[4096,3,128]{0,2,1:T(8,128)(2,1)S(1)} copy(bf16[4096,3,128]{2,0,1:T(8,128)(2,1)} %param.7) | data formatting | bytes 6291456 | tf_op args[1]
  6.5 53.7 %input_gather_and_filter_to_owner.1 = (bf16[32,128,512]{2,1,0:T(8,128)(2,1)}, bf16[8,16,512]{2,1,0:T(8,128)(2,1)}) custom-call(bf16[128,512]{1,0:T(8,128)(2,1)} %bitcast.132, bf16[8,16,512]{2,1,0:T(8,128)(2,1)} %bitcast.133), custom_call_target="tpu_custom_call" | custom-call | tf_op jit(solution)/shard_map/input_gather_and_filter_to_owner/pallas_call | solution.py:183
  60.2 4.0 %convolution_convert_fusion.1 = bf16[512,384]{0,1:T(8,128)(2,1)S(1)} fusion(bf16[4096,384]{0,1:T(8,128)(2,1)S(1)} %bitcast.124, bf16[4096,512]{1,0:T(8,128)(2,1)} %bitcast.136), kind=kOutput, calls=%fused_computation.11 | convolution fusion | flops 1610809344 | bytes 7733248 | tf_op jit(solution)/shard_map/input_projection/dot_general | solution.py:340
  64.2 0.8 copy.32
  65.0 10.8 %projection_to_owner.1 = bf16[8,3,16,512]{3,2,1,0:T(8,128)(2,1)} custom-call(bf16[8,3,16,512]{3,2,1,0:T(8,128)(2,1)} %bitcast.131), custom_call_target="tpu_custom_call" | custom-call | tf_op jit(solution)/shard_map/projection_to_owner/pallas_call | solution.py:145
  75.8 0.0 copy-start
  75.8 0.0 copy-start.6
  75.8 2.3 %copy.23 = bf16[128,4096]{0,1:T(8,128)(2,1)} copy(bf16[128,4096]{1,0:T(8,128)(2,1)} %param.11) | data formatting | bytes 2097152 | tf_op jit(solution)/shard_map/out_weight_columns/optimization_barrier | solution.py:349
  78.2 3.8 %all-to-all-start = ((bf16[128,16,256]{0,2,1:T(8,128)(2,1)}), bf16[128,16,256]{0,2,1:T(8,128)(2,1)S(1)}, u32[]{:S(2)}, u32[]{:S(2)}) async-start(bf16[128,16,256]{0,2,1:T(8,128)(2,1)} %bitcast.8), calls=%async_computation | async-start | bytes 2097152 | tf_op jit(solution)/shard_map/out_weight_columns/all_to_all | solution.py:352
  82.0 0.5 fusion.45
  82.5 0.0 copy-done
  82.6 0.1 slice.141
  82.7 0.2 fusion.13
  82.9 0.6 fusion.48
  83.5 0.0 copy-done.6
  83.5 0.1 fusion.69
  83.6 0.4 add_convert_fusion
  84.0 1.5 negate_convert_fusion
  85.5 0.0 copy-start.1
  85.5 0.0 copy-start.3
  85.5 0.0 copy-start.5
  85.5 0.8 convolution_convert_fusion
  86.3 0.1 slice_convert_fusion.2
  86.5 0.1 copy-done.5
  86.6 0.1 slice.101
  86.7 0.1 copy-done.1
  86.8 0.7 copy-done.3
  87.4 1.5 fusion.3
  88.9 0.1 slice_convert_fusion.3
  89.1 0.7 fusion.59
  89.8 0.7 fusion.60
  90.5 0.1 fusion.57
  90.6 0.0 copy-start.7
  90.6 0.1 fusion.58
  90.7 0.1 fusion.55
  90.7 0.1 fusion.56
  90.8 0.1 fusion.54
  90.9 0.1 fusion.53
  91.0 0.7 fusion.37
  91.6 0.6 fusion.38
  92.2 0.6 fusion.39
  92.9 0.6 fusion.40
  93.5 0.6 fusion.41
  94.1 0.0 copy-done.7
  94.1 0.1 dynamic_slice.13
  94.2 1.4 fusion.42
  95.6 0.1 fusion.61
  95.8 0.0 copy-start.2
  95.8 0.1 fusion.62
  95.9 0.6 fusion.43
  96.6 0.2 fusion.63
  96.7 0.2 fusion.64
  96.9 0.6 fusion.44
  97.5 0.5 copy-done.4
  98.0 2.2 %fusion.10.t_ref = bf16[8,16,512]{2,1,0:T(8,128)(2,1)} fusion(bf16[8,16,2048]{2,1,0:T(8,128)(2,1)} %fusion.44, bf16[1024,1024]{1,0:T(8,128)(2,1)S(1)} %bitcast.130, bf16[1024,1024]{1,0:T(8,128)(2,1)S(1)} %bitcast.127, bf16[8,3,16,512]{3,2,0,1:T(8,128)(2,1)S(1)} %add_convert_fusion, f32[16]{0:T(128)S(1)} %dynamic_slice.13), kind=kOutput, calls=%fused_computation.15 | convolution fusion | flops 273350656 | bytes 5242944 | tf_op jit(solution)/shard_map/inverse_and_gate/idf,fa->ida/dot_general | solution.py:402
  100.2 6.2 %all-to-all-done = bf16[128,16,256]{0,2,1:T(8,128)(2,1)S(1)} async-done(((bf16[128,16,256]{0,2,1:T(8,128)(2,1)}), bf16[128,16,256]{0,2,1:T(8,128)(2,1)S(1)}, u32[]{:S(2)}, u32[]{:S(2)}) %all-to-all-start) | async-done | bytes 1048608 | tf_op jit(solution)/shard_map/out_weight_columns/all_to_all | solution.py:352
  106.4 0.5 copy.24
  106.9 38.7 %output_projection.1 = bf16[16,128,512]{2,1,0:T(8,128)(2,1)} custom-call(bf16[8,16,512]{2,1,0:T(8,128)(2,1)} %fusion.10.t_ref), custom_call_target="tpu_custom_call" | custom-call | tf_op jit(solution)/shard_map/output_projection/pallas_call | solution.py:289
  145.6 2.3 %fusion.77 = f32[512,256]{1,0:T(8,128)S(1)} fusion(bf16[2048,512]{1,0:T(8,128)(2,1)} %bitcast.121, bf16[2048,256]{1,0:T(8,128)(2,1)S(1)} %bitcast.122), kind=kOutput, calls=%fused_computation.124 | convolution fusion | flops 536870912 | bytes 3670016 | tf_op jit(solution)/shard_map/output_projection/dot_general | solution.py:412
  148.0 6.2 %collective-permute-start = (f32[512,128]{1,0:T(8,128)S(1)}, f32[512,128]{1,0:T(8,128)S(1)}, u32[]{:S(2)}, u32[]{:S(2)}) collective-permute-start(f32[512,128]{1,0:T(8,128)S(1)} %constant_dynamic-slice_fusion.2), channel_id=1, source_target_pairs={{0,1},{1,0},{2,3},{3,2},{4,5},{5,4},{6,7},{7,6},{8,9},{9,8},{10,11... | collective-permute-start | bytes 786440 | tf_op jit(solution)/shard_map/output_projection/ppermute | solution.py:419
  154.2 1.2 collective-permute-done
  155.3 0.7 add_convert_fusion.1
  (7 shorter events, 0.1 us)
Async XLA Ops:
  75.8 6.7 %copy-start = (bf16[8,3,16,512]{3,2,1,0:T(8,128)(2,1)S(1)}, bf16[8,3,16,512]{3,2,1,0:T(8,128)(2,1)}, u32[]{:S(2)}) copy-start(bf16[8,3,16,512]{3,2,1,0:T(8,128)(2,1)} %projection_to_owner.1) | copy-start | bytes 1179652
  75.8 7.7 %copy-start.6 = (bf16[3,3,128]{2,1,0:T(4,128)(2,1)S(1)}, bf16[3,3,128]{2,1,0:T(4,128)(2,1)}, u32[]{:S(2)}) copy-start(bf16[3,3,128]{2,1,0:T(4,128)(2,1)} %param.8) | copy-start | bytes 6916
  78.2 28.2 %all-to-all-start = ((bf16[128,16,256]{0,2,1:T(8,128)(2,1)}), bf16[128,16,256]{0,2,1:T(8,128)(2,1)S(1)}, u32[]{:S(2)}, u32[]{:S(2)}) async-start(bf16[128,16,256]{0,2,1:T(8,128)(2,1)} %bitcast.8), calls=%async_computation | async-start | bytes 2097152 | tf_op jit(solution)/shard_map/out_weight_columns/all_to_all | solution.py:352
  85.5 1.3 copy-start.1
  85.5 2.0 %copy-start.3 = (bf16[32,32,1024]{2,1,0:T(8,128)(2,1)}, bf16[32,32,1024]{2,1,0:T(8,128)(2,1)S(1)}, u32[]{:S(2)}) copy-start(bf16[32,32,1024]{2,1,0:T(8,128)(2,1)S(1)} %get-tuple-element.28) | copy-start | bytes 6291460
  85.5 1.1 copy-start.5
  90.6 3.6 %copy-start.7 = (f32[128]{0:T(128)S(1)}, f32[128]{0:T(128)}, u32[]{:S(2)}) copy-start(f32[128]{0:T(128)} %param.9) | copy-start | bytes 1540
  95.8 1.8 %copy-start.2 = (bf16[32,32,1024]{2,1,0:T(8,128)(2,1)S(1)}, bf16[32,32,1024]{2,1,0:T(8,128)(2,1)}, u32[]{:S(2)}) copy-start(bf16[32,32,1024]{2,1,0:T(8,128)(2,1)} %copy-done.1) | copy-start | bytes 6291460
  95.8 2.3 %copy-start.4 = (bf16[32,32,1024]{2,1,0:T(8,128)(2,1)S(1)}, bf16[32,32,1024]{2,1,0:T(8,128)(2,1)}, u32[]{:S(2)}) copy-start(bf16[32,32,1024]{2,1,0:T(8,128)(2,1)} %copy-done.3) | copy-start | bytes 6291460
  148.0 7.3 %collective-permute-start = (f32[512,128]{1,0:T(8,128)S(1)}, f32[512,128]{1,0:T(8,128)S(1)}, u32[]{:S(2)}, u32[]{:S(2)}) collective-permute-start(f32[512,128]{1,0:T(8,128)S(1)} %constant_dynamic-slice_fusion.2), channel_id=1, source_target_pairs={{0,1},{1,0},{2,3},{3,2},{4,5},{5,4},{6,7},{7,6},{8,9},{9,8},{10,11... | collective-permute-start | bytes 786440 | tf_op jit(solution)/shard_map/output_projection/ppermute | solution.py:419

commit v11 on v10

--- a/solution.py
+++ b/solution.py
@@ -407,7 +407,6 @@
         gated_out = (gate_out.astype(jnp.float32) * long_out).astype(jnp.bfloat16)
 
     with jax.named_scope("output_projection"):
-        w_cols, gated_out = lax.optimization_barrier((w_cols, gated_out))
         gathered = half_gather(gated_out, 1)
         partial = lax.dot_general(
             gathered, w_cols, (((0,), (0,)), ((), ())), preferred_element_type=jnp.float32

time: 157 us -> 152 us (0.968)
  waiting for transfers between devices: 7.32 us -> 1.16 us
    all_to_all x1, waiting for transfers between devices: 6.15 us -> 0.01 us  [body(): lax.all_to_all(w_late, 'chan', 1, 0, tiled=True, axis_index_groups=same_c...]
  transfers between devices with their start and end apart: 2 -> 2, of which waited for: 2 -> 1; matrix products, arithmetic and copies ran while one was open for 11% -> 11% of each run, Pallas kernels for 0% -> 26%
where the time goes in v11:
time: 152 us; the launch traced here: 151 us
  Pallas kernels  104 us (68%)
  other arithmetic  12.5 us (8%)
  local copies, waits for them, and re-layouts  12 us (8%)
  matrix products  10.8 us (7%)
  starting transfers between devices  10.3 us (7%)
    pallas_call x1, Pallas kernels, chan_gather(): pl.pallas_call(functools.partial(gather_kernel, chips, groups), out_shape...  53.7 us
    pallas_call x1, Pallas kernels, half_gather(): pl.pallas_call(functools.partial(half_gather_kernel, chips, groups), out_...  39.8 us
    pallas_call x1, Pallas kernels, ctx_exchange(): pl.pallas_call(functools.partial(exchange_kernel, groups), out_shape=jax....  10.8 us
    ppermute x1, starting transfers between devices, body(): result = (mine + lax.ppermute(other, 'chan', pairs)).astype(jnp.bfloat16)  6.53 us
    unnamed x18, local copies, waits for them, and re-layouts  6.24 us
    unnamed x7, other arithmetic  5.21 us
    dot_general x1, matrix products, body(): lax.dot_general(w_flat, inputs_t, (((0,), (0,)), ((), ())), preferred_ele...  3.97 us
    all_to_all x1, starting transfers between devices, body(): lax.all_to_all(w_late, 'chan', 1, 0, tiled=True, axis_index_groups=same_c...  3.81 us
  transfers between devices with their start and end apart: 2, of which 1 were waited for; matrix products, arithmetic and copies ran while one was open for 11% of the time, Pallas kernels for 26%

profile of v11, /device:TPU:1, one launch (start us, length us, event | category | flops | bytes accessed | tf_op | source)
XLA Modules:
  0.0 151.5 jit_solution(5224666291005316097)
XLA Ops:
  0.0 1.7 %copy.13 = bf16[512,128]{0,1:T(8,128)(2,1)} copy(bf16[512,128]{1,0:T(8,128)(2,1)} %param.6) | data formatting | bytes 262144 | tf_op args[0]
  1.7 1.7 %copy.14 = bf16[128,512]{1,0:T(8,128)(2,1)} copy(bf16[128,512]{0,1:T(8,128)(2,1)} %bitcast.134) | data formatting | bytes 262144 | tf_op jit(solution)/shard_map/input_gather_and_filter_to_owner/transpose | solution.py:335
  3.3 3.2 %copy.15 = bf16[4096,3,128]{0,2,1:T(8,128)(2,1)S(1)} copy(bf16[4096,3,128]{2,0,1:T(8,128)(2,1)} %param.7) | data formatting | bytes 6291456 | tf_op args[1]
  6.5 53.7 %input_gather_and_filter_to_owner.1 = (bf16[32,128,512]{2,1,0:T(8,128)(2,1)}, bf16[8,16,512]{2,1,0:T(8,128)(2,1)}) custom-call(bf16[128,512]{1,0:T(8,128)(2,1)} %bitcast.131, bf16[8,16,512]{2,1,0:T(8,128)(2,1)} %bitcast.132), custom_call_target="tpu_custom_call" | custom-call | tf_op jit(solution)/shard_map/input_gather_and_filter_to_owner/pallas_call | solution.py:183
  60.2 4.0 %convolution_convert_fusion.1 = bf16[512,384]{0,1:T(8,128)(2,1)S(1)} fusion(bf16[4096,384]{0,1:T(8,128)(2,1)S(1)} %bitcast.123, bf16[4096,512]{1,0:T(8,128)(2,1)} %bitcast.135), kind=kOutput, calls=%fused_computation.11 | convolution fusion | flops 1610809344 | bytes 7733248 | tf_op jit(solution)/shard_map/input_projection/dot_general | solution.py:340
  64.2 0.8 copy.28
  65.0 10.8 %projection_to_owner.1 = bf16[8,3,16,512]{3,2,1,0:T(8,128)(2,1)} custom-call(bf16[8,3,16,512]{3,2,1,0:T(8,128)(2,1)} %bitcast.130), custom_call_target="tpu_custom_call" | custom-call | tf_op jit(solution)/shard_map/projection_to_owner/pallas_call | solution.py:145
  75.8 0.0 copy-start
  75.8 1.7 %copy.20 = bf16[128,4096]{0,1:T(8,128)(2,1)S(1)} copy(bf16[128,4096]{1,0:T(8,128)(2,1)} %param.11) | data formatting | bytes 2097152 | tf_op jit(solution)/shard_map/out_weight_columns/optimization_barrier | solution.py:349
  77.5 0.0 copy-start.6
  77.5 1.3 copy.21
  78.8 3.8 %all-to-all-start = ((bf16[128,16,256]{2,0,1:T(8,128)(2,1)}), bf16[128,16,256]{2,0,1:T(8,128)(2,1)S(1)}, u32[]{:S(2)}, u32[]{:S(2)}) async-start(bf16[128,16,256]{2,0,1:T(8,128)(2,1)} %copy.21), calls=%async_computation | async-start | bytes 2097152 | tf_op jit(solution)/shard_map/out_weight_columns/all_to_all | solution.py:352
  82.7 0.5 fusion.46
  83.2 0.0 copy-done
  83.3 0.1 slice.141
  83.3 0.2 fusion.14
  83.6 0.6 fusion.49
  84.2 0.0 copy-done.6
  84.2 0.1 fusion.70
  84.3 0.4 add_convert_fusion
  84.7 1.5 negate_convert_fusion
  86.1 0.0 copy-start.1
  86.2 0.0 copy-start.3
  86.2 0.0 copy-start.5
  86.2 0.8 convolution_convert_fusion
  87.0 0.1 slice_convert_fusion.2
  87.1 0.1 copy-done.5
  87.2 0.1 slice.101
  87.4 0.1 copy-done.1
  87.5 0.7 copy-done.3
  88.1 1.5 fusion.3
  89.6 0.1 slice_convert_fusion.3
  89.7 0.7 fusion.60
  90.5 0.7 fusion.61
  91.2 0.1 fusion.58
  91.2 0.0 copy-start.7
  91.3 0.1 fusion.59
  91.3 0.1 fusion.56
  91.4 0.1 fusion.57
  91.5 0.1 fusion.55
  91.6 0.1 fusion.54
  91.6 0.7 fusion.38
  92.3 0.6 fusion.39
  92.9 0.6 fusion.40
  93.5 0.6 fusion.41
  94.2 0.6 fusion.42
  94.8 0.1 dynamic_slice.13
  94.9 1.4 fusion.43
  96.3 0.1 fusion.62
  96.4 0.0 copy-start.2
  96.4 0.0 copy-start.4
  96.5 0.1 fusion.63
  96.6 0.6 fusion.44
  97.2 0.2 fusion.64
  97.4 0.2 fusion.65
  97.6 0.6 fusion.45
  98.2 0.5 copy-done.4
  98.7 2.2 %fusion.10.t_ref = bf16[8,16,512]{2,1,0:T(8,128)(2,1)} fusion(bf16[8,16,2048]{2,1,0:T(8,128)(2,1)} %fusion.45, bf16[1024,1024]{1,0:T(8,128)(2,1)S(1)} %bitcast.129, bf16[1024,1024]{1,0:T(8,128)(2,1)S(1)} %bitcast.126, bf16[8,3,16,512]{3,2,0,1:T(8,128)(2,1)S(1)} %add_convert_fusion, f32[16]{0:T(128)S(1)} %dynamic_slice.13), kind=kOutput, calls=%fused_computation.16 | convolution fusion | flops 273350656 | bytes 5242944 | tf_op jit(solution)/shard_map/inverse_and_gate/idf,fa->ida/dot_general | solution.py:402
  100.9 39.8 %output_projection.1 = bf16[16,128,512]{2,1,0:T(8,128)(2,1)} custom-call(bf16[8,16,512]{2,1,0:T(8,128)(2,1)} %fusion.10.t_ref), custom_call_target="tpu_custom_call" | custom-call | tf_op jit(solution)/shard_map/output_projection/pallas_call | solution.py:289
  140.7 0.0 all-to-all-done
  140.7 2.3 %convolution_bitcast_fusion = f32[512,256]{1,0:T(8,128)S(1)} fusion(bf16[16,128,512]{2,1,0:T(8,128)(2,1)} %output_projection.1, bf16[128,16,256]{2,0,1:T(8,128)(2,1)S(1)} %all-to-all-done), kind=kOutput, calls=%fused_computation.12 | convolution fusion | flops 536870912 | bytes 3670016 | tf_op jit(solution)/shard_map/output_projection/dot_general | solution.py:411
  143.1 6.5 %collective-permute-start = (f32[512,128]{1,0:T(8,128)S(1)}, f32[512,128]{1,0:T(8,128)S(1)}, u32[]{:S(2)}, u32[]{:S(2)}) collective-permute-start(f32[512,128]{1,0:T(8,128)S(1)} %constant_dynamic-slice_fusion.2), channel_id=1, source_target_pairs={{0,1},{1,0},{2,3},{3,2},{4,5},{5,4},{6,7},{7,6},{8,9},{9,8},{10,11... | collective-permute-start | bytes 786440 | tf_op jit(solution)/shard_map/output_projection/ppermute | solution.py:418
  149.6 1.2 collective-permute-done
  150.8 0.7 add_convert_fusion.1
  (7 shorter events, 0.1 us)
Async XLA Ops:
  75.8 7.4 %copy-start = (bf16[8,3,16,512]{3,2,1,0:T(8,128)(2,1)S(1)}, bf16[8,3,16,512]{3,2,1,0:T(8,128)(2,1)}, u32[]{:S(2)}) copy-start(bf16[8,3,16,512]{3,2,1,0:T(8,128)(2,1)} %projection_to_owner.1) | copy-start | bytes 1179652
  77.5 6.7 %copy-start.6 = (bf16[3,3,128]{2,1,0:T(4,128)(2,1)S(1)}, bf16[3,3,128]{2,1,0:T(4,128)(2,1)}, u32[]{:S(2)}) copy-start(bf16[3,3,128]{2,1,0:T(4,128)(2,1)} %param.8) | copy-start | bytes 6916
  78.8 61.9 %all-to-all-start = ((bf16[128,16,256]{2,0,1:T(8,128)(2,1)}), bf16[128,16,256]{2,0,1:T(8,128)(2,1)S(1)}, u32[]{:S(2)}, u32[]{:S(2)}) async-start(bf16[128,16,256]{2,0,1:T(8,128)(2,1)} %copy.21), calls=%async_computation | async-start | bytes 2097152 | tf_op jit(solution)/shard_map/out_weight_columns/all_to_all | solution.py:352
  86.1 1.3 copy-start.1
  86.2 2.0 %copy-start.3 = (bf16[32,32,1024]{2,1,0:T(8,128)(2,1)}, bf16[32,32,1024]{2,1,0:T(8,128)(2,1)S(1)}, u32[]{:S(2)}) copy-start(bf16[32,32,1024]{2,1,0:T(8,128)(2,1)S(1)} %get-tuple-element.24) | copy-start | bytes 6291460
  86.2 1.1 copy-start.5
  91.2 3.6 %copy-start.7 = (f32[128]{0:T(128)S(1)}, f32[128]{0:T(128)}, u32[]{:S(2)}) copy-start(f32[128]{0:T(128)} %param.9) | copy-start | bytes 1540
  96.4 1.8 %copy-start.2 = (bf16[32,32,1024]{2,1,0:T(8,128)(2,1)S(1)}, bf16[32,32,1024]{2,1,0:T(8,128)(2,1)}, u32[]{:S(2)}) copy-start(bf16[32,32,1024]{2,1,0:T(8,128)(2,1)} %copy-done.1) | copy-start | bytes 6291460
  96.4 2.3 %copy-start.4 = (bf16[32,32,1024]{2,1,0:T(8,128)(2,1)S(1)}, bf16[32,32,1024]{2,1,0:T(8,128)(2,1)}, u32[]{:S(2)}) copy-start(bf16[32,32,1024]{2,1,0:T(8,128)(2,1)} %copy-done.3) | copy-start | bytes 6291460
  143.1 7.7 %collective-permute-start = (f32[512,128]{1,0:T(8,128)S(1)}, f32[512,128]{1,0:T(8,128)S(1)}, u32[]{:S(2)}, u32[]{:S(2)}) collective-permute-start(f32[512,128]{1,0:T(8,128)S(1)} %constant_dynamic-slice_fusion.2), channel_id=1, source_target_pairs={{0,1},{1,0},{2,3},{3,2},{4,5},{5,4},{6,7},{7,6},{8,9},{9,8},{10,11... | collective-permute-start | bytes 786440 | tf_op jit(solution)/shard_map/output_projection/ppermute | solution.py:418

commit v12 on v11

--- a/solution.py
+++ b/solution.py
@@ -387,16 +387,16 @@
         imag_g = spectra_taps[:, :, double_len:].astype(jnp.float32)
         real_u = spectra_in[:, :, :double_len].astype(jnp.float32)
         imag_u = spectra_in[:, :, double_len:].astype(jnp.float32)
-        mixed = []
-        for target in range(groups):
-            acc_r = jnp.zeros((own, double_len), jnp.float32)
-            acc_i = jnp.zeros((own, double_len), jnp.float32)
-            for source in range(target + 1):
-                lag = target - source
-                acc_r = acc_r + (real_g[lag] * real_u[source] - imag_g[lag] * imag_u[source])
-                acc_i = acc_i + (real_g[lag] * imag_u[source] + imag_g[lag] * real_u[source])
-            mixed.append(jnp.concatenate([acc_r, acc_i], 1))
-        mixture = jnp.stack(mixed, 0).astype(jnp.bfloat16)
+        acc_r = jnp.zeros(real_u.shape, jnp.float32)
+        acc_i = jnp.zeros(real_u.shape, jnp.float32)
+        for lag in range(groups):
+            keep = groups - lag
+            shift = ((lag, 0), (0, 0), (0, 0))
+            acc_r = acc_r + jnp.pad(
+                real_g[lag] * real_u[:keep] - imag_g[lag] * imag_u[:keep], shift)
+            acc_i = acc_i + jnp.pad(
+                real_g[lag] * imag_u[:keep] + imag_g[lag] * real_u[:keep], shift)
+        mixture = jnp.concatenate([acc_r, acc_i], 2).astype(jnp.bfloat16)
 
     with jax.named_scope("inverse_and_gate"):
         long_out = jnp.einsum(

time: 152 us -> 147 us (0.967)
  other arithmetic: 12.5 us -> 5.25 us
  Pallas kernels: 104 us -> 111 us
  starting transfers between devices: 10.3 us -> 8.37 us
    pallas_call x1, Pallas kernels: 39.8 us -> 46.2 us  [half_gather(): pl.pallas_call(functools.partial(half_gather_kernel, chips, groups), out_...]
    unnamed x7 -> x0, other arithmetic: 5.21 us -> none
    another operation x12 -> x3, other arithmetic: 4.43 us -> 1.99 us
    ppermute x1, starting transfers between devices: 6.53 us -> 4.56 us  [body(): result = (mine + lax.ppermute(other, 'chan', pairs)).astype(jnp.bfloat16)]
    unnamed x18 -> x10, local copies, waits for them, and re-layouts: 6.24 us -> 4.88 us
  transfers between devices with their start and end apart: 2 -> 2, of which waited for: 1 -> 1; matrix products, arithmetic and copies ran while one was open for 11% -> 6% of each run, Pallas kernels for 26% -> 32%
where the time goes in v12:
time: 147 us; the launch traced here: 146 us
  Pallas kernels  111 us (76%)
  local copies, waits for them, and re-layouts  10.6 us (7%)
  matrix products  9.77 us (7%)
  starting transfers between devices  8.37 us (6%)
  other arithmetic  5.25 us (4%)
    pallas_call x1, Pallas kernels, chan_gather(): pl.pallas_call(functools.partial(gather_kernel, chips, groups), out_shape...  53.7 us
    pallas_call x1, Pallas kernels, half_gather(): pl.pallas_call(functools.partial(half_gather_kernel, chips, groups), out_...  46.2 us
    pallas_call x1, Pallas kernels, ctx_exchange(): pl.pallas_call(functools.partial(exchange_kernel, groups), out_shape=jax....  10.8 us
    unnamed x10, local copies, waits for them, and re-layouts  4.88 us
    ppermute x1, starting transfers between devices, body(): result = (mine + lax.ppermute(other, 'chan', pairs)).astype(jnp.bfloat16)  4.56 us
    dot_general x1, matrix products, body(): lax.dot_general(w_flat, inputs_t, (((0,), (0,)), ((), ())), preferred_ele...  3.97 us
    all_to_all x1, starting transfers between devices, body(): lax.all_to_all(w_late, 'chan', 1, 0, tiled=True, axis_index_groups=same_c...  3.81 us
  transfers between devices with their start and end apart: 2, of which 1 were waited for; matrix products, arithmetic and copies ran while one was open for 6% of the time, Pallas kernels for 32%

profile of v12, /device:TPU:1, one launch (start us, length us, event | category | flops | bytes accessed | tf_op | source)
XLA Modules:
  0.0 146.2 jit_solution(5194107036455785494)
XLA Ops:
  0.0 1.7 %copy.13 = bf16[512,128]{0,1:T(8,128)(2,1)} copy(bf16[512,128]{1,0:T(8,128)(2,1)} %param.6) | data formatting | bytes 262144 | tf_op args[0]
  1.7 1.7 %copy.14 = bf16[128,512]{1,0:T(8,128)(2,1)} copy(bf16[128,512]{0,1:T(8,128)(2,1)} %bitcast.97) | data formatting | bytes 262144 | tf_op jit(solution)/shard_map/input_gather_and_filter_to_owner/transpose | solution.py:335
  3.3 3.2 %copy.15 = bf16[4096,3,128]{0,2,1:T(8,128)(2,1)S(1)} copy(bf16[4096,3,128]{2,0,1:T(8,128)(2,1)} %param.7) | data formatting | bytes 6291456 | tf_op args[1]
  6.5 53.7 %input_gather_and_filter_to_owner.1 = (bf16[32,128,512]{2,1,0:T(8,128)(2,1)}, bf16[8,16,512]{2,1,0:T(8,128)(2,1)}) custom-call(bf16[128,512]{1,0:T(8,128)(2,1)} %bitcast.94, bf16[8,16,512]{2,1,0:T(8,128)(2,1)} %bitcast.95), custom_call_target="tpu_custom_call" | custom-call | tf_op jit(solution)/shard_map/input_gather_and_filter_to_owner/pallas_call | solution.py:183
  60.2 4.0 %convolution_convert_fusion.1 = bf16[512,384]{0,1:T(8,128)(2,1)S(1)} fusion(bf16[4096,384]{0,1:T(8,128)(2,1)S(1)} %bitcast.86, bf16[4096,512]{1,0:T(8,128)(2,1)} %bitcast.98), kind=kOutput, calls=%fused_computation.11 | convolution fusion | flops 1610809344 | bytes 7733248 | tf_op jit(solution)/shard_map/input_projection/dot_general | solution.py:340
  64.2 0.8 copy.28
  65.0 10.8 %projection_to_owner.1 = bf16[8,3,16,512]{3,2,1,0:T(8,128)(2,1)} custom-call(bf16[8,3,16,512]{3,2,1,0:T(8,128)(2,1)} %bitcast.93), custom_call_target="tpu_custom_call" | custom-call | tf_op jit(solution)/shard_map/projection_to_owner/pallas_call | solution.py:145
  75.8 0.0 copy-start
  75.8 1.7 %copy.20 = bf16[128,4096]{0,1:T(8,128)(2,1)S(1)} copy(bf16[128,4096]{1,0:T(8,128)(2,1)} %param.11) | data formatting | bytes 2097152 | tf_op jit(solution)/shard_map/out_weight_columns/optimization_barrier | solution.py:349
  77.5 0.0 copy-start.2
  77.5 1.3 copy.21
  78.8 3.8 %all-to-all-start = ((bf16[128,16,256]{2,0,1:T(8,128)(2,1)}), bf16[128,16,256]{2,0,1:T(8,128)(2,1)S(1)}, u32[]{:S(2)}, u32[]{:S(2)}) async-start(bf16[128,16,256]{2,0,1:T(8,128)(2,1)} %copy.21), calls=%async_computation | async-start | bytes 2097152 | tf_op jit(solution)/shard_map/out_weight_columns/all_to_all | solution.py:352
  82.7 0.5 fusion.41
  83.2 0.0 copy-done
  83.2 0.1 slice.210
  83.3 0.2 fusion.17
  83.6 0.6 fusion.44
  84.2 0.0 copy-done.2
  84.2 0.1 fusion.49
  84.3 0.4 add_convert_fusion
  84.6 1.5 %negate_convert_fusion = (bf16[32,32,1024]{2,1,0:T(8,128)(2,1)S(1)}, bf16[32,32,1024]{2,1,0:T(8,128)(2,1)S(1)}) fusion(f32[32,1024]{1,0:T(8,128)S(1)} %get-tuple-element.52, f32[32,1024]{1,0:T(8,128)S(1)} %get-tuple-element.51, f32[32,1024]{1,0:T(8,128)S(1)} %get-tuple-element.53, f32[32,1024]{1,0:T(8,128)S(1)} %get-tuple-element.50), kind=kLoop, calls=%fused_computation.5 | loop fusion | flops 9437184 | bytes 4718592 | tf_op jit(solution)/shard_map/convert.8
  86.1 0.0 copy-start.1
  86.1 0.8 convolution_convert_fusion
  87.0 0.1 slice_convert_fusion.2
  87.1 0.0 copy-done.1
  87.1 0.1 slice.172
  87.2 0.0 copy-start.3
  87.2 1.5 %fusion.3 = bf16[8,16,2048]{2,1,0:T(8,128)(2,1)S(1)} fusion(bf16[1024,1024]{1,0:T(8,128)(2,1)S(1)} %bitcast.88, bf16[1024,1024]{1,0:T(8,128)(2,1)S(1)} %bitcast.91, bf16[7,16,511]{2,1,0:T(8,128)(2,1)S(1)} %slice.172, bf16[8,16,512]{2,1,0:T(8,128)(2,1)S(1)} %copy-done.1, bf16[1024]{0:T(1024)(128)(2,1)S(1)} %pad.78.clone), kind=kOutput, calls=%fused_computation.7 | convolution fusion | flops 546570240 | bytes 4966176 | tf_op jit(solution)/shard_map/spectra/kdm,fm->kdf/dot_general | solution.py:381
  88.8 0.1 slice_convert_fusion.3
  88.9 0.0 copy-done.3
  88.9 0.1 dynamic_slice.13
  89.0 0.1 multiply_subtract_fusion.6
  89.1 0.1 multiply_subtract_fusion.3
  89.2 0.1 multiply_subtract_fusion.2
  89.3 0.1 multiply_subtract_fusion.1
  89.4 0.1 multiply_subtract_fusion
  89.6 0.3 add_convert_fusion.2
  89.8 0.3 add_convert_fusion.1
  90.1 1.1 fusion.10.t_ref
  91.2 46.2 %output_projection.1 = bf16[16,128,512]{2,1,0:T(8,128)(2,1)} custom-call(bf16[8,16,512]{2,1,0:T(8,128)(2,1)} %fusion.10.t_ref), custom_call_target="tpu_custom_call" | custom-call | tf_op jit(solution)/shard_map/output_projection/pallas_call | solution.py:289
  137.4 0.0 all-to-all-done
  137.4 2.3 %convolution_bitcast_fusion = f32[512,256]{1,0:T(8,128)S(1)} fusion(bf16[16,128,512]{2,1,0:T(8,128)(2,1)} %output_projection.1, bf16[128,16,256]{2,0,1:T(8,128)(2,1)S(1)} %all-to-all-done), kind=kOutput, calls=%fused_computation.12 | convolution fusion | flops 536870912 | bytes 3670016 | tf_op jit(solution)/shard_map/output_projection/dot_general | solution.py:411
  139.8 4.6 %collective-permute-start = (f32[512,128]{1,0:T(8,128)S(1)}, f32[512,128]{1,0:T(8,128)S(1)}, u32[]{:S(2)}, u32[]{:S(2)}) collective-permute-start(f32[512,128]{1,0:T(8,128)S(1)} %constant_dynamic-slice_fusion.2), channel_id=1, source_target_pairs={{0,1},{1,0},{2,3},{3,2},{4,5},{5,4},{6,7},{7,6},{8,9},{9,8},{10,11... | collective-permute-start | bytes 786440 | tf_op jit(solution)/shard_map/output_projection/ppermute | solution.py:418
  144.3 1.2 collective-permute-done
  145.5 0.7 add_convert_fusion.3
  (7 shorter events, 0.2 us)
Async XLA Ops:
  75.8 7.4 %copy-start = (bf16[8,3,16,512]{3,2,1,0:T(8,128)(2,1)S(1)}, bf16[8,3,16,512]{3,2,1,0:T(8,128)(2,1)}, u32[]{:S(2)}) copy-start(bf16[8,3,16,512]{3,2,1,0:T(8,128)(2,1)} %projection_to_owner.1) | copy-start | bytes 1179652
  77.5 6.7 %copy-start.2 = (bf16[3,3,128]{2,1,0:T(4,128)(2,1)S(1)}, bf16[3,3,128]{2,1,0:T(4,128)(2,1)}, u32[]{:S(2)}) copy-start(bf16[3,3,128]{2,1,0:T(4,128)(2,1)} %param.8) | copy-start | bytes 6916
  78.8 58.6 %all-to-all-start = ((bf16[128,16,256]{2,0,1:T(8,128)(2,1)}), bf16[128,16,256]{2,0,1:T(8,128)(2,1)S(1)}, u32[]{:S(2)}, u32[]{:S(2)}) async-start(bf16[128,16,256]{2,0,1:T(8,128)(2,1)} %copy.21), calls=%async_computation | async-start | bytes 2097152 | tf_op jit(solution)/shard_map/out_weight_columns/all_to_all | solution.py:352
  86.1 1.0 copy-start.1
  87.2 1.6 %copy-start.3 = (f32[128]{0:T(128)S(1)}, f32[128]{0:T(128)}, u32[]{:S(2)}) copy-start(f32[128]{0:T(128)} %param.9) | copy-start | bytes 1540
  139.8 5.7 %collective-permute-start = (f32[512,128]{1,0:T(8,128)S(1)}, f32[512,128]{1,0:T(8,128)S(1)}, u32[]{:S(2)}, u32[]{:S(2)}) collective-permute-start(f32[512,128]{1,0:T(8,128)S(1)} %constant_dynamic-slice_fusion.2), channel_id=1, source_target_pairs={{0,1},{1,0},{2,3},{3,2},{4,5},{5,4},{6,7},{7,6},{8,9},{9,8},{10,11... | collective-permute-start | bytes 786440 | tf_op jit(solution)/shard_map/output_projection/ppermute | solution.py:418

commit v13 on v12

--- a/solution.py
+++ b/solution.py
@@ -335,6 +335,12 @@
         taps_t = filter_taps.T.reshape(groups, own, span_len)
         inputs_t, taps_t = chan_gather(inputs.T, taps_t, 0)
 
+    with jax.named_scope("out_weight_columns"):
+        w_late, inputs_t = lax.optimization_barrier((w_out, inputs_t))
+        size = lax.axis_size("chan")
+        same_core = [list(range(c, size, 2)) for c in range(2)]
+        w_cols = lax.all_to_all(w_late, "chan", 1, 0, tiled=True, axis_index_groups=same_core)
+
     with jax.named_scope("input_projection"):
         w_flat = w_in.reshape(w_in.shape[0], 3 * width_dev)
         proj_t = lax.dot_general(
@@ -344,12 +350,6 @@
     with jax.named_scope("projection_to_owner"):
         proj_t = proj_t.reshape(3, groups, own, span_len).transpose(1, 0, 2, 3)
         proj_t = ctx_exchange(proj_t, 3)
-
-    with jax.named_scope("out_weight_columns"):
-        w_late, proj_t = lax.optimization_barrier((w_out, proj_t))
-        size = lax.axis_size("chan")
-        same_core = [list(range(c, size, 2)) for c in range(2)]
-        w_cols = lax.all_to_all(w_late, "chan", 1, 0, tiled=True, axis_index_groups=same_core)
 
     with jax.named_scope("short_conv"):
         start = position * own

time: 147 us -> 153 us (1.041)
  local copies, waits for them, and re-layouts: 10.6 us -> 13.1 us
  starting transfers between devices: 8.37 us -> 10.6 us
  other arithmetic: 5.25 us -> 7.27 us
  Pallas kernels: 111 us -> 109 us
    pallas_call x1, Pallas kernels: 46.2 us -> 39.5 us  [half_gather(): pl.pallas_call(functools.partial(half_gather_kernel, chips, groups), out_...]
    pallas_call x1, Pallas kernels: 10.8 us -> 16 us  [ctx_exchange(): pl.pallas_call(functools.partial(exchange_kernel, groups), out_shape=jax....]
    ppermute x1, starting transfers between devices: 4.56 us -> 6.79 us  [body(): result = (mine + lax.ppermute(other, 'chan', pairs)).astype(jnp.bfloat16)]
    unnamed x10 -> x9, local copies, waits for them, and re-layouts: 4.88 us -> 6.47 us
  transfers between devices with their start and end apart: 2 -> 2, of which waited for: 1 -> 1; matrix products, arithmetic and copies ran while one was open for 6% -> 14% of each run, Pallas kernels for 32% -> 36%
where the time goes in v13:
time: 153 us; the launch traced here: 152 us
  Pallas kernels  109 us (71%)
  local copies, waits for them, and re-layouts  13.1 us (9%)
  matrix products  10.7 us (7%)
  starting transfers between devices  10.6 us (7%)
  other arithmetic  7.27 us (5%)
    pallas_call x1, Pallas kernels, chan_gather(): pl.pallas_call(functools.partial(gather_kernel, chips, groups), out_shape...  53.5 us
    pallas_call x1, Pallas kernels, half_gather(): pl.pallas_call(functools.partial(half_gather_kernel, chips, groups), out_...  39.5 us
    pallas_call x1, Pallas kernels, ctx_exchange(): pl.pallas_call(functools.partial(exchange_kernel, groups), out_shape=jax....  16 us
    ppermute x1, starting transfers between devices, body(): result = (mine + lax.ppermute(other, 'chan', pairs)).astype(jnp.bfloat16)  6.79 us
    unnamed x9, local copies, waits for them, and re-layouts  6.47 us
    dot_general x1, matrix products, body(): lax.dot_general(w_flat, inputs_t, (((0,), (0,)), ((), ())), preferred_ele...  4.92 us
    all_to_all x1, starting transfers between devices, body(): lax.all_to_all(w_late, 'chan', 1, 0, tiled=True, axis_index_groups=same_c...  3.81 us
  transfers between devices with their start and end apart: 2, of which 1 were waited for; matrix products, arithmetic and copies ran while one was open for 14% of the time, Pallas kernels for 36%

profile of v13, /device:TPU:1, one launch (start us, length us, event | category | flops | bytes accessed | tf_op | source)
XLA Modules:
  0.0 152.2 jit_solution(3903589490847269281)
XLA Ops:
  0.0 1.7 %copy.13 = bf16[512,128]{0,1:T(8,128)(2,1)} copy(bf16[512,128]{1,0:T(8,128)(2,1)} %param.6) | data formatting | bytes 262144 | tf_op args[0]
  1.7 1.7 %copy.14 = bf16[128,512]{1,0:T(8,128)(2,1)} copy(bf16[128,512]{0,1:T(8,128)(2,1)} %bitcast.97) | data formatting | bytes 262144 | tf_op jit(solution)/shard_map/input_gather_and_filter_to_owner/transpose | solution.py:335
  3.3 53.5 %input_gather_and_filter_to_owner.1 = (bf16[32,128,512]{2,1,0:T(8,128)(2,1)}, bf16[8,16,512]{2,1,0:T(8,128)(2,1)}) custom-call(bf16[128,512]{1,0:T(8,128)(2,1)} %bitcast.94, bf16[8,16,512]{2,1,0:T(8,128)(2,1)} %bitcast.95), custom_call_target="tpu_custom_call" | custom-call | tf_op jit(solution)/shard_map/input_gather_and_filter_to_owner/pallas_call | solution.py:183
  56.9 1.6 %copy.20 = bf16[128,4096]{0,1:T(8,128)(2,1)S(1)} copy(bf16[128,4096]{1,0:T(8,128)(2,1)} %param.11) | data formatting | bytes 2097152 | tf_op jit(solution)/shard_map/out_weight_columns/optimization_barrier | solution.py:339
  58.5 1.4 copy.21
  59.8 3.8 %all-to-all-start = ((bf16[128,16,256]{2,0,1:T(8,128)(2,1)}), bf16[128,16,256]{2,0,1:T(8,128)(2,1)S(1)}, u32[]{:S(2)}, u32[]{:S(2)}) async-start(bf16[128,16,256]{2,0,1:T(8,128)(2,1)} %copy.21), calls=%async_computation | async-start | bytes 2097152 | tf_op jit(solution)/shard_map/out_weight_columns/all_to_all | solution.py:342
  63.7 0.5 fusion.41
  64.2 4.8 %copy.15 = bf16[4096,3,128]{0,2,1:T(8,128)(2,1)} copy(bf16[4096,3,128]{2,0,1:T(8,128)(2,1)} %param.7) | data formatting | bytes 6291456 | tf_op args[1]
  69.0 4.9 %convolution_convert_fusion.1 = bf16[512,384]{0,1:T(8,128)(2,1)S(1)} fusion(bf16[4096,384]{0,1:T(8,128)(2,1)} %bitcast.86, bf16[4096,512]{1,0:T(8,128)(2,1)} %bitcast.98), kind=kOutput, calls=%fused_computation.11 | convolution fusion | flops 1610809344 | bytes 7733248 | tf_op jit(solution)/shard_map/input_projection/dot_general | solution.py:346
  73.9 0.0 copy-start.1
  73.9 0.8 copy.28
  74.7 16.0 %projection_to_owner.1 = bf16[8,3,16,512]{3,2,1,0:T(8,128)(2,1)} custom-call(bf16[8,3,16,512]{3,2,1,0:T(8,128)(2,1)} %bitcast.93), custom_call_target="tpu_custom_call" | custom-call | tf_op jit(solution)/shard_map/projection_to_owner/pallas_call | solution.py:145
  90.7 1.0 slice.210
  91.7 1.2 fusion.17
  93.0 0.6 fusion.44
  93.6 0.0 copy-done.1
  93.6 0.1 fusion.49
  93.7 1.4 add_convert_fusion
  95.1 1.5 negate_convert_fusion
  96.6 0.0 copy-start
  96.6 0.8 convolution_convert_fusion
  97.4 0.1 slice_convert_fusion.2
  97.5 0.0 copy-done
  97.6 0.1 slice.172
  97.7 0.0 copy-start.2
  97.7 1.5 fusion.3
  99.2 0.1 slice_convert_fusion.3
  99.3 0.0 copy-done.2
  99.3 0.1 dynamic_slice.13
  99.4 0.1 multiply_subtract_fusion.6
  99.4 0.1 multiply_subtract_fusion.4
  99.6 0.1 multiply_subtract_fusion.3
  99.6 0.1 multiply_subtract_fusion.2
  99.7 0.1 multiply_subtract_fusion.1
  99.9 0.1 multiply_subtract_fusion
  100.0 0.3 add_convert_fusion.2
  100.3 0.2 add_convert_fusion.1
  100.5 1.1 fusion.10.t_ref
  101.7 39.5 %output_projection.1 = bf16[16,128,512]{2,1,0:T(8,128)(2,1)} custom-call(bf16[8,16,512]{2,1,0:T(8,128)(2,1)} %fusion.10.t_ref), custom_call_target="tpu_custom_call" | custom-call | tf_op jit(solution)/shard_map/output_projection/pallas_call | solution.py:289
  141.2 0.0 all-to-all-done
  141.2 2.3 %convolution_bitcast_fusion = f32[512,256]{1,0:T(8,128)S(1)} fusion(bf16[16,128,512]{2,1,0:T(8,128)(2,1)} %output_projection.1, bf16[128,16,256]{2,0,1:T(8,128)(2,1)S(1)} %all-to-all-done), kind=kOutput, calls=%fused_computation.12 | convolution fusion | flops 536870912 | bytes 3670016 | tf_op jit(solution)/shard_map/output_projection/dot_general | solution.py:411
  143.6 6.8 %collective-permute-start = (f32[512,128]{1,0:T(8,128)S(1)}, f32[512,128]{1,0:T(8,128)S(1)}, u32[]{:S(2)}, u32[]{:S(2)}) collective-permute-start(f32[512,128]{1,0:T(8,128)S(1)} %constant_dynamic-slice_fusion.2), channel_id=1, source_target_pairs={{0,1},{1,0},{2,3},{3,2},{4,5},{5,4},{6,7},{7,6},{8,9},{9,8},{10,11... | collective-permute-start | bytes 786440 | tf_op jit(solution)/shard_map/output_projection/ppermute | solution.py:418
  150.4 1.2 collective-permute-done
  151.5 0.7 add_convert_fusion.3
  (6 shorter events, 0.1 us)
Async XLA Ops:
  59.8 81.3 %all-to-all-start = ((bf16[128,16,256]{2,0,1:T(8,128)(2,1)}), bf16[128,16,256]{2,0,1:T(8,128)(2,1)S(1)}, u32[]{:S(2)}, u32[]{:S(2)}) async-start(bf16[128,16,256]{2,0,1:T(8,128)(2,1)} %copy.21), calls=%async_computation | async-start | bytes 2097152 | tf_op jit(solution)/shard_map/out_weight_columns/all_to_all | solution.py:342
  73.9 19.6 %copy-start.1 = (bf16[3,3,128]{2,1,0:T(4,128)(2,1)S(1)}, bf16[3,3,128]{2,1,0:T(4,128)(2,1)}, u32[]{:S(2)}) copy-start(bf16[3,3,128]{2,1,0:T(4,128)(2,1)} %param.8) | copy-start | bytes 6916
  96.6 1.0 copy-start
  97.7 1.6 %copy-start.2 = (f32[128]{0:T(128)S(1)}, f32[128]{0:T(128)}, u32[]{:S(2)}) copy-start(f32[128]{0:T(128)} %param.9) | copy-start | bytes 1540
  143.6 8.0 %collective-permute-start = (f32[512,128]{1,0:T(8,128)S(1)}, f32[512,128]{1,0:T(8,128)S(1)}, u32[]{:S(2)}, u32[]{:S(2)}) collective-permute-start(f32[512,128]{1,0:T(8,128)S(1)} %constant_dynamic-slice_fusion.2), channel_id=1, source_target_pairs={{0,1},{1,0},{2,3},{3,2},{4,5},{5,4},{6,7},{7,6},{8,9},{9,8},{10,11... | collective-permute-start | bytes 786440 | tf_op jit(solution)/shard_map/output_projection/ppermute | solution.py:418

commit v14 on v12

--- a/solution.py
+++ b/solution.py
@@ -48,12 +48,17 @@
         for copy in t_sends:
             copy.start()
 
-    local = pltpu.make_async_copy(x_ref, out_ref.at[me], local_sem)
+    width = x_ref.shape[1]
+
+    def cols(first, count):
+        return out_ref.at[:, pl.ds(pl.multiple_of(first * width, width), count * width)]
+
+    local = pltpu.make_async_copy(x_ref, cols(me, 1), local_sem)
     local.start()
 
     def cross(k, peer, slot):
         return pltpu.make_async_remote_copy(
-            src_ref=x_ref, dst_ref=out_ref.at[slot], send_sem=cross_send.at[k],
+            src_ref=x_ref, dst_ref=cols(slot, 1), send_sem=cross_send.at[k],
             recv_sem=cross_recv.at[k], device_id=(row, peer), device_id_type=MESH)
 
     for k, peer in enumerate(partners):
@@ -67,9 +72,8 @@
 
     def part(chip, s, half):
         if s < last:
-            return out_ref.at[pl.ds(pl.multiple_of(chip * PER_Z, PER_Z), PER_Z)]
-        start = pl.multiple_of(chip * PER_Z + half * (PER_Z // 2), PER_Z // 2)
-        return out_ref.at[pl.ds(start, PER_Z // 2)]
+            return cols(chip * PER_Z, PER_Z)
+        return cols(chip * PER_Z + half * (PER_Z // 2), PER_Z // 2)
 
     def ring(s, chip):
         return pltpu.make_async_remote_copy(
@@ -163,7 +167,7 @@
     longest = chips // 2
     assert chips % 2 == 0
     operands = (x,) if t is None else (x, t)
-    out_shape = [jax.ShapeDtypeStruct((size,) + x.shape, x.dtype)]
+    out_shape = [jax.ShapeDtypeStruct((x.shape[0], size * x.shape[1]), x.dtype)]
     scratch = [
         pltpu.SemaphoreType.DMA(()),
         pltpu.SemaphoreType.DMA((3,)),
@@ -188,7 +192,7 @@
         scratch_shapes=scratch,
         compiler_params=pltpu.CompilerParams(collective_id=collective_id, has_side_effects=True),
     )(*operands)
-    gathered = outs[0].reshape(size * x.shape[0], x.shape[1])
+    gathered = outs[0]
     return gathered if t is None else (gathered, outs[1])
 
 
@@ -309,6 +313,31 @@
     return out.reshape(size // 2 * block[0], block[1])
 
 
+def matmul_kernel(depth, x_ref, w_ref, out_ref):
+    for stream in range(w_ref.shape[0]):
+        def step(k, acc):
+            rows = pl.ds(pl.multiple_of(k * depth, depth), depth)
+            return acc + jnp.dot(x_ref[:, rows], w_ref[stream, rows, :],
+                                 preferred_element_type=jnp.float32)
+
+        total = lax.fori_loop(0, x_ref.shape[1] // depth, step,
+                              jnp.zeros(out_ref.shape[1:], jnp.float32))
+        out_ref[stream] = total.astype(out_ref.dtype)
+
+
+def project(x, w):
+    depth = 512
+    return pl.pallas_call(
+        functools.partial(matmul_kernel, depth),
+        out_shape=jax.ShapeDtypeStruct((w.shape[0], x.shape[0], w.shape[2]), jnp.bfloat16),
+        in_specs=[pl.BlockSpec(memory_space=pltpu.VMEM)] * 2,
+        out_specs=pl.BlockSpec(memory_space=pltpu.VMEM),
+        cost_estimate=pl.CostEstimate(
+            flops=2 * x.shape[0] * x.shape[1] * w.shape[0] * w.shape[2], transcendentals=0,
+            bytes_accessed=2 * (x.size + w.size + x.shape[0] * w.shape[0] * w.shape[2])),
+    )(x, w)
+
+
 def dft_table(double_len):
     step = 32
     hi_ids = jnp.arange(double_len // step, dtype=jnp.int32)[:, None]
@@ -333,16 +362,13 @@
 
     with jax.named_scope("input_gather_and_filter_to_owner"):
         taps_t = filter_taps.T.reshape(groups, own, span_len)
-        inputs_t, taps_t = chan_gather(inputs.T, taps_t, 0)
+        inputs_all, taps_t = chan_gather(inputs, taps_t, 0)
 
     with jax.named_scope("input_projection"):
-        w_flat = w_in.reshape(w_in.shape[0], 3 * width_dev)
-        proj_t = lax.dot_general(
-            w_flat, inputs_t, (((0,), (0,)), ((), ())), preferred_element_type=jnp.float32
-        ).astype(jnp.bfloat16)
+        projected = project(inputs_all, jnp.transpose(w_in, (1, 0, 2)))
 
     with jax.named_scope("projection_to_owner"):
-        proj_t = proj_t.reshape(3, groups, own, span_len).transpose(1, 0, 2, 3)
+        proj_t = projected.reshape(3, span_len, groups, own).transpose(2, 0, 3, 1)
         proj_t = ctx_exchange(proj_t, 3)
 
     with jax.named_scope("out_weight_columns"):

time: 147 us -> 149 us (1.014)
  Pallas kernels: 111 us -> 122 us
  local copies, waits for them, and re-layouts: 10.6 us -> 5.96 us
  matrix products: 9.77 us -> 5.8 us
    pallas_call x0 -> x1, Pallas kernels: none -> 11.3 us  [project(): pl.pallas_call(functools.partial(matmul_kernel, depth), out_shape=jax.Sha...]
    unnamed x10, local copies, waits for them, and re-layouts: 4.88 us -> 0.03 us
    dot_general x1 -> x0, matrix products: 3.97 us -> none  [body(): lax.dot_general(w_flat, inputs_t, (((0,), (0,)), ((), ())), preferred_ele...]
  transfers between devices with their start and end apart: 2 -> 2, of which waited for: 1 -> 1; matrix products, arithmetic and copies ran while one was open for 6% -> 6% of each run, Pallas kernels for 32% -> 31%
where the time goes in v14:
time: 149 us
  Pallas kernels  122 us (82%)
  starting transfers between devices  8.36 us (6%)
  local copies, waits for them, and re-layouts  5.96 us (4%)
  matrix products  5.8 us (4%)
  other arithmetic  5.25 us (4%)
    pallas_call x1, Pallas kernels, chan_gather(): pl.pallas_call(functools.partial(gather_kernel, chips, groups), out_shape...  53.5 us
    pallas_call x1, Pallas kernels, half_gather(): pl.pallas_call(functools.partial(half_gather_kernel, chips, groups), out_...  46.2 us
    pallas_call x1, Pallas kernels, project(): pl.pallas_call(functools.partial(matmul_kernel, depth), out_shape=jax.Sha...  11.3 us
    pallas_call x1, Pallas kernels, ctx_exchange(): pl.pallas_call(functools.partial(exchange_kernel, groups), out_shape=jax....  10.8 us
    ppermute x1, starting transfers between devices, body(): result = (mine + lax.ppermute(other, 'chan', pairs)).astype(jnp.bfloat16)  4.54 us
    all_to_all x1, starting transfers between devices, body(): lax.all_to_all(w_late, 'chan', 1, 0, tiled=True, axis_index_groups=same_c...  3.83 us
  transfers between devices with their start and end apart: 2, of which 1 were waited for; matrix products, arithmetic and copies ran while one was open for 6% of the time, Pallas kernels for 31%

profile of v14, /device:TPU:1, one launch (start us, length us, event | category | flops | bytes accessed | tf_op | source)
XLA Modules:
  0.0 148.7 jit_solution(14469184937939312425)
XLA Ops:
  0.0 1.7 %copy.12 = bf16[128,512]{1,0:T(8,128)(2,1)} copy(bf16[128,512]{0,1:T(8,128)(2,1)} %bitcast.90) | data formatting | bytes 262144 | tf_op jit(solution)/shard_map/input_gather_and_filter_to_owner/transpose | solution.py:364
  1.7 53.5 %input_gather_and_filter_to_owner.1 = (bf16[512,4096]{1,0:T(8,128)(2,1)}, bf16[8,16,512]{2,1,0:T(8,128)(2,1)}) custom-call(bf16[512,128]{1,0:T(8,128)(2,1)} %refs_0_.1, bf16[8,16,512]{2,1,0:T(8,128)(2,1)} %bitcast.89), custom_call_target="tpu_custom_call" | custom-call | tf_op jit(solution)/shard_map/input_gather_and_filter_to_owner/pallas_call | solution.py:187
  55.2 0.0 copy-start.1
  55.2 11.3 %input_projection.1 = bf16[3,512,128]{2,1,0:T(8,128)(2,1)} custom-call(bf16[512,4096]{1,0:T(8,128)(2,1)} %get-tuple-element.9.x_ref, bf16[3,4096,128]{2,1,0:T(8,128)(2,1)} %bitcast.80), custom_call_target="tpu_custom_call" | custom-call | flops 1610612736 | bytes 7733248 | tf_op jit(solution)/shard_map/input_projection/pallas_call | solution.py:330
  66.5 1.2 copy.13
  67.7 0.8 copy.26
  68.5 10.8 %projection_to_owner.1 = bf16[8,3,16,512]{3,2,1,0:T(8,128)(2,1)} custom-call(bf16[8,3,16,512]{3,2,1,0:T(8,128)(2,1)} %bitcast.88), custom_call_target="tpu_custom_call" | custom-call | tf_op jit(solution)/shard_map/projection_to_owner/pallas_call | solution.py:149
  79.3 0.0 copy-done.1
  79.3 0.0 copy-start
  79.3 0.0 copy-start.3
  79.4 0.7 copy.18
  80.0 1.3 copy.19
  81.3 3.8 %all-to-all-start = ((bf16[128,16,256]{2,0,1:T(8,128)(2,1)}), bf16[128,16,256]{2,0,1:T(8,128)(2,1)S(1)}, u32[]{:S(2)}, u32[]{:S(2)}) async-start(bf16[128,16,256]{2,0,1:T(8,128)(2,1)} %copy.19), calls=%async_computation | async-start | bytes 2097152 | tf_op jit(solution)/shard_map/out_weight_columns/all_to_all | solution.py:378
  85.2 0.5 fusion.41
  85.7 0.0 copy-done
  85.8 0.1 slice.210
  85.9 0.2 fusion.17
  86.1 0.6 fusion.44
  86.7 0.0 copy-done.3
  86.7 0.1 fusion.49
  86.8 0.4 add_convert_fusion
  87.2 1.5 negate_convert_fusion
  88.7 0.0 copy-start.2
  88.7 0.8 convolution_convert_fusion
  89.5 0.1 slice_convert_fusion.2
  89.6 0.0 copy-done.2
  89.6 0.1 slice.172
  89.8 0.0 copy-start.4
  89.8 1.5 %fusion.3 = bf16[8,16,2048]{2,1,0:T(8,128)(2,1)S(1)} fusion(bf16[1024,1024]{1,0:T(8,128)(2,1)S(1)} %bitcast.82, bf16[1024,1024]{1,0:T(8,128)(2,1)S(1)} %bitcast.85, bf16[7,16,511]{2,1,0:T(8,128)(2,1)S(1)} %slice.172, bf16[8,16,512]{2,1,0:T(8,128)(2,1)S(1)} %copy-done.2, bf16[1024]{0:T(1024)(128)(2,1)S(1)} %pad.78.clone), kind=kOutput, calls=%fused_computation.7 | convolution fusion | flops 546570240 | bytes 4966176 | tf_op jit(solution)/shard_map/spectra/kdm,fm->kdf/dot_general | solution.py:407
  91.3 0.1 slice_convert_fusion.3
  91.4 0.0 copy-done.4
  91.4 0.1 dynamic_slice.13
  91.5 0.1 multiply_subtract_fusion.6
  91.7 0.1 multiply_subtract_fusion.3
  91.8 0.1 multiply_subtract_fusion.2
  91.9 0.1 multiply_subtract_fusion.1
  92.0 0.1 multiply_subtract_fusion
  92.1 0.3 add_convert_fusion.2
  92.4 0.3 add_convert_fusion.1
  92.6 1.1 fusion.10.t_ref
  93.7 46.2 %output_projection.1 = bf16[16,128,512]{2,1,0:T(8,128)(2,1)} custom-call(bf16[8,16,512]{2,1,0:T(8,128)(2,1)} %fusion.10.t_ref), custom_call_target="tpu_custom_call" | custom-call | tf_op jit(solution)/shard_map/output_projection/pallas_call | solution.py:293
  140.0 0.0 all-to-all-done
  140.0 2.3 %convolution_bitcast_fusion = f32[512,256]{1,0:T(8,128)S(1)} fusion(bf16[16,128,512]{2,1,0:T(8,128)(2,1)} %output_projection.1, bf16[128,16,256]{2,0,1:T(8,128)(2,1)S(1)} %all-to-all-done), kind=kOutput, calls=%fused_computation.11 | convolution fusion | flops 536870912 | bytes 3670016 | tf_op jit(solution)/shard_map/output_projection/dot_general | solution.py:437
  142.3 4.5 %collective-permute-start = (f32[512,128]{1,0:T(8,128)S(1)}, f32[512,128]{1,0:T(8,128)S(1)}, u32[]{:S(2)}, u32[]{:S(2)}) collective-permute-start(f32[512,128]{1,0:T(8,128)S(1)} %constant_dynamic-slice_fusion.2), channel_id=1, source_target_pairs={{0,1},{1,0},{2,3},{3,2},{4,5},{5,4},{6,7},{7,6},{8,9},{9,8},{10,11... | collective-permute-start | bytes 786440 | tf_op jit(solution)/shard_map/output_projection/ppermute | solution.py:444
  146.9 1.2 collective-permute-done
  148.0 0.7 add_convert_fusion.3
  (7 shorter events, 0.2 us)
Async XLA Ops:
  55.2 24.1 %copy-start.1 = (bf16[128,4096]{1,0:T(8,128)(2,1)S(1)}, bf16[128,4096]{1,0:T(8,128)(2,1)}, u32[]{:S(2)}) copy-start(bf16[128,4096]{1,0:T(8,128)(2,1)} %param.11) | copy-start | bytes 3145732
  79.3 6.4 %copy-start = (bf16[8,3,16,512]{3,2,1,0:T(8,128)(2,1)S(1)}, bf16[8,3,16,512]{3,2,1,0:T(8,128)(2,1)}, u32[]{:S(2)}) copy-start(bf16[8,3,16,512]{3,2,1,0:T(8,128)(2,1)} %projection_to_owner.1) | copy-start | bytes 1179652
  79.3 7.4 %copy-start.3 = (bf16[3,3,128]{2,1,0:T(4,128)(2,1)S(1)}, bf16[3,3,128]{2,1,0:T(4,128)(2,1)}, u32[]{:S(2)}) copy-start(bf16[3,3,128]{2,1,0:T(4,128)(2,1)} %param.8) | copy-start | bytes 6916
  81.3 58.6 %all-to-all-start = ((bf16[128,16,256]{2,0,1:T(8,128)(2,1)}), bf16[128,16,256]{2,0,1:T(8,128)(2,1)S(1)}, u32[]{:S(2)}, u32[]{:S(2)}) async-start(bf16[128,16,256]{2,0,1:T(8,128)(2,1)} %copy.19), calls=%async_computation | async-start | bytes 2097152 | tf_op jit(solution)/shard_map/out_weight_columns/all_to_all | solution.py:378
  88.7 1.0 copy-start.2
  89.8 1.6 %copy-start.4 = (f32[128]{0:T(128)S(1)}, f32[128]{0:T(128)}, u32[]{:S(2)}) copy-start(f32[128]{0:T(128)} %param.9) | copy-start | bytes 1540
  142.3 5.7 %collective-permute-start = (f32[512,128]{1,0:T(8,128)S(1)}, f32[512,128]{1,0:T(8,128)S(1)}, u32[]{:S(2)}, u32[]{:S(2)}) collective-permute-start(f32[512,128]{1,0:T(8,128)S(1)} %constant_dynamic-slice_fusion.2), channel_id=1, source_target_pairs={{0,1},{1,0},{2,3},{3,2},{4,5},{5,4},{6,7},{7,6},{8,9},{9,8},{10,11... | collective-permute-start | bytes 786440 | tf_op jit(solution)/shard_map/output_projection/ppermute | solution.py:444

commit v15 on v14

--- a/solution.py
+++ b/solution.py
@@ -315,14 +315,9 @@
 
 def matmul_kernel(depth, x_ref, w_ref, out_ref):
     for stream in range(w_ref.shape[0]):
-        def step(k, acc):
-            rows = pl.ds(pl.multiple_of(k * depth, depth), depth)
-            return acc + jnp.dot(x_ref[:, rows], w_ref[stream, rows, :],
-                                 preferred_element_type=jnp.float32)
-
-        total = lax.fori_loop(0, x_ref.shape[1] // depth, step,
-                              jnp.zeros(out_ref.shape[1:], jnp.float32))
-        out_ref[stream] = total.astype(out_ref.dtype)
+        out_ref[stream] = jnp.dot(
+            x_ref[...], w_ref[stream], preferred_element_type=jnp.float32
+        ).astype(out_ref.dtype)
 
 
 def project(x, w):

time: 149 us -> 145 us (0.973)
  Pallas kernels: 122 us -> 118 us
    pallas_call x1, Pallas kernels: 11.3 us -> 7.4 us  [project(): pl.pallas_call(functools.partial(matmul_kernel, depth), out_shape=jax.Sha...]
  transfers between devices with their start and end apart: 2 -> 2, of which waited for: 1 -> 1; matrix products, arithmetic and copies ran while one was open for 6% -> 6% of each run, Pallas kernels for 31% -> 32%
where the time goes in v15:
time: 145 us
  Pallas kernels  118 us (81%)
  starting transfers between devices  8.37 us (6%)
  local copies, waits for them, and re-layouts  5.96 us (4%)
  matrix products  5.81 us (4%)
  other arithmetic  5.25 us (4%)
    pallas_call x1, Pallas kernels, chan_gather(): pl.pallas_call(functools.partial(gather_kernel, chips, groups), out_shape...  53.5 us
    pallas_call x1, Pallas kernels, half_gather(): pl.pallas_call(functools.partial(half_gather_kernel, chips, groups), out_...  46.2 us
    pallas_call x1, Pallas kernels, ctx_exchange(): pl.pallas_call(functools.partial(exchange_kernel, groups), out_shape=jax....  10.8 us
    pallas_call x1, Pallas kernels, project(): pl.pallas_call(functools.partial(matmul_kernel, depth), out_shape=jax.Sha...  7.4 us
    ppermute x1, starting transfers between devices, body(): result = (mine + lax.ppermute(other, 'chan', pairs)).astype(jnp.bfloat16)  4.54 us
    all_to_all x1, starting transfers between devices, body(): lax.all_to_all(w_late, 'chan', 1, 0, tiled=True, axis_index_groups=same_c...  3.82 us
  transfers between devices with their start and end apart: 2, of which 1 were waited for; matrix products, arithmetic and copies ran while one was open for 6% of the time, Pallas kernels for 32%

profile of v15, /device:TPU:1, one launch (start us, length us, event | category | flops | bytes accessed | tf_op | source)
XLA Modules:
  0.0 144.8 jit_solution(10606020901949811727)
XLA Ops:
  0.0 1.7 %copy.12 = bf16[128,512]{1,0:T(8,128)(2,1)} copy(bf16[128,512]{0,1:T(8,128)(2,1)} %bitcast.90) | data formatting | bytes 262144 | tf_op jit(solution)/shard_map/input_gather_and_filter_to_owner/transpose | solution.py:359
  1.7 53.5 %input_gather_and_filter_to_owner.1 = (bf16[512,4096]{1,0:T(8,128)(2,1)}, bf16[8,16,512]{2,1,0:T(8,128)(2,1)}) custom-call(bf16[512,128]{1,0:T(8,128)(2,1)} %refs_0_.1, bf16[8,16,512]{2,1,0:T(8,128)(2,1)} %bitcast.89), custom_call_target="tpu_custom_call" | custom-call | tf_op jit(solution)/shard_map/input_gather_and_filter_to_owner/pallas_call | solution.py:187
  55.2 0.0 copy-start.1
  55.2 7.4 %input_projection.1 = bf16[3,512,128]{2,1,0:T(8,128)(2,1)} custom-call(bf16[512,4096]{1,0:T(8,128)(2,1)} %get-tuple-element.9.x_ref, bf16[3,4096,128]{2,1,0:T(8,128)(2,1)} %bitcast.80), custom_call_target="tpu_custom_call" | custom-call | flops 1610612736 | bytes 7733248 | tf_op jit(solution)/shard_map/input_projection/pallas_call | solution.py:325
  62.6 1.2 copy.13
  63.8 0.8 copy.26
  64.5 10.8 %projection_to_owner.1 = bf16[8,3,16,512]{3,2,1,0:T(8,128)(2,1)} custom-call(bf16[8,3,16,512]{3,2,1,0:T(8,128)(2,1)} %bitcast.88), custom_call_target="tpu_custom_call" | custom-call | tf_op jit(solution)/shard_map/projection_to_owner/pallas_call | solution.py:149
  75.4 0.0 copy-done.1
  75.4 0.0 copy-start
  75.4 0.0 copy-start.3
  75.4 0.7 copy.18
  76.1 1.3 copy.19
  77.4 3.8 %all-to-all-start = ((bf16[128,16,256]{2,0,1:T(8,128)(2,1)}), bf16[128,16,256]{2,0,1:T(8,128)(2,1)S(1)}, u32[]{:S(2)}, u32[]{:S(2)}) async-start(bf16[128,16,256]{2,0,1:T(8,128)(2,1)} %copy.19), calls=%async_computation | async-start | bytes 2097152 | tf_op jit(solution)/shard_map/out_weight_columns/all_to_all | solution.py:373
  81.3 0.5 fusion.41
  81.8 0.0 copy-done
  81.8 0.1 slice.210
  81.9 0.2 fusion.17
  82.2 0.6 fusion.44
  82.8 0.0 copy-done.3
  82.8 0.1 fusion.49
  82.9 0.4 add_convert_fusion
  83.3 1.5 %negate_convert_fusion = (bf16[32,32,1024]{2,1,0:T(8,128)(2,1)S(1)}, bf16[32,32,1024]{2,1,0:T(8,128)(2,1)S(1)}) fusion(f32[32,1024]{1,0:T(8,128)S(1)} %get-tuple-element.52, f32[32,1024]{1,0:T(8,128)S(1)} %get-tuple-element.51, f32[32,1024]{1,0:T(8,128)S(1)} %get-tuple-element.53, f32[32,1024]{1,0:T(8,128)S(1)} %get-tuple-element.50), kind=kLoop, calls=%fused_computation.5 | loop fusion | flops 9437184 | bytes 4718592 | tf_op jit(solution)/shard_map/convert.8
  84.7 0.0 copy-start.2
  84.8 0.8 convolution_convert_fusion
  85.6 0.1 slice_convert_fusion.2
  85.7 0.0 copy-done.2
  85.7 0.1 slice.172
  85.8 0.0 copy-start.4
  85.9 1.5 %fusion.3 = bf16[8,16,2048]{2,1,0:T(8,128)(2,1)S(1)} fusion(bf16[1024,1024]{1,0:T(8,128)(2,1)S(1)} %bitcast.82, bf16[1024,1024]{1,0:T(8,128)(2,1)S(1)} %bitcast.85, bf16[7,16,511]{2,1,0:T(8,128)(2,1)S(1)} %slice.172, bf16[8,16,512]{2,1,0:T(8,128)(2,1)S(1)} %copy-done.2, bf16[1024]{0:T(1024)(128)(2,1)S(1)} %pad.78.clone), kind=kOutput, calls=%fused_computation.7 | convolution fusion | flops 546570240 | bytes 4966176 | tf_op jit(solution)/shard_map/spectra/kdm,fm->kdf/dot_general | solution.py:402
  87.4 0.1 slice_convert_fusion.3
  87.5 0.0 copy-done.4
  87.5 0.1 dynamic_slice.13
  87.6 0.1 multiply_subtract_fusion.6
  87.8 0.1 multiply_subtract_fusion.3
  87.8 0.1 multiply_subtract_fusion.2
  87.9 0.1 multiply_subtract_fusion.1
  88.0 0.1 multiply_subtract_fusion
  88.2 0.3 add_convert_fusion.2
  88.4 0.3 add_convert_fusion.1
  88.7 1.1 fusion.10.t_ref
  89.8 46.2 %output_projection.1 = bf16[16,128,512]{2,1,0:T(8,128)(2,1)} custom-call(bf16[8,16,512]{2,1,0:T(8,128)(2,1)} %fusion.10.t_ref), custom_call_target="tpu_custom_call" | custom-call | tf_op jit(solution)/shard_map/output_projection/pallas_call | solution.py:293
  136.0 0.0 all-to-all-done
  136.0 2.3 %convolution_bitcast_fusion = f32[512,256]{1,0:T(8,128)S(1)} fusion(bf16[16,128,512]{2,1,0:T(8,128)(2,1)} %output_projection.1, bf16[128,16,256]{2,0,1:T(8,128)(2,1)S(1)} %all-to-all-done), kind=kOutput, calls=%fused_computation.11 | convolution fusion | flops 536870912 | bytes 3670016 | tf_op jit(solution)/shard_map/output_projection/dot_general | solution.py:432
  138.4 4.5 %collective-permute-start = (f32[512,128]{1,0:T(8,128)S(1)}, f32[512,128]{1,0:T(8,128)S(1)}, u32[]{:S(2)}, u32[]{:S(2)}) collective-permute-start(f32[512,128]{1,0:T(8,128)S(1)} %constant_dynamic-slice_fusion.2), channel_id=1, source_target_pairs={{0,1},{1,0},{2,3},{3,2},{4,5},{5,4},{6,7},{7,6},{8,9},{9,8},{10,11... | collective-permute-start | bytes 786440 | tf_op jit(solution)/shard_map/output_projection/ppermute | solution.py:439
  143.0 1.2 collective-permute-done
  144.1 0.7 add_convert_fusion.3
  (7 shorter events, 0.2 us)
Async XLA Ops:
  55.2 20.2 %copy-start.1 = (bf16[128,4096]{1,0:T(8,128)(2,1)S(1)}, bf16[128,4096]{1,0:T(8,128)(2,1)}, u32[]{:S(2)}) copy-start(bf16[128,4096]{1,0:T(8,128)(2,1)} %param.11) | copy-start | bytes 3145732
  75.4 6.4 %copy-start = (bf16[8,3,16,512]{3,2,1,0:T(8,128)(2,1)S(1)}, bf16[8,3,16,512]{3,2,1,0:T(8,128)(2,1)}, u32[]{:S(2)}) copy-start(bf16[8,3,16,512]{3,2,1,0:T(8,128)(2,1)} %projection_to_owner.1) | copy-start | bytes 1179652
  75.4 7.4 %copy-start.3 = (bf16[3,3,128]{2,1,0:T(4,128)(2,1)S(1)}, bf16[3,3,128]{2,1,0:T(4,128)(2,1)}, u32[]{:S(2)}) copy-start(bf16[3,3,128]{2,1,0:T(4,128)(2,1)} %param.8) | copy-start | bytes 6916
  77.4 58.6 %all-to-all-start = ((bf16[128,16,256]{2,0,1:T(8,128)(2,1)}), bf16[128,16,256]{2,0,1:T(8,128)(2,1)S(1)}, u32[]{:S(2)}, u32[]{:S(2)}) async-start(bf16[128,16,256]{2,0,1:T(8,128)(2,1)} %copy.19), calls=%async_computation | async-start | bytes 2097152 | tf_op jit(solution)/shard_map/out_weight_columns/all_to_all | solution.py:373
  84.7 1.0 copy-start.2
  85.8 1.6 %copy-start.4 = (f32[128]{0:T(128)S(1)}, f32[128]{0:T(128)}, u32[]{:S(2)}) copy-start(f32[128]{0:T(128)} %param.9) | copy-start | bytes 1540
  138.4 5.7 %collective-permute-start = (f32[512,128]{1,0:T(8,128)S(1)}, f32[512,128]{1,0:T(8,128)S(1)}, u32[]{:S(2)}, u32[]{:S(2)}) collective-permute-start(f32[512,128]{1,0:T(8,128)S(1)} %constant_dynamic-slice_fusion.2), channel_id=1, source_target_pairs={{0,1},{1,0},{2,3},{3,2},{4,5},{5,4},{6,7},{7,6},{8,9},{9,8},{10,11... | collective-permute-start | bytes 786440 | tf_op jit(solution)/shard_map/output_projection/ppermute | solution.py:439

commit v16 on v15

--- a/solution.py
+++ b/solution.py
@@ -314,10 +314,11 @@
 
 
 def matmul_kernel(depth, x_ref, w_ref, out_ref):
-    for stream in range(w_ref.shape[0]):
-        out_ref[stream] = jnp.dot(
-            x_ref[...], w_ref[stream], preferred_element_type=jnp.float32
-        ).astype(out_ref.dtype)
+    streams, _, width = w_ref.shape
+    joined = jnp.concatenate([w_ref[stream] for stream in range(streams)], axis=1)
+    total = jnp.dot(x_ref[...], joined, preferred_element_type=jnp.float32)
+    for stream in range(streams):
+        out_ref[stream] = total[:, stream * width : (stream + 1) * width].astype(out_ref.dtype)
 
 
 def project(x, w):

time: 145 us -> 144 us (level)
  no operation moved by 1% of the time
where the time goes in v16:
time: 144 us
  Pallas kernels  117 us (81%)
  starting transfers between devices  8.37 us (6%)
  local copies, waits for them, and re-layouts  5.96 us (4%)
  matrix products  5.8 us (4%)
  other arithmetic  5.25 us (4%)
    pallas_call x1, Pallas kernels, chan_gather(): pl.pallas_call(functools.partial(gather_kernel, chips, groups), out_shape...  53.5 us
    pallas_call x1, Pallas kernels, half_gather(): pl.pallas_call(functools.partial(half_gather_kernel, chips, groups), out_...  46.2 us
    pallas_call x1, Pallas kernels, ctx_exchange(): pl.pallas_call(functools.partial(exchange_kernel, groups), out_shape=jax....  10.8 us
    pallas_call x1, Pallas kernels, project(): pl.pallas_call(functools.partial(matmul_kernel, depth), out_shape=jax.Sha...  6.32 us
    ppermute x1, starting transfers between devices, body(): result = (mine + lax.ppermute(other, 'chan', pairs)).astype(jnp.bfloat16)  4.55 us
    all_to_all x1, starting transfers between devices, body(): lax.all_to_all(w_late, 'chan', 1, 0, tiled=True, axis_index_groups=same_c...  3.81 us
  transfers between devices with their start and end apart: 2, of which 1 were waited for; matrix products, arithmetic and copies ran while one was open for 6% of the time, Pallas kernels for 32%

profile of v16, /device:TPU:1, one launch (start us, length us, event | category | flops | bytes accessed | tf_op | source)
XLA Modules:
  0.0 143.7 jit_solution(9073394775873866988)
XLA Ops:
  0.0 1.7 %copy.12 = bf16[128,512]{1,0:T(8,128)(2,1)} copy(bf16[128,512]{0,1:T(8,128)(2,1)} %bitcast.90) | data formatting | bytes 262144 | tf_op jit(solution)/shard_map/input_gather_and_filter_to_owner/transpose | solution.py:360
  1.7 53.5 %input_gather_and_filter_to_owner.1 = (bf16[512,4096]{1,0:T(8,128)(2,1)}, bf16[8,16,512]{2,1,0:T(8,128)(2,1)}) custom-call(bf16[512,128]{1,0:T(8,128)(2,1)} %refs_0_.1, bf16[8,16,512]{2,1,0:T(8,128)(2,1)} %bitcast.89), custom_call_target="tpu_custom_call" | custom-call | tf_op jit(solution)/shard_map/input_gather_and_filter_to_owner/pallas_call | solution.py:187
  55.2 0.0 copy-start.1
  55.2 6.3 %input_projection.1 = bf16[3,512,128]{2,1,0:T(8,128)(2,1)} custom-call(bf16[512,4096]{1,0:T(8,128)(2,1)} %get-tuple-element.9.x_ref, bf16[3,4096,128]{2,1,0:T(8,128)(2,1)} %bitcast.80), custom_call_target="tpu_custom_call" | custom-call | flops 1610612736 | bytes 7733248 | tf_op jit(solution)/shard_map/input_projection/pallas_call | solution.py:326
  61.5 1.2 copy.13
  62.7 0.8 copy.26
  63.5 10.8 %projection_to_owner.1 = bf16[8,3,16,512]{3,2,1,0:T(8,128)(2,1)} custom-call(bf16[8,3,16,512]{3,2,1,0:T(8,128)(2,1)} %bitcast.88), custom_call_target="tpu_custom_call" | custom-call | tf_op jit(solution)/shard_map/projection_to_owner/pallas_call | solution.py:149
  74.3 0.0 copy-done.1
  74.3 0.0 copy-start
  74.3 0.0 copy-start.3
  74.3 0.7 copy.18
  75.0 1.3 copy.19
  76.3 3.8 %all-to-all-start = ((bf16[128,16,256]{2,0,1:T(8,128)(2,1)}), bf16[128,16,256]{2,0,1:T(8,128)(2,1)S(1)}, u32[]{:S(2)}, u32[]{:S(2)}) async-start(bf16[128,16,256]{2,0,1:T(8,128)(2,1)} %copy.19), calls=%async_computation | async-start | bytes 2097152 | tf_op jit(solution)/shard_map/out_weight_columns/all_to_all | solution.py:374
  80.2 0.5 fusion.41
  80.7 0.0 copy-done
  80.8 0.1 slice.210
  80.9 0.2 fusion.17
  81.1 0.6 fusion.44
  81.7 0.0 copy-done.3
  81.7 0.1 fusion.49
  81.8 0.4 add_convert_fusion
  82.2 1.5 %negate_convert_fusion = (bf16[32,32,1024]{2,1,0:T(8,128)(2,1)S(1)}, bf16[32,32,1024]{2,1,0:T(8,128)(2,1)S(1)}) fusion(f32[32,1024]{1,0:T(8,128)S(1)} %get-tuple-element.52, f32[32,1024]{1,0:T(8,128)S(1)} %get-tuple-element.51, f32[32,1024]{1,0:T(8,128)S(1)} %get-tuple-element.53, f32[32,1024]{1,0:T(8,128)S(1)} %get-tuple-element.50), kind=kLoop, calls=%fused_computation.5 | loop fusion | flops 9437184 | bytes 4718592 | tf_op jit(solution)/shard_map/convert.8
  83.7 0.0 copy-start.2
  83.7 0.8 convolution_convert_fusion
  84.5 0.1 slice_convert_fusion.2
  84.6 0.0 copy-done.2
  84.6 0.1 slice.172
  84.7 0.0 copy-start.4
  84.8 1.5 %fusion.3 = bf16[8,16,2048]{2,1,0:T(8,128)(2,1)S(1)} fusion(bf16[1024,1024]{1,0:T(8,128)(2,1)S(1)} %bitcast.82, bf16[1024,1024]{1,0:T(8,128)(2,1)S(1)} %bitcast.85, bf16[7,16,511]{2,1,0:T(8,128)(2,1)S(1)} %slice.172, bf16[8,16,512]{2,1,0:T(8,128)(2,1)S(1)} %copy-done.2, bf16[1024]{0:T(1024)(128)(2,1)S(1)} %pad.78.clone), kind=kOutput, calls=%fused_computation.7 | convolution fusion | flops 546570240 | bytes 4966176 | tf_op jit(solution)/shard_map/spectra/kdm,fm->kdf/dot_general | solution.py:403
  86.3 0.1 slice_convert_fusion.3
  86.4 0.0 copy-done.4
  86.4 0.1 dynamic_slice.13
  86.5 0.1 multiply_subtract_fusion.6
  86.7 0.1 multiply_subtract_fusion.3
  86.7 0.1 multiply_subtract_fusion.2
  86.8 0.1 multiply_subtract_fusion.1
  86.9 0.1 multiply_subtract_fusion
  87.1 0.3 add_convert_fusion.2
  87.3 0.3 add_convert_fusion.1
  87.6 1.1 fusion.10.t_ref
  88.7 46.2 %output_projection.1 = bf16[16,128,512]{2,1,0:T(8,128)(2,1)} custom-call(bf16[8,16,512]{2,1,0:T(8,128)(2,1)} %fusion.10.t_ref), custom_call_target="tpu_custom_call" | custom-call | tf_op jit(solution)/shard_map/output_projection/pallas_call | solution.py:293
  134.9 0.0 all-to-all-done
  134.9 2.3 %convolution_bitcast_fusion = f32[512,256]{1,0:T(8,128)S(1)} fusion(bf16[16,128,512]{2,1,0:T(8,128)(2,1)} %output_projection.1, bf16[128,16,256]{2,0,1:T(8,128)(2,1)S(1)} %all-to-all-done), kind=kOutput, calls=%fused_computation.11 | convolution fusion | flops 536870912 | bytes 3670016 | tf_op jit(solution)/shard_map/output_projection/dot_general | solution.py:433
  137.3 4.6 %collective-permute-start = (f32[512,128]{1,0:T(8,128)S(1)}, f32[512,128]{1,0:T(8,128)S(1)}, u32[]{:S(2)}, u32[]{:S(2)}) collective-permute-start(f32[512,128]{1,0:T(8,128)S(1)} %constant_dynamic-slice_fusion.2), channel_id=1, source_target_pairs={{0,1},{1,0},{2,3},{3,2},{4,5},{5,4},{6,7},{7,6},{8,9},{9,8},{10,11... | collective-permute-start | bytes 786440 | tf_op jit(solution)/shard_map/output_projection/ppermute | solution.py:440
  141.9 1.2 collective-permute-done
  143.0 0.7 add_convert_fusion.3
  (7 shorter events, 0.2 us)
Async XLA Ops:
  55.2 19.1 %copy-start.1 = (bf16[128,4096]{1,0:T(8,128)(2,1)S(1)}, bf16[128,4096]{1,0:T(8,128)(2,1)}, u32[]{:S(2)}) copy-start(bf16[128,4096]{1,0:T(8,128)(2,1)} %param.11) | copy-start | bytes 3145732
  74.3 6.4 %copy-start = (bf16[8,3,16,512]{3,2,1,0:T(8,128)(2,1)S(1)}, bf16[8,3,16,512]{3,2,1,0:T(8,128)(2,1)}, u32[]{:S(2)}) copy-start(bf16[8,3,16,512]{3,2,1,0:T(8,128)(2,1)} %projection_to_owner.1) | copy-start | bytes 1179652
  74.3 7.4 %copy-start.3 = (bf16[3,3,128]{2,1,0:T(4,128)(2,1)S(1)}, bf16[3,3,128]{2,1,0:T(4,128)(2,1)}, u32[]{:S(2)}) copy-start(bf16[3,3,128]{2,1,0:T(4,128)(2,1)} %param.8) | copy-start | bytes 6916
  76.3 58.6 %all-to-all-start = ((bf16[128,16,256]{2,0,1:T(8,128)(2,1)}), bf16[128,16,256]{2,0,1:T(8,128)(2,1)S(1)}, u32[]{:S(2)}, u32[]{:S(2)}) async-start(bf16[128,16,256]{2,0,1:T(8,128)(2,1)} %copy.19), calls=%async_computation | async-start | bytes 2097152 | tf_op jit(solution)/shard_map/out_weight_columns/all_to_all | solution.py:374
  83.7 1.0 copy-start.2
  84.7 1.6 %copy-start.4 = (f32[128]{0:T(128)S(1)}, f32[128]{0:T(128)}, u32[]{:S(2)}) copy-start(f32[128]{0:T(128)} %param.9) | copy-start | bytes 1540
  137.3 5.7 %collective-permute-start = (f32[512,128]{1,0:T(8,128)S(1)}, f32[512,128]{1,0:T(8,128)S(1)}, u32[]{:S(2)}, u32[]{:S(2)}) collective-permute-start(f32[512,128]{1,0:T(8,128)S(1)} %constant_dynamic-slice_fusion.2), channel_id=1, source_target_pairs={{0,1},{1,0},{2,3},{3,2},{4,5},{5,4},{6,7},{7,6},{8,9},{9,8},{10,11... | collective-permute-start | bytes 786440 | tf_op jit(solution)/shard_map/output_projection/ppermute | solution.py:440

commit v17 on v16

--- a/solution.py
+++ b/solution.py
@@ -313,24 +313,28 @@
     return out.reshape(size // 2 * block[0], block[1])
 
 
-def matmul_kernel(depth, x_ref, w_ref, out_ref):
-    streams, _, width = w_ref.shape
+def matmul_kernel(x_ref, w_ref, out_ref):
+    groups, streams, own, _ = out_ref.shape
+    width = w_ref.shape[2]
     joined = jnp.concatenate([w_ref[stream] for stream in range(streams)], axis=1)
-    total = jnp.dot(x_ref[...], joined, preferred_element_type=jnp.float32)
+    total = jnp.dot(x_ref[...], joined, preferred_element_type=jnp.float32).T
     for stream in range(streams):
-        out_ref[stream] = total[:, stream * width : (stream + 1) * width].astype(out_ref.dtype)
-
-
-def project(x, w):
-    depth = 512
+        for g in range(groups):
+            first = stream * width + g * own
+            out_ref[g, stream] = total[first : first + own, :].astype(out_ref.dtype)
+
+
+def project(x, w, groups):
+    streams, _, width = w.shape
     return pl.pallas_call(
-        functools.partial(matmul_kernel, depth),
-        out_shape=jax.ShapeDtypeStruct((w.shape[0], x.shape[0], w.shape[2]), jnp.bfloat16),
+        matmul_kernel,
+        out_shape=jax.ShapeDtypeStruct((groups, streams, width // groups, x.shape[0]),
+                                       jnp.bfloat16),
         in_specs=[pl.BlockSpec(memory_space=pltpu.VMEM)] * 2,
         out_specs=pl.BlockSpec(memory_space=pltpu.VMEM),
         cost_estimate=pl.CostEstimate(
-            flops=2 * x.shape[0] * x.shape[1] * w.shape[0] * w.shape[2], transcendentals=0,
-            bytes_accessed=2 * (x.size + w.size + x.shape[0] * w.shape[0] * w.shape[2])),
+            flops=2 * x.shape[0] * x.shape[1] * streams * width, transcendentals=0,
+            bytes_accessed=2 * (x.size + w.size + x.shape[0] * streams * width)),
     )(x, w)
 
 
@@ -361,10 +365,9 @@
         inputs_all, taps_t = chan_gather(inputs, taps_t, 0)
 
     with jax.named_scope("input_projection"):
-        projected = project(inputs_all, jnp.transpose(w_in, (1, 0, 2)))
+        proj_t = project(inputs_all, jnp.transpose(w_in, (1, 0, 2)), groups)
 
     with jax.named_scope("projection_to_owner"):
-        proj_t = projected.reshape(3, span_len, groups, own).transpose(2, 0, 3, 1)
         proj_t = ctx_exchange(proj_t, 3)
 
     with jax.named_scope("out_weight_columns"):

time: 144 us -> 142 us (0.986)
  local copies, waits for them, and re-layouts: 5.96 us -> 4.02 us
  transfers between devices with their start and end apart: 2 -> 2, of which waited for: 1 -> 1; matrix products, arithmetic and copies ran while one was open for 6% -> 6% of each run, Pallas kernels for 32% -> 33%
where the time goes in v17:
time: 142 us
  Pallas kernels  117 us (82%)
  starting transfers between devices  8.37 us (6%)
  matrix products  5.8 us (4%)
  other arithmetic  5.25 us (4%)
  local copies, waits for them, and re-layouts  4.02 us (3%)
    pallas_call x1, Pallas kernels, chan_gather(): pl.pallas_call(functools.partial(gather_kernel, chips, groups), out_shape...  53.5 us
    pallas_call x1, Pallas kernels, half_gather(): pl.pallas_call(functools.partial(half_gather_kernel, chips, groups), out_...  46.2 us
    pallas_call x1, Pallas kernels, ctx_exchange(): pl.pallas_call(functools.partial(exchange_kernel, groups), out_shape=jax....  10.8 us
    pallas_call x1, Pallas kernels, project(): pl.pallas_call(matmul_kernel, out_shape=jax.ShapeDtypeStruct((groups, str...  6.39 us
    ppermute x1, starting transfers between devices, body(): result = (mine + lax.ppermute(other, 'chan', pairs)).astype(jnp.bfloat16)  4.55 us
    all_to_all x1, starting transfers between devices, body(): lax.all_to_all(w_late, 'chan', 1, 0, tiled=True, axis_index_groups=same_c...  3.81 us
  transfers between devices with their start and end apart: 2, of which 1 were waited for; matrix products, arithmetic and copies ran while one was open for 6% of the time, Pallas kernels for 33%

profile of v17, /device:TPU:1, one launch (start us, length us, event | category | flops | bytes accessed | tf_op | source)
XLA Modules:
  0.0 141.9 jit_solution(13466352495525408316)
XLA Ops:
  0.0 1.7 %copy.12 = bf16[128,512]{1,0:T(8,128)(2,1)} copy(bf16[128,512]{0,1:T(8,128)(2,1)} %bitcast.84) | data formatting | bytes 262144 | tf_op jit(solution)/shard_map/input_gather_and_filter_to_owner/transpose | solution.py:364
  1.7 53.5 %input_gather_and_filter_to_owner.1 = (bf16[512,4096]{1,0:T(8,128)(2,1)}, bf16[8,16,512]{2,1,0:T(8,128)(2,1)}) custom-call(bf16[512,128]{1,0:T(8,128)(2,1)} %refs_0_.1, bf16[8,16,512]{2,1,0:T(8,128)(2,1)} %bitcast.83), custom_call_target="tpu_custom_call" | custom-call | tf_op jit(solution)/shard_map/input_gather_and_filter_to_owner/pallas_call | solution.py:187
  55.2 0.0 copy-start.1
  55.2 6.4 %input_projection.1.x_ref = bf16[8,3,16,512]{3,2,1,0:T(8,128)(2,1)} custom-call(bf16[512,4096]{1,0:T(8,128)(2,1)} %get-tuple-element.9.x_ref, bf16[3,4096,128]{2,1,0:T(8,128)(2,1)} %bitcast.76), custom_call_target="tpu_custom_call" | custom-call | flops 1610612736 | bytes 7733248 | tf_op jit(solution)/shard_map/input_projection/pallas_call | solution.py:329
  61.6 10.8 %projection_to_owner.1 = bf16[8,3,16,512]{3,2,1,0:T(8,128)(2,1)} custom-call(bf16[8,3,16,512]{3,2,1,0:T(8,128)(2,1)} %input_projection.1.x_ref), custom_call_target="tpu_custom_call" | custom-call | tf_op jit(solution)/shard_map/projection_to_owner/pallas_call | solution.py:149
  72.4 0.0 copy-done.1
  72.5 0.0 copy-start
  72.5 0.0 copy-start.3
  72.5 0.7 copy.16
  73.1 1.3 copy.17
  74.5 3.8 %all-to-all-start = ((bf16[128,16,256]{2,0,1:T(8,128)(2,1)}), bf16[128,16,256]{2,0,1:T(8,128)(2,1)S(1)}, u32[]{:S(2)}, u32[]{:S(2)}) async-start(bf16[128,16,256]{2,0,1:T(8,128)(2,1)} %copy.17), calls=%async_computation | async-start | bytes 2097152 | tf_op jit(solution)/shard_map/out_weight_columns/all_to_all | solution.py:377
  78.3 0.5 fusion.41
  78.8 0.0 copy-done
  78.9 0.1 slice.210
  79.0 0.2 fusion.17
  79.2 0.6 fusion.44
  79.8 0.0 copy-done.3
  79.8 0.1 fusion.49
  79.9 0.4 add_convert_fusion
  80.3 1.5 %negate_convert_fusion = (bf16[32,32,1024]{2,1,0:T(8,128)(2,1)S(1)}, bf16[32,32,1024]{2,1,0:T(8,128)(2,1)S(1)}) fusion(f32[32,1024]{1,0:T(8,128)S(1)} %get-tuple-element.52, f32[32,1024]{1,0:T(8,128)S(1)} %get-tuple-element.51, f32[32,1024]{1,0:T(8,128)S(1)} %get-tuple-element.53, f32[32,1024]{1,0:T(8,128)S(1)} %get-tuple-element.50), kind=kLoop, calls=%fused_computation.5 | loop fusion | flops 9437184 | bytes 4718592 | tf_op jit(solution)/shard_map/convert.8
  81.8 0.0 copy-start.2
  81.8 0.8 convolution_convert_fusion
  82.6 0.1 slice_convert_fusion.2
  82.7 0.0 copy-done.2
  82.8 0.1 slice.172
  82.9 0.0 copy-start.4
  82.9 1.5 %fusion.3 = bf16[8,16,2048]{2,1,0:T(8,128)(2,1)S(1)} fusion(bf16[1024,1024]{1,0:T(8,128)(2,1)S(1)} %bitcast.78, bf16[1024,1024]{1,0:T(8,128)(2,1)S(1)} %bitcast.81, bf16[7,16,511]{2,1,0:T(8,128)(2,1)S(1)} %slice.172, bf16[8,16,512]{2,1,0:T(8,128)(2,1)S(1)} %copy-done.2, bf16[1024]{0:T(1024)(128)(2,1)S(1)} %pad.78.clone), kind=kOutput, calls=%fused_computation.7 | convolution fusion | flops 546570240 | bytes 4966176 | tf_op jit(solution)/shard_map/spectra/kdm,fm->kdf/dot_general | solution.py:406
  84.4 0.1 slice_convert_fusion.3
  84.5 0.0 copy-done.4
  84.5 0.1 dynamic_slice.13
  84.6 0.1 multiply_subtract_fusion.6
  84.8 0.1 multiply_subtract_fusion.3
  84.9 0.1 multiply_subtract_fusion.2
  85.0 0.1 multiply_subtract_fusion.1
  85.1 0.1 multiply_subtract_fusion
  85.2 0.3 add_convert_fusion.2
  85.5 0.3 add_convert_fusion.1
  85.7 1.1 fusion.10.t_ref
  86.9 46.2 %output_projection.1 = bf16[16,128,512]{2,1,0:T(8,128)(2,1)} custom-call(bf16[8,16,512]{2,1,0:T(8,128)(2,1)} %fusion.10.t_ref), custom_call_target="tpu_custom_call" | custom-call | tf_op jit(solution)/shard_map/output_projection/pallas_call | solution.py:293
  133.1 0.0 all-to-all-done
  133.1 2.3 %convolution_bitcast_fusion = f32[512,256]{1,0:T(8,128)S(1)} fusion(bf16[16,128,512]{2,1,0:T(8,128)(2,1)} %output_projection.1, bf16[128,16,256]{2,0,1:T(8,128)(2,1)S(1)} %all-to-all-done), kind=kOutput, calls=%fused_computation.11 | convolution fusion | flops 536870912 | bytes 3670016 | tf_op jit(solution)/shard_map/output_projection/dot_general | solution.py:436
  135.4 4.6 %collective-permute-start = (f32[512,128]{1,0:T(8,128)S(1)}, f32[512,128]{1,0:T(8,128)S(1)}, u32[]{:S(2)}, u32[]{:S(2)}) collective-permute-start(f32[512,128]{1,0:T(8,128)S(1)} %constant_dynamic-slice_fusion.2), channel_id=1, source_target_pairs={{0,1},{1,0},{2,3},{3,2},{4,5},{5,4},{6,7},{7,6},{8,9},{9,8},{10,11... | collective-permute-start | bytes 786440 | tf_op jit(solution)/shard_map/output_projection/ppermute | solution.py:443
  140.0 1.2 collective-permute-done
  141.2 0.7 add_convert_fusion.3
  (7 shorter events, 0.2 us)
Async XLA Ops:
  55.2 17.3 %copy-start.1 = (bf16[128,4096]{1,0:T(8,128)(2,1)S(1)}, bf16[128,4096]{1,0:T(8,128)(2,1)}, u32[]{:S(2)}) copy-start(bf16[128,4096]{1,0:T(8,128)(2,1)} %param.11) | copy-start | bytes 3145732
  72.5 6.4 %copy-start = (bf16[8,3,16,512]{3,2,1,0:T(8,128)(2,1)S(1)}, bf16[8,3,16,512]{3,2,1,0:T(8,128)(2,1)}, u32[]{:S(2)}) copy-start(bf16[8,3,16,512]{3,2,1,0:T(8,128)(2,1)} %projection_to_owner.1) | copy-start | bytes 1179652
  72.5 7.4 %copy-start.3 = (bf16[3,3,128]{2,1,0:T(4,128)(2,1)S(1)}, bf16[3,3,128]{2,1,0:T(4,128)(2,1)}, u32[]{:S(2)}) copy-start(bf16[3,3,128]{2,1,0:T(4,128)(2,1)} %param.8) | copy-start | bytes 6916
  74.5 58.6 %all-to-all-start = ((bf16[128,16,256]{2,0,1:T(8,128)(2,1)}), bf16[128,16,256]{2,0,1:T(8,128)(2,1)S(1)}, u32[]{:S(2)}, u32[]{:S(2)}) async-start(bf16[128,16,256]{2,0,1:T(8,128)(2,1)} %copy.17), calls=%async_computation | async-start | bytes 2097152 | tf_op jit(solution)/shard_map/out_weight_columns/all_to_all | solution.py:377
  81.8 1.0 copy-start.2
  82.9 1.6 %copy-start.4 = (f32[128]{0:T(128)S(1)}, f32[128]{0:T(128)}, u32[]{:S(2)}) copy-start(f32[128]{0:T(128)} %param.9) | copy-start | bytes 1540
  135.4 5.7 %collective-permute-start = (f32[512,128]{1,0:T(8,128)S(1)}, f32[512,128]{1,0:T(8,128)S(1)}, u32[]{:S(2)}, u32[]{:S(2)}) collective-permute-start(f32[512,128]{1,0:T(8,128)S(1)} %constant_dynamic-slice_fusion.2), channel_id=1, source_target_pairs={{0,1},{1,0},{2,3},{3,2},{4,5},{5,4},{6,7},{7,6},{8,9},{9,8},{10,11... | collective-permute-start | bytes 786440 | tf_op jit(solution)/shard_map/output_projection/ppermute | solution.py:443

commit v18 on v17

--- a/solution.py
+++ b/solution.py
@@ -338,6 +338,23 @@
     )(x, w)
 
 
+def split_kernel(w_ref, out_ref):
+    pieces, _, width = out_ref.shape
+    for m in range(pieces):
+        out_ref[m] = w_ref[:, m * width : (m + 1) * width]
+
+
+def split_columns(w, pieces):
+    rows, cols = w.shape
+    return pl.pallas_call(
+        split_kernel,
+        out_shape=jax.ShapeDtypeStruct((pieces, rows, cols // pieces), w.dtype),
+        in_specs=[pl.BlockSpec(memory_space=pltpu.VMEM)],
+        out_specs=pl.BlockSpec(memory_space=pltpu.VMEM),
+        cost_estimate=pl.CostEstimate(flops=0, transcendentals=0, bytes_accessed=4 * w.size),
+    )(w)
+
+
 def dft_table(double_len):
     step = 32
     hi_ids = jnp.arange(double_len // step, dtype=jnp.int32)[:, None]
@@ -374,7 +391,9 @@
         w_late, proj_t = lax.optimization_barrier((w_out, proj_t))
         size = lax.axis_size("chan")
         same_core = [list(range(c, size, 2)) for c in range(2)]
-        w_cols = lax.all_to_all(w_late, "chan", 1, 0, tiled=True, axis_index_groups=same_core)
+        pieces = split_columns(w_late, size // 2)
+        w_cols = lax.all_to_all(pieces, "chan", 0, 1, tiled=True, axis_index_groups=same_core)
+        w_cols = w_cols.reshape(size // 2 * width_dev, -1)
 
     with jax.named_scope("short_conv"):
         start = position * own

time: 142 us -> 142 us (level)
  Pallas kernels: 117 us -> 119 us
  local copies, waits for them, and re-layouts: 4.02 us -> 2.03 us
    pallas_call x0 -> x1, Pallas kernels: none -> 2.32 us  [split_columns(): pl.pallas_call(split_kernel, out_shape=jax.ShapeDtypeStruct((pieces, rows...]
  transfers between devices with their start and end apart: 2 -> 2, of which waited for: 1 -> 1; matrix products, arithmetic and copies ran while one was open for 6% -> 6% of each run, Pallas kernels for 33% -> 32%
where the time goes in v18:
time: 142 us
  Pallas kernels  119 us (84%)
  starting transfers between devices  8.37 us (6%)
  matrix products  5.8 us (4%)
  other arithmetic  5.25 us (4%)
  local copies, waits for them, and re-layouts  2.03 us (1%)
    pallas_call x1, Pallas kernels, chan_gather(): pl.pallas_call(functools.partial(gather_kernel, chips, groups), out_shape...  53.5 us
    pallas_call x1, Pallas kernels, half_gather(): pl.pallas_call(functools.partial(half_gather_kernel, chips, groups), out_...  46.2 us
    pallas_call x1, Pallas kernels, ctx_exchange(): pl.pallas_call(functools.partial(exchange_kernel, groups), out_shape=jax....  10.9 us
    pallas_call x1, Pallas kernels, project(): pl.pallas_call(matmul_kernel, out_shape=jax.ShapeDtypeStruct((groups, str...  6.31 us
    ppermute x1, starting transfers between devices, body(): result = (mine + lax.ppermute(other, 'chan', pairs)).astype(jnp.bfloat16)  4.55 us
    all_to_all x1, starting transfers between devices, body(): lax.all_to_all(pieces, 'chan', 0, 1, tiled=True, axis_index_groups=same_c...  3.81 us
  transfers between devices with their start and end apart: 2, of which 1 were waited for; matrix products, arithmetic and copies ran while one was open for 6% of the time, Pallas kernels for 32%

profile of v18, /device:TPU:1, one launch (start us, length us, event | category | flops | bytes accessed | tf_op | source)
XLA Modules:
  0.0 142.1 jit_solution(2493853789244505905)
XLA Ops:
  0.0 1.7 %copy.7 = bf16[128,512]{1,0:T(8,128)(2,1)} copy(bf16[128,512]{0,1:T(8,128)(2,1)} %bitcast.80) | data formatting | bytes 262144 | tf_op jit(solution)/shard_map/input_gather_and_filter_to_owner/transpose | solution.py:381
  1.7 53.5 %input_gather_and_filter_to_owner.1 = (bf16[512,4096]{1,0:T(8,128)(2,1)}, bf16[8,16,512]{2,1,0:T(8,128)(2,1)}) custom-call(bf16[512,128]{1,0:T(8,128)(2,1)} %refs_0_.1, bf16[8,16,512]{2,1,0:T(8,128)(2,1)} %bitcast.79), custom_call_target="tpu_custom_call" | custom-call | tf_op jit(solution)/shard_map/input_gather_and_filter_to_owner/pallas_call | solution.py:187
  55.2 6.3 %input_projection.1.x_ref = bf16[8,3,16,512]{3,2,1,0:T(8,128)(2,1)} custom-call(bf16[512,4096]{1,0:T(8,128)(2,1)} %get-tuple-element.9.x_ref, bf16[3,4096,128]{2,1,0:T(8,128)(2,1)} %bitcast.72), custom_call_target="tpu_custom_call" | custom-call | flops 1610612736 | bytes 7733248 | tf_op jit(solution)/shard_map/input_projection/pallas_call | solution.py:329
  61.5 0.0 copy-start.2
  61.5 10.9 %projection_to_owner.1 = bf16[8,3,16,512]{3,2,1,0:T(8,128)(2,1)} custom-call(bf16[8,3,16,512]{3,2,1,0:T(8,128)(2,1)} %input_projection.1.x_ref), custom_call_target="tpu_custom_call" | custom-call | tf_op jit(solution)/shard_map/projection_to_owner/pallas_call | solution.py:149
  72.4 0.0 copy-start
  72.4 2.3 %out_weight_columns.1 = bf16[16,128,256]{2,1,0:T(8,128)(2,1)} custom-call(bf16[128,4096]{1,0:T(8,128)(2,1)} %w_ref), custom_call_target="tpu_custom_call" | custom-call | bytes 2097152 | tf_op jit(solution)/shard_map/out_weight_columns/pallas_call | solution.py:349
  74.7 3.8 %all-to-all-start = ((bf16[16,128,256]{2,1,0:T(8,128)(2,1)}), bf16[16,128,256]{2,1,0:T(8,128)(2,1)S(1)}, u32[]{:S(2)}, u32[]{:S(2)}) async-start(bf16[16,128,256]{2,1,0:T(8,128)(2,1)} %out_weight_columns.1), calls=%async_computation | async-start | bytes 2097152 | tf_op jit(solution)/shard_map/out_weight_columns/all_to_all | solution.py:395
  78.5 0.5 fusion.40
  79.1 0.0 copy-done
  79.1 0.1 slice.210
  79.2 0.2 fusion.16
  79.5 0.6 fusion.43
  80.0 0.0 copy-done.2
  80.1 0.1 fusion.48
  80.1 0.4 add_convert_fusion
  80.5 1.5 %negate_convert_fusion = (bf16[32,32,1024]{2,1,0:T(8,128)(2,1)S(1)}, bf16[32,32,1024]{2,1,0:T(8,128)(2,1)S(1)}) fusion(f32[32,1024]{1,0:T(8,128)S(1)} %get-tuple-element.52, f32[32,1024]{1,0:T(8,128)S(1)} %get-tuple-element.51, f32[32,1024]{1,0:T(8,128)S(1)} %get-tuple-element.53, f32[32,1024]{1,0:T(8,128)S(1)} %get-tuple-element.50), kind=kLoop, calls=%fused_computation.5 | loop fusion | flops 9437184 | bytes 4718592 | tf_op jit(solution)/shard_map/convert.8
  82.0 0.0 copy-start.1
  82.0 0.8 convolution_convert_fusion
  82.8 0.1 slice_convert_fusion.2
  83.0 0.0 copy-done.1
  83.0 0.1 slice.172
  83.1 0.0 copy-start.3
  83.1 1.5 %fusion.3 = bf16[8,16,2048]{2,1,0:T(8,128)(2,1)S(1)} fusion(bf16[1024,1024]{1,0:T(8,128)(2,1)S(1)} %bitcast.74, bf16[1024,1024]{1,0:T(8,128)(2,1)S(1)} %bitcast.77, bf16[7,16,511]{2,1,0:T(8,128)(2,1)S(1)} %slice.172, bf16[8,16,512]{2,1,0:T(8,128)(2,1)S(1)} %copy-done.1, bf16[1024]{0:T(1024)(128)(2,1)S(1)} %pad.78.clone), kind=kOutput, calls=%fused_computation.7 | convolution fusion | flops 546570240 | bytes 4966176 | tf_op jit(solution)/shard_map/spectra/kdm,fm->kdf/dot_general | solution.py:425
  84.6 0.1 slice_convert_fusion.3
  84.7 0.0 copy-done.3
  84.7 0.1 dynamic_slice.13
  84.8 0.1 multiply_subtract_fusion.6
  85.0 0.1 multiply_subtract_fusion.3
  85.1 0.1 multiply_subtract_fusion.2
  85.2 0.1 multiply_subtract_fusion.1
  85.3 0.1 multiply_subtract_fusion
  85.4 0.3 add_convert_fusion.2
  85.7 0.3 add_convert_fusion.1
  85.9 1.1 fusion.10.t_ref
  87.1 46.2 %output_projection.1 = bf16[16,128,512]{2,1,0:T(8,128)(2,1)} custom-call(bf16[8,16,512]{2,1,0:T(8,128)(2,1)} %fusion.10.t_ref), custom_call_target="tpu_custom_call" | custom-call | tf_op jit(solution)/shard_map/output_projection/pallas_call | solution.py:293
  133.3 0.0 all-to-all-done
  133.3 2.3 %convolution_bitcast_fusion = f32[512,256]{1,0:T(8,128)S(1)} fusion(bf16[16,128,512]{2,1,0:T(8,128)(2,1)} %output_projection.1, bf16[16,128,256]{2,1,0:T(8,128)(2,1)S(1)} %all-to-all-done), kind=kOutput, calls=%fused_computation.11 | convolution fusion | flops 536870912 | bytes 3670016 | tf_op jit(solution)/shard_map/output_projection/dot_general | solution.py:455
  135.7 4.6 %collective-permute-start = (f32[512,128]{1,0:T(8,128)S(1)}, f32[512,128]{1,0:T(8,128)S(1)}, u32[]{:S(2)}, u32[]{:S(2)}) collective-permute-start(f32[512,128]{1,0:T(8,128)S(1)} %constant_dynamic-slice_fusion.2), channel_id=1, source_target_pairs={{0,1},{1,0},{2,3},{3,2},{4,5},{5,4},{6,7},{7,6},{8,9},{9,8},{10,11... | collective-permute-start | bytes 786440 | tf_op jit(solution)/shard_map/output_projection/ppermute | solution.py:462
  140.2 1.2 collective-permute-done
  141.4 0.7 add_convert_fusion.3
  (7 shorter events, 0.2 us)
Async XLA Ops:
  61.5 18.6 %copy-start.2 = (bf16[3,3,128]{2,1,0:T(4,128)(2,1)S(1)}, bf16[3,3,128]{2,1,0:T(4,128)(2,1)}, u32[]{:S(2)}) copy-start(bf16[3,3,128]{2,1,0:T(4,128)(2,1)} %param.8) | copy-start | bytes 6916
  72.4 6.7 %copy-start = (bf16[8,3,16,512]{3,2,1,0:T(8,128)(2,1)S(1)}, bf16[8,3,16,512]{3,2,1,0:T(8,128)(2,1)}, u32[]{:S(2)}) copy-start(bf16[8,3,16,512]{3,2,1,0:T(8,128)(2,1)} %projection_to_owner.1) | copy-start | bytes 1179652
  74.7 58.6 %all-to-all-start = ((bf16[16,128,256]{2,1,0:T(8,128)(2,1)}), bf16[16,128,256]{2,1,0:T(8,128)(2,1)S(1)}, u32[]{:S(2)}, u32[]{:S(2)}) async-start(bf16[16,128,256]{2,1,0:T(8,128)(2,1)} %out_weight_columns.1), calls=%async_computation | async-start | bytes 2097152 | tf_op jit(solution)/shard_map/out_weight_columns/all_to_all | solution.py:395
  82.0 1.0 copy-start.1
  83.1 1.6 %copy-start.3 = (f32[128]{0:T(128)S(1)}, f32[128]{0:T(128)}, u32[]{:S(2)}) copy-start(f32[128]{0:T(128)} %param.9) | copy-start | bytes 1540
  135.7 5.7 %collective-permute-start = (f32[512,128]{1,0:T(8,128)S(1)}, f32[512,128]{1,0:T(8,128)S(1)}, u32[]{:S(2)}, u32[]{:S(2)}) collective-permute-start(f32[512,128]{1,0:T(8,128)S(1)} %constant_dynamic-slice_fusion.2), channel_id=1, source_target_pairs={{0,1},{1,0},{2,3},{3,2},{4,5},{5,4},{6,7},{7,6},{8,9},{9,8},{10,11... | collective-permute-start | bytes 786440 | tf_op jit(solution)/shard_map/output_projection/ppermute | solution.py:462

commit v19 on v17

--- a/solution.py
+++ b/solution.py
@@ -117,10 +117,26 @@
             src_ref=x_ref.at[peer], dst_ref=out_ref.at[slot], send_sem=send_sem.at[k - 1],
             recv_sem=recv_sem.at[k - 1], device_id=(peer, col), device_id_type=MESH)
 
-    sends = [send(k, (me + k) % groups, me) for k in range(1, groups)]
-    sources = [(me - k + groups) % groups for k in range(1, groups)]
-    receipts = [send(k, source, source) for k, source in zip(range(1, groups), sources)]
+    order = far_first(groups)
+    peers = [flip(me, k) for k in order]
+    sends = [send(i + 1, peer, me) for i, peer in enumerate(peers)]
+    receipts = [send(i + 1, peer, peer) for i, peer in enumerate(peers)]
     return local, sends, receipts
+
+
+def flip(me, k):
+    out, bit = 0, 1
+    while bit <= k:
+        mine = (me // bit) % 2
+        theirs = (k // bit) % 2
+        out = out + bit * (mine + theirs - 2 * mine * theirs)
+        bit *= 2
+    return out + (me // bit) * bit
+
+
+def far_first(groups):
+    hops = lambda k: 2 * (k % 2) + [0, 1, 2, 1][(k // 2) % 4]
+    return sorted(range(1, groups), key=lambda k: -hops(k))
 
 
 def ctx_peers(groups):

time: 142 us -> 142 us (level)
  no operation moved by 1% of the time
where the time goes in v19:
time: 142 us
  Pallas kernels  118 us (83%)
  starting transfers between devices  7.93 us (6%)
  matrix products  5.8 us (4%)
  other arithmetic  5.25 us (4%)
  local copies, waits for them, and re-layouts  4.02 us (3%)
    pallas_call x1, Pallas kernels, chan_gather(): pl.pallas_call(functools.partial(gather_kernel, chips, groups), out_shape...  53.7 us
    pallas_call x1, Pallas kernels, half_gather(): pl.pallas_call(functools.partial(half_gather_kernel, chips, groups), out_...  46.6 us
    pallas_call x1, Pallas kernels, ctx_exchange(): pl.pallas_call(functools.partial(exchange_kernel, groups), out_shape=jax....  10.9 us
    pallas_call x1, Pallas kernels, project(): pl.pallas_call(matmul_kernel, out_shape=jax.ShapeDtypeStruct((groups, str...  6.39 us
    ppermute x1, starting transfers between devices, body(): result = (mine + lax.ppermute(other, 'chan', pairs)).astype(jnp.bfloat16)  4.27 us
    all_to_all x1, starting transfers between devices, body(): lax.all_to_all(w_late, 'chan', 1, 0, tiled=True, axis_index_groups=same_c...  3.65 us
  transfers between devices with their start and end apart: 2, of which 1 were waited for; matrix products, arithmetic and copies ran while one was open for 6% of the time, Pallas kernels for 33%

profile of v19, /device:TPU:1, one launch (start us, length us, event | category | flops | bytes accessed | tf_op | source)
XLA Modules:
  0.0 142.0 jit_solution(4946995109707158307)
XLA Ops:
  0.0 1.7 %copy.12 = bf16[128,512]{1,0:T(8,128)(2,1)} copy(bf16[128,512]{0,1:T(8,128)(2,1)} %bitcast.84) | data formatting | bytes 262144 | tf_op jit(solution)/shard_map/input_gather_and_filter_to_owner/transpose | solution.py:380
  1.7 53.7 %input_gather_and_filter_to_owner.1 = (bf16[512,4096]{1,0:T(8,128)(2,1)}, bf16[8,16,512]{2,1,0:T(8,128)(2,1)}) custom-call(bf16[512,128]{1,0:T(8,128)(2,1)} %refs_0_.1, bf16[8,16,512]{2,1,0:T(8,128)(2,1)} %bitcast.83), custom_call_target="tpu_custom_call" | custom-call | tf_op jit(solution)/shard_map/input_gather_and_filter_to_owner/pallas_call | solution.py:203
  55.4 0.0 copy-start.1
  55.4 6.4 %input_projection.1.x_ref = bf16[8,3,16,512]{3,2,1,0:T(8,128)(2,1)} custom-call(bf16[512,4096]{1,0:T(8,128)(2,1)} %get-tuple-element.9.x_ref, bf16[3,4096,128]{2,1,0:T(8,128)(2,1)} %bitcast.76), custom_call_target="tpu_custom_call" | custom-call | flops 1610612736 | bytes 7733248 | tf_op jit(solution)/shard_map/input_projection/pallas_call | solution.py:345
  61.8 10.9 %projection_to_owner.1 = bf16[8,3,16,512]{3,2,1,0:T(8,128)(2,1)} custom-call(bf16[8,3,16,512]{3,2,1,0:T(8,128)(2,1)} %input_projection.1.x_ref), custom_call_target="tpu_custom_call" | custom-call | tf_op jit(solution)/shard_map/projection_to_owner/pallas_call | solution.py:165
  72.7 0.0 copy-done.1
  72.7 0.0 copy-start
  72.7 0.0 copy-start.3
  72.7 0.7 copy.16
  73.4 1.3 copy.17
  74.7 3.7 %all-to-all-start = ((bf16[128,16,256]{2,0,1:T(8,128)(2,1)}), bf16[128,16,256]{2,0,1:T(8,128)(2,1)S(1)}, u32[]{:S(2)}, u32[]{:S(2)}) async-start(bf16[128,16,256]{2,0,1:T(8,128)(2,1)} %copy.17), calls=%async_computation | async-start | bytes 2097152 | tf_op jit(solution)/shard_map/out_weight_columns/all_to_all | solution.py:393
  78.4 0.5 fusion.41
  78.9 0.0 copy-done
  79.0 0.1 slice.210
  79.1 0.2 fusion.17
  79.3 0.6 fusion.44
  79.9 0.0 copy-done.3
  79.9 0.1 fusion.49
  80.0 0.4 add_convert_fusion
  80.4 1.5 %negate_convert_fusion = (bf16[32,32,1024]{2,1,0:T(8,128)(2,1)S(1)}, bf16[32,32,1024]{2,1,0:T(8,128)(2,1)S(1)}) fusion(f32[32,1024]{1,0:T(8,128)S(1)} %get-tuple-element.52, f32[32,1024]{1,0:T(8,128)S(1)} %get-tuple-element.51, f32[32,1024]{1,0:T(8,128)S(1)} %get-tuple-element.53, f32[32,1024]{1,0:T(8,128)S(1)} %get-tuple-element.50), kind=kLoop, calls=%fused_computation.5 | loop fusion | flops 9437184 | bytes 4718592 | tf_op jit(solution)/shard_map/convert.8
  81.9 0.0 copy-start.2
  81.9 0.8 convolution_convert_fusion
  82.7 0.1 slice_convert_fusion.2
  82.8 0.0 copy-done.2
  82.8 0.1 slice.172
  82.9 0.0 copy-start.4
  83.0 1.5 %fusion.3 = bf16[8,16,2048]{2,1,0:T(8,128)(2,1)S(1)} fusion(bf16[1024,1024]{1,0:T(8,128)(2,1)S(1)} %bitcast.78, bf16[1024,1024]{1,0:T(8,128)(2,1)S(1)} %bitcast.81, bf16[7,16,511]{2,1,0:T(8,128)(2,1)S(1)} %slice.172, bf16[8,16,512]{2,1,0:T(8,128)(2,1)S(1)} %copy-done.2, bf16[1024]{0:T(1024)(128)(2,1)S(1)} %pad.78.clone), kind=kOutput, calls=%fused_computation.7 | convolution fusion | flops 546570240 | bytes 4966176 | tf_op jit(solution)/shard_map/spectra/kdm,fm->kdf/dot_general | solution.py:422
  84.5 0.1 slice_convert_fusion.3
  84.6 0.0 copy-done.4
  84.6 0.1 dynamic_slice.13
  84.7 0.1 multiply_subtract_fusion.6
  84.9 0.1 multiply_subtract_fusion.3
  84.9 0.1 multiply_subtract_fusion.2
  85.0 0.1 multiply_subtract_fusion.1
  85.1 0.1 multiply_subtract_fusion
  85.3 0.3 add_convert_fusion.2
  85.5 0.3 add_convert_fusion.1
  85.8 1.1 fusion.10.t_ref
  86.9 46.6 %output_projection.1 = bf16[16,128,512]{2,1,0:T(8,128)(2,1)} custom-call(bf16[8,16,512]{2,1,0:T(8,128)(2,1)} %fusion.10.t_ref), custom_call_target="tpu_custom_call" | custom-call | tf_op jit(solution)/shard_map/output_projection/pallas_call | solution.py:309
  133.5 0.0 all-to-all-done
  133.5 2.3 %convolution_bitcast_fusion = f32[512,256]{1,0:T(8,128)S(1)} fusion(bf16[16,128,512]{2,1,0:T(8,128)(2,1)} %output_projection.1, bf16[128,16,256]{2,0,1:T(8,128)(2,1)S(1)} %all-to-all-done), kind=kOutput, calls=%fused_computation.11 | convolution fusion | flops 536870912 | bytes 3670016 | tf_op jit(solution)/shard_map/output_projection/dot_general | solution.py:452
  135.9 4.3 %collective-permute-start = (f32[512,128]{1,0:T(8,128)S(1)}, f32[512,128]{1,0:T(8,128)S(1)}, u32[]{:S(2)}, u32[]{:S(2)}) collective-permute-start(f32[512,128]{1,0:T(8,128)S(1)} %constant_dynamic-slice_fusion.2), channel_id=1, source_target_pairs={{0,1},{1,0},{2,3},{3,2},{4,5},{5,4},{6,7},{7,6},{8,9},{9,8},{10,11... | collective-permute-start | bytes 786440 | tf_op jit(solution)/shard_map/output_projection/ppermute | solution.py:459
  140.2 1.2 collective-permute-done
  141.3 0.7 add_convert_fusion.3
  (7 shorter events, 0.2 us)
Async XLA Ops:
  55.4 17.3 %copy-start.1 = (bf16[128,4096]{1,0:T(8,128)(2,1)S(1)}, bf16[128,4096]{1,0:T(8,128)(2,1)}, u32[]{:S(2)}) copy-start(bf16[128,4096]{1,0:T(8,128)(2,1)} %param.11) | copy-start | bytes 3145732
  72.7 6.2 %copy-start = (bf16[8,3,16,512]{3,2,1,0:T(8,128)(2,1)S(1)}, bf16[8,3,16,512]{3,2,1,0:T(8,128)(2,1)}, u32[]{:S(2)}) copy-start(bf16[8,3,16,512]{3,2,1,0:T(8,128)(2,1)} %projection_to_owner.1) | copy-start | bytes 1179652
  72.7 7.2 %copy-start.3 = (bf16[3,3,128]{2,1,0:T(4,128)(2,1)S(1)}, bf16[3,3,128]{2,1,0:T(4,128)(2,1)}, u32[]{:S(2)}) copy-start(bf16[3,3,128]{2,1,0:T(4,128)(2,1)} %param.8) | copy-start | bytes 6916
  74.7 58.8 %all-to-all-start = ((bf16[128,16,256]{2,0,1:T(8,128)(2,1)}), bf16[128,16,256]{2,0,1:T(8,128)(2,1)S(1)}, u32[]{:S(2)}, u32[]{:S(2)}) async-start(bf16[128,16,256]{2,0,1:T(8,128)(2,1)} %copy.17), calls=%async_computation | async-start | bytes 2097152 | tf_op jit(solution)/shard_map/out_weight_columns/all_to_all | solution.py:393
  81.9 1.0 copy-start.2
  82.9 1.6 %copy-start.4 = (f32[128]{0:T(128)S(1)}, f32[128]{0:T(128)}, u32[]{:S(2)}) copy-start(f32[128]{0:T(128)} %param.9) | copy-start | bytes 1540
  135.9 5.4 %collective-permute-start = (f32[512,128]{1,0:T(8,128)S(1)}, f32[512,128]{1,0:T(8,128)S(1)}, u32[]{:S(2)}, u32[]{:S(2)}) collective-permute-start(f32[512,128]{1,0:T(8,128)S(1)} %constant_dynamic-slice_fusion.2), channel_id=1, source_target_pairs={{0,1},{1,0},{2,3},{3,2},{4,5},{5,4},{6,7},{7,6},{8,9},{9,8},{10,11... | collective-permute-start | bytes 786440 | tf_op jit(solution)/shard_map/output_projection/ppermute | solution.py:459
